TPU v7x, 128 devices: a whole 4x4x4 slice. The times are simulated.
128 devices in a mesh: img: 8 (over z, core), cap: 16 (over y, x).
Axes of the slice: x: 4, y: 4, z: 4, core: 2. Of those that a mesh axis runs over, the one named last changes fastest.
Arguments:
- images: bfloat16 [65536, 256], P('img'), may hold values from -24 to 24
- captions: bfloat16 [8192, 256], P('cap'), may hold values from -4 to 4
- image_logw: float32 [65536], P('img'), may hold values from -1 to 1
- caption_logw: float32 [8192], P('cap'), may hold values from -1 to 1
- image_cot: float32 [65536], P('img'), may hold values from -6 to 6
- caption_cot: float32 [8192], P('cap'), may hold values from -6 to 6
Outputs:
- image_grad: float32 [65536, 256], P(('img', 'cap'))
- caption_grad: float32 [8192, 256], P(('cap', 'img'))
All inputs are finite; a program needn't handle non-finite values.
Results may differ from a plain program's by a relative error of at most 0.0029.
Values may be sent and summed in bfloat16 or wider, within the bound.
A program may use at most 128 MiB of HBM per device.

v0:
```python
import math

import jax
import jax.numpy as jnp
from jax import lax
from jax.sharding import PartitionSpec as P

ITERS = 3


SMOOTHING = 0.25


def combined_all(value, axis, join):
    pieces = jax.tree.map(lambda part: lax.all_gather(part, axis), value)
    head = jax.tree.map(lambda part: part[0], pieces)
    tail = jax.tree.map(lambda part: part[1:], pieces)
    total, _ = lax.scan(lambda total, section: (join(total, section), None), head, tail)
    return total


def pair_combine(first, second):
    top = jnp.maximum(first[0], second[0])
    return (top, first[1] * jnp.exp(first[0] - top) + second[1] * jnp.exp(second[0] - top))


def body(images, captions, image_logw, caption_logw, image_cot, caption_cot):
    inv_root = 1.0 / math.sqrt(images.shape[1])

    def get_tile():
        return jnp.dot(images, captions.T, preferred_element_type=jnp.float32) * inv_root

    col_hist = [jnp.zeros((captions.shape[0],), jnp.float32)]
    row_hist = []
    for level in range(ITERS):
        scores = get_tile()
        logits = (col_hist[-1][None, :] + scores) / SMOOTHING
        top = jnp.max(logits, axis=1)
        total = jnp.sum(jnp.exp(logits - top[:, None]), axis=1)
        top, total = combined_all((top, total), "cap", pair_combine)
        row_pot = SMOOTHING * image_logw - SMOOTHING * (top + jnp.log(total))
        row_hist.append(row_pot)
        logits = (row_pot[:, None] + scores) / SMOOTHING
        top = jnp.max(logits, axis=0)
        total = jnp.sum(jnp.exp(logits - top[None, :]), axis=0)
        top, total = combined_all((top, total), "img", pair_combine)
        col_hist.append(SMOOTHING * caption_logw - SMOOTHING * (top + jnp.log(total)))
    adjoint = jnp.zeros((images.shape[0], captions.shape[0]), jnp.float32)
    col_bar = caption_cot
    for level in reversed(range(ITERS)):
        scores = get_tile()
        row_pot = row_hist[level]
        shift_col = caption_logw - col_hist[level + 1] / SMOOTHING
        col_plan = jnp.exp((row_pot[:, None] + scores) / SMOOTHING - shift_col[None, :])
        weighted = col_plan * col_bar[None, :]
        adjoint = adjoint - weighted
        row_bar = -lax.psum(jnp.sum(weighted, axis=1), "cap")
        if level == ITERS - 1:
            row_bar = image_cot + row_bar
        shift_row = image_logw - row_pot / SMOOTHING
        row_plan = jnp.exp((col_hist[level][None, :] + scores) / SMOOTHING - shift_row[:, None])
        weighted = row_plan * row_bar[:, None]
        adjoint = adjoint - weighted
        if level > 0:
            col_bar = -lax.psum(jnp.sum(weighted, axis=0), "img")
    rounded = adjoint.astype(jnp.bfloat16)
    image_grad = lax.psum_scatter(
        jnp.dot(rounded, captions, preferred_element_type=jnp.float32) * inv_root,
        "cap",
        scatter_dimension=0,
        tiled=True,
    )
    caption_grad = lax.psum_scatter(
        lax.dot_general(
            rounded, images, (((0,), (0,)), ((), ())), preferred_element_type=jnp.float32
        )
        * inv_root,
        "img",
        scatter_dimension=0,
        tiled=True,
    )
    return (image_grad, caption_grad)


def solution(mesh):
    in_specs = (P("img", None), P("cap", None), P("img"), P("cap"), P("img"), P("cap"))
    out_specs = (P(("img", "cap"), None), P(("cap", "img"), None))
    return jax.shard_map(body, mesh=mesh, in_specs=in_specs, out_specs=out_specs, check_vma=False)
```

profile of v0, /device:TPU:0, one launch (start us, length us, event | category | flops | bytes accessed | tf_op | source)
XLA Modules:
  0.0 758.0 jit_solution(11606264779599436448)
XLA Ops:
  7.2 0.9 copy-done
  8.1 10.3 %multiply_reduce_fusion = (f32[8192]{0:T(1024)S(1)}, f32[8192,512]{0,1:T(8,128)}) fusion(bf16[8192,256]{1,0:T(8,128)(2,1)} %param.18, bf16[512,256]{1,0:T(8,128)(2,1)S(1)} %copy-done), kind=kOutput, calls=%fused_computation.35 | convolution fusion | flops 2155864064 | bytes 21266432 | tf_op jit(solution)/shard_map/dot_general | solution.py:31
  18.4 24.5 %all-gather = f32[131072]{0:T(1024)S(1)} all-gather(f32[8192]{0:T(1024)S(1)} %get-tuple-element.276), channel_id=2, replica_groups=mesh['img'=8,'cap'=16] {'cap'}, dimensions={0}, use_global_device_ids=true | all-gather | bytes 557056 | tf_op jit(solution)/shard_map/all_gather | solution.py:15
  42.9 8.5 %exponential_reduce_fusion.5 = f32[8192]{0:T(1024)S(1)} fusion(f32[8192,512]{0,1:T(8,128)} %get-tuple-element.277, f32[8192]{0:T(1024)S(1)} %get-tuple-element.276), kind=kLoop, calls=%fused_computation.34 | loop fusion | flops 12574720 | bytes 16842752 | tf_op jit(solution)/shard_map/reduce_sum | solution.py:39
  51.5 23.4 %all-gather.1 = f32[131072]{0:T(1024)S(1)} all-gather(f32[8192]{0:T(1024)S(1)} %exponential_reduce_fusion.5), channel_id=3, replica_groups=mesh['img'=8,'cap'=16] {'cap'}, dimensions={0}, use_global_device_ids=true | all-gather | bytes 557056 | tf_op jit(solution)/shard_map/all_gather | solution.py:15
  75.1 1.7 while.72
  76.9 8.0 %fusion.5 = f32[512]{0:T(512)S(1)} fusion(f32[8192,512]{0,1:T(8,128)} %get-tuple-element.277, f32[8192]{0:T(1024)S(1)} %get-tuple-element.255), kind=kLoop, calls=%fused_computation.41 | loop fusion | flops 16776704 | bytes 16812032 | tf_op jit(solution)/shard_map/reduce_max | solution.py:44
  84.9 8.1 %exponential_reduce_fusion.4 = f32[512]{0:T(512)S(1)} fusion(f32[8192,512]{0,1:T(8,128)} %get-tuple-element.277, f32[512]{0:T(512)S(1)} %fusion.5, f32[8192]{0:T(1024)S(1)} %get-tuple-element.255), kind=kLoop, calls=%fused_computation.32 | loop fusion | flops 20971008 | bytes 16814080 | tf_op jit(solution)/shard_map/reduce_sum | solution.py:45
  93.0 12.9 %all-gather.13 = f32[8,1,512]{2,1,0:T(1,128)S(1)} all-gather(f32[1,1,512]{2,1,0:T(1,128)S(1)} %bitcast.99), channel_id=5, replica_groups=mesh['img'=8,'cap'=16] {'img'}, dimensions={0}, use_global_device_ids=true | all-gather | bytes 18432 | tf_op jit(solution)/shard_map/all_gather | solution.py:15
  105.9 11.5 %all-gather.12 = f32[8,1,512]{2,1,0:T(1,128)S(1)} all-gather(f32[1,1,512]{2,1,0:T(1,128)S(1)} %bitcast.96), channel_id=4, replica_groups=mesh['img'=8,'cap'=16] {'img'}, dimensions={0}, use_global_device_ids=true | all-gather | bytes 18432 | tf_op jit(solution)/shard_map/all_gather | solution.py:15
  117.3 0.4 while.73
  117.7 8.2 %fusion.6 = f32[8192]{0:T(1024)S(1)} fusion(f32[8192,512]{0,1:T(8,128)} %get-tuple-element.277, f32[512]{0:T(512)S(1)} %get-tuple-element.257), kind=kLoop, calls=%fused_computation.42 | loop fusion | flops 16769024 | bytes 16812032 | tf_op jit(solution)/shard_map/reduce_max | solution.py:38
  126.0 8.0 %exponential_reduce_fusion.3 = f32[8192]{0:T(1024)S(1)} fusion(f32[8192,512]{0,1:T(8,128)} %get-tuple-element.277, f32[8192]{0:T(1024)S(1)} %fusion.6, f32[512]{0:T(512)S(1)} %get-tuple-element.257), kind=kLoop, calls=%fused_computation.30 | loop fusion | flops 20963328 | bytes 16844800 | tf_op jit(solution)/shard_map/reduce_sum | solution.py:39
  134.0 22.0 %all-gather.4 = f32[131072]{0:T(1024)S(1)} all-gather(f32[8192]{0:T(1024)S(1)} %fusion.6), channel_id=6, replica_groups=mesh['img'=8,'cap'=16] {'cap'}, dimensions={0}, use_global_device_ids=true | all-gather | bytes 557056 | tf_op jit(solution)/shard_map/all_gather | solution.py:15
  156.1 23.1 %all-gather.5 = f32[131072]{0:T(1024)S(1)} all-gather(f32[8192]{0:T(1024)S(1)} %exponential_reduce_fusion.3), channel_id=7, replica_groups=mesh['img'=8,'cap'=16] {'cap'}, dimensions={0}, use_global_device_ids=true | all-gather | bytes 557056 | tf_op jit(solution)/shard_map/all_gather | solution.py:15
  179.5 1.7 while.74
  181.2 8.2 %fusion.7 = f32[512]{0:T(512)S(1)} fusion(f32[8192,512]{0,1:T(8,128)} %get-tuple-element.277, f32[8192]{0:T(1024)S(1)} %get-tuple-element.259), kind=kLoop, calls=%fused_computation.43 | loop fusion | flops 16776704 | bytes 16812032 | tf_op jit(solution)/shard_map/reduce_max | solution.py:44
  189.5 8.2 %exponential_reduce_fusion.2 = f32[512]{0:T(512)S(1)} fusion(f32[8192,512]{0,1:T(8,128)} %get-tuple-element.277, f32[512]{0:T(512)S(1)} %fusion.7, f32[8192]{0:T(1024)S(1)} %get-tuple-element.259), kind=kLoop, calls=%fused_computation.28 | loop fusion | flops 20971008 | bytes 16814080 | tf_op jit(solution)/shard_map/reduce_sum | solution.py:45
  197.6 11.4 %all-gather.15 = f32[8,1,512]{2,1,0:T(1,128)S(1)} all-gather(f32[1,1,512]{2,1,0:T(1,128)S(1)} %bitcast.100), channel_id=9, replica_groups=mesh['img'=8,'cap'=16] {'img'}, dimensions={0}, use_global_device_ids=true | all-gather | bytes 18432 | tf_op jit(solution)/shard_map/all_gather | solution.py:15
  209.1 11.7 %all-gather.14 = f32[8,1,512]{2,1,0:T(1,128)S(1)} all-gather(f32[1,1,512]{2,1,0:T(1,128)S(1)} %bitcast.97), channel_id=8, replica_groups=mesh['img'=8,'cap'=16] {'img'}, dimensions={0}, use_global_device_ids=true | all-gather | bytes 18432 | tf_op jit(solution)/shard_map/all_gather | solution.py:15
  220.8 0.4 while.75
  221.2 8.2 %fusion.8 = f32[8192]{0:T(1024)S(1)} fusion(f32[8192,512]{0,1:T(8,128)} %get-tuple-element.277, f32[512]{0:T(512)S(1)} %get-tuple-element.261), kind=kLoop, calls=%fused_computation.44 | loop fusion | flops 16769024 | bytes 16812032 | tf_op jit(solution)/shard_map/reduce_max | solution.py:38
  229.4 8.0 %exponential_reduce_fusion.1 = f32[8192]{0:T(1024)S(1)} fusion(f32[8192,512]{0,1:T(8,128)} %get-tuple-element.277, f32[8192]{0:T(1024)S(1)} %fusion.8, f32[512]{0:T(512)S(1)} %get-tuple-element.261), kind=kLoop, calls=%fused_computation.26 | loop fusion | flops 20963328 | bytes 16844800 | tf_op jit(solution)/shard_map/reduce_sum | solution.py:39
  237.5 22.0 %all-gather.8 = f32[131072]{0:T(1024)S(1)} all-gather(f32[8192]{0:T(1024)S(1)} %fusion.8), channel_id=10, replica_groups=mesh['img'=8,'cap'=16] {'cap'}, dimensions={0}, use_global_device_ids=true | all-gather | bytes 557056 | tf_op jit(solution)/shard_map/all_gather | solution.py:15
  259.5 23.1 %all-gather.9 = f32[131072]{0:T(1024)S(1)} all-gather(f32[8192]{0:T(1024)S(1)} %exponential_reduce_fusion.1), channel_id=11, replica_groups=mesh['img'=8,'cap'=16] {'cap'}, dimensions={0}, use_global_device_ids=true | all-gather | bytes 557056 | tf_op jit(solution)/shard_map/all_gather | solution.py:15
  282.8 0.1 reshape.68
  282.9 1.7 while.76
  284.7 8.3 %fusion.9 = f32[512]{0:T(512)S(1)} fusion(f32[8192,512]{0,1:T(8,128)} %get-tuple-element.277, f32[8192]{0:T(1024)S(1)} %get-tuple-element.263), kind=kLoop, calls=%fused_computation.45 | loop fusion | flops 16776704 | bytes 16812032 | tf_op jit(solution)/shard_map/reduce_max | solution.py:44
  292.9 8.2 %exponential_reduce_fusion = f32[512]{0:T(512)S(1)} fusion(f32[8192,512]{0,1:T(8,128)} %get-tuple-element.277, f32[512]{0:T(512)S(1)} %fusion.9, f32[8192]{0:T(1024)S(1)} %get-tuple-element.263), kind=kLoop, calls=%fused_computation.24 | loop fusion | flops 20971008 | bytes 16814080 | tf_op jit(solution)/shard_map/reduce_sum | solution.py:45
  301.1 11.4 %all-gather.17 = f32[8,1,512]{2,1,0:T(1,128)S(1)} all-gather(f32[1,1,512]{2,1,0:T(1,128)S(1)} %bitcast.101), channel_id=13, replica_groups=mesh['img'=8,'cap'=16] {'img'}, dimensions={0}, use_global_device_ids=true | all-gather | bytes 18432 | tf_op jit(solution)/shard_map/all_gather | solution.py:15
  312.5 11.3 %all-gather.16 = f32[8,1,512]{2,1,0:T(1,128)S(1)} all-gather(f32[1,1,512]{2,1,0:T(1,128)S(1)} %bitcast.98), channel_id=12, replica_groups=mesh['img'=8,'cap'=16] {'img'}, dimensions={0}, use_global_device_ids=true | all-gather | bytes 18432 | tf_op jit(solution)/shard_map/all_gather | solution.py:15
  323.8 0.4 while.77
  324.2 8.3 %fusion = f32[8192]{0:T(1024)S(1)} fusion(f32[8192,512]{0,1:T(8,128)} %get-tuple-element.277, f32[512]{0:T(512)S(1)} %copy-done.5, f32[512]{0:T(512)S(1)} %multiply_subtract_fusion.8, f32[8192]{0:T(1024)S(1)} %get-tuple-element.263), kind=kLoop, calls=%fused_computation.36 | loop fusion | flops 25157632 | bytes 16846848 | tf_op jit(solution)/shard_map/reduce_sum | solution.py:57
  332.5 72.3 %psum.35 = f32[8192]{0:T(1024)S(1)} all-reduce(f32[8192]{0:T(1024)S(1)} %fusion), channel_id=1, replica_groups=mesh['img'=8,'cap'=16] {'cap'}, use_global_device_ids=true, to_apply=%region_25.26 | all-reduce | flops 8192 | bytes 65536 | tf_op jit(solution)/shard_map/psum | solution.py:57
  404.9 8.6 %fusion.1 = f32[512]{0:T(512)S(1)} fusion(f32[8192,512]{0,1:T(8,128)} %get-tuple-element.277, f32[8192]{0:T(1024)S(1)} %negate_add_fusion, f32[8192]{0:T(1024)S(1)} %get-tuple-element.262, f32[512]{0:T(512)S(1)} %get-tuple-element.261), kind=kLoop, calls=%fused_computation.37 | loop fusion | flops 25165312 | bytes 16846848 | tf_op jit(solution)/shard_map/reduce_sum | solution.py:65
  413.4 12.4 %psum.36 = f32[512]{0:T(512)S(1)} all-reduce(f32[512]{0:T(512)S(1)} %fusion.1), channel_id=1, replica_groups=mesh['img'=8,'cap'=16] {'img'}, use_global_device_ids=true, to_apply=%region_27.28 | all-reduce | flops 512 | bytes 4096 | tf_op jit(solution)/shard_map/psum | solution.py:65
  425.9 8.3 %fusion.2 = f32[8192]{0:T(1024)S(1)} fusion(f32[8192,512]{0,1:T(8,128)} %get-tuple-element.277, f32[512]{0:T(512)S(1)} %neg.16, f32[512]{0:T(512)S(1)} %get-tuple-element.260, f32[8192]{0:T(1024)S(1)} %get-tuple-element.259), kind=kLoop, calls=%fused_computation.38 | loop fusion | flops 25157632 | bytes 16846848 | tf_op jit(solution)/shard_map/reduce_sum | solution.py:57
  434.1 69.5 %psum.37 = f32[8192]{0:T(1024)S(1)} all-reduce(f32[8192]{0:T(1024)S(1)} %fusion.2), channel_id=1, replica_groups=mesh['img'=8,'cap'=16] {'cap'}, use_global_device_ids=true, to_apply=%region_29.30 | all-reduce | flops 8192 | bytes 65536 | tf_op jit(solution)/shard_map/psum | solution.py:57
  503.7 8.6 %fusion.3 = f32[512]{0:T(512)S(1)} fusion(f32[8192,512]{0,1:T(8,128)} %get-tuple-element.277, f32[8192]{0:T(1024)S(1)} %neg.17, f32[8192]{0:T(1024)S(1)} %get-tuple-element.258, f32[512]{0:T(512)S(1)} %get-tuple-element.257), kind=kLoop, calls=%fused_computation.39 | loop fusion | flops 25165312 | bytes 16846848 | tf_op jit(solution)/shard_map/reduce_sum | solution.py:65
  512.3 12.4 %psum.38 = f32[512]{0:T(512)S(1)} all-reduce(f32[512]{0:T(512)S(1)} %fusion.3), channel_id=1, replica_groups=mesh['img'=8,'cap'=16] {'img'}, use_global_device_ids=true, to_apply=%region_31.32 | all-reduce | flops 512 | bytes 4096 | tf_op jit(solution)/shard_map/psum | solution.py:65
  524.7 8.3 %fusion.4 = f32[8192]{0:T(1024)S(1)} fusion(f32[8192,512]{0,1:T(8,128)} %get-tuple-element.277, f32[512]{0:T(512)S(1)} %neg.18, f32[512]{0:T(512)S(1)} %get-tuple-element.256, f32[8192]{0:T(1024)S(1)} %get-tuple-element.255), kind=kLoop, calls=%fused_computation.40 | loop fusion | flops 25157632 | bytes 16846848 | tf_op jit(solution)/shard_map/reduce_sum | solution.py:57
  533.0 69.5 %psum.39 = f32[8192]{0:T(1024)S(1)} all-reduce(f32[8192]{0:T(1024)S(1)} %fusion.4), channel_id=1, replica_groups=mesh['img'=8,'cap'=16] {'cap'}, use_global_device_ids=true, to_apply=%region_33.34 | all-reduce | flops 8192 | bytes 65536 | tf_op jit(solution)/shard_map/psum | solution.py:57
  602.5 28.6 %subtract_convert_fusion = bf16[8192,512]{0,1:T(8,128)(2,1)S(1)} fusion(f32[8192,512]{0,1:T(8,128)} %get-tuple-element.277, f32[8192]{0:T(1024)S(1)} %neg.19, f32[8192]{0:T(1024)S(1)} %get-tuple-element.254, f32[512]{0:T(512)S(1)} %neg.18, f32[512]{0:T(512)S(1)} %get-tuple-element.256, f32[8192]{0:T(1024)S(1)} %neg.17, f32[8192]{0:T(1024)S(1)} %get-tuple-element.258, ...), kind=kLoop, calls=%fused_computation.18 | loop fusion | flops 130023424 | bytes 25477120 | tf_op jit(solution)/shard_map/convert_element_type | solution.py:66
  631.2 3.2 copy-done.6
  634.4 3.1 convolution_multiply_fusion.1
  637.6 9.0 %convolution_multiply_fusion = f32[8192,256]{1,0:T(8,128)} fusion(bf16[8192,512]{0,1:T(8,128)(2,1)} %copy-done.6, bf16[512,256]{1,0:T(8,128)(2,1)S(1)} %copy-done), kind=kOutput, calls=%fused_computation.46 | convolution fusion | flops 2149580800 | bytes 17039360 | tf_op jit(solution)/shard_map/dot_general | solution.py:68
  646.6 15.9 %reduce-scatter.5.cloned.1.call-done = f32[64,256]{1,0:T(8,128)} async-done(((f32[512,256]{1,0:T(8,128)}), f32[64,256]{1,0:T(8,128)}) %reduce-scatter.5.cloned.1.call-update) | async-done | bytes 65552 | tf_op jit(solution)/shard_map/reduce_scatter | solution.py:73
  662.5 88.4 %reduce-scatter.3.cloned.1.call-done = f32[512,256]{1,0:T(8,128)} async-done(((f32[8192,256]{1,0:T(8,128)}), f32[512,256]{1,0:T(8,128)}) %reduce-scatter.3.cloned.1.call-update) | async-done | bytes 524304 | tf_op jit(solution)/shard_map/reduce_scatter | solution.py:67
  (194 shorter events, 5.7 us)
Async XLA Ops:
  7.2 1.0 copy-start
  7.2 655.3 %reduce-scatter.5.cloned.1.call-start = ((), (), s32[]{:S(2)}) async-start(), calls=%async_computation.3 | async-start | bytes 589824 | tf_op jit(solution)/shard_map/reduce_scatter | solution.py:73
  18.4 58.5 %copy-start.2 = (f32[8192]{0:T(1024)S(1)}, f32[8192]{0:T(1024)}, u32[]{:S(2)}) copy-start(f32[8192]{0:T(1024)} %param.20) | copy-start | bytes 98308
  76.9 40.8 %copy-start.4 = (f32[512]{0:T(512)S(1)}, f32[512]{0:T(512)}, u32[]{:S(2)}) copy-start(f32[512]{0:T(512)} %param.21) | copy-start | bytes 6148
  284.7 39.6 %copy-start.5 = (f32[512]{0:T(512)S(1)}, f32[512]{0:T(512)}, u32[]{:S(2)}) copy-start(f32[512]{0:T(512)} %param.23) | copy-start | bytes 6148
  292.9 112.0 %copy-start.3 = (f32[8192]{0:T(1024)S(1)}, f32[8192]{0:T(1024)}, u32[]{:S(2)}) copy-start(f32[8192]{0:T(1024)} %param.22) | copy-start | bytes 98308
  602.5 31.9 %copy-start.1 = (bf16[8192,256]{1,0:T(8,128)(2,1)S(1)}, bf16[8192,256]{1,0:T(8,128)(2,1)}, u32[]{:S(2)}) copy-start(bf16[8192,256]{1,0:T(8,128)(2,1)} %param.18) | copy-start | bytes 12582916
  631.2 3.2 copy-start.6
  637.5 113.4 %reduce-scatter.3.cloned.1.call-start = ((), (), s32[]{:S(2)}) async-start(), calls=%async_computation.2 | async-start | bytes 8912896 | tf_op jit(solution)/shard_map/reduce_scatter | solution.py:67
Sparse Core Ops, SparseCore 0:
  637.6 24.8 reduce-scatter.4
  666.5 84.4 reduce-scatter.2
where the time goes:
time: 767 us; the launch traced here: 758 us
  blocking collectives  445 us (58%)
  other arithmetic  163 us (21%)
  waiting for transfers between devices  104 us (14%)
  matrix products  22.4 us (3%)
  between operations  14.6 us (2%)
    psum x3, blocking collectives, body(): row_bar = -lax.psum(jnp.sum(weighted, axis=1), 'cap')  211 us
    all_gather x12, blocking collectives, combined_all(): pieces = jax.tree.map(lambda part: lax.all_gather(part, axis), value)  208 us
    reduce_scatter x1, waiting for transfers between devices, body(): lax.psum_scatter(jnp.dot(rounded, captions, preferred_element_type=jnp.fl...  88.4 us
    convert_element_type x1, other arithmetic, body(): rounded = adjoint.astype(jnp.bfloat16)  28.6 us
    psum x2, blocking collectives, body(): col_bar = -lax.psum(jnp.sum(weighted, axis=0), 'img')  24.8 us
    reduce_sum x3, other arithmetic, body(): row_bar = -lax.psum(jnp.sum(weighted, axis=1), 'cap')  24.8 us
    reduce_sum x3, other arithmetic, body(): total = jnp.sum(jnp.exp(logits - top[:, None]), axis=1)  24.6 us
    reduce_max x3, other arithmetic, body(): top = jnp.max(logits, axis=0)  24.5 us
  transfers between devices with their start and end apart: 2, of which 2 were waited for; matrix products, arithmetic and copies ran while one was open for 1% of the time, Pallas kernels for 0%

commit v1 on v0

--- a/solution.py
+++ b/solution.py
@@ -11,17 +11,14 @@
 SMOOTHING = 0.25
 
 
-def combined_all(value, axis, join):
-    pieces = jax.tree.map(lambda part: lax.all_gather(part, axis), value)
-    head = jax.tree.map(lambda part: part[0], pieces)
-    tail = jax.tree.map(lambda part: part[1:], pieces)
-    total, _ = lax.scan(lambda total, section: (join(total, section), None), head, tail)
-    return total
+def gathered_lse(part, axis):
+    pieces = lax.all_gather(part, axis)
+    top = jnp.max(pieces, axis=0)
+    return top + jnp.log(jnp.sum(jnp.exp(pieces - top[None]), axis=0))
 
 
-def pair_combine(first, second):
-    top = jnp.maximum(first[0], second[0])
-    return (top, first[1] * jnp.exp(first[0] - top) + second[1] * jnp.exp(second[0] - top))
+def gathered_sum(part, axis):
+    return jnp.sum(lax.all_gather(part, axis), axis=0)
 
 
 def body(images, captions, image_logw, caption_logw, image_cot, caption_cot):
@@ -36,15 +33,13 @@
         scores = get_tile()
         logits = (col_hist[-1][None, :] + scores) / SMOOTHING
         top = jnp.max(logits, axis=1)
-        total = jnp.sum(jnp.exp(logits - top[:, None]), axis=1)
-        top, total = combined_all((top, total), "cap", pair_combine)
-        row_pot = SMOOTHING * image_logw - SMOOTHING * (top + jnp.log(total))
+        part = top + jnp.log(jnp.sum(jnp.exp(logits - top[:, None]), axis=1))
+        row_pot = SMOOTHING * image_logw - SMOOTHING * gathered_lse(part, "cap")
         row_hist.append(row_pot)
         logits = (row_pot[:, None] + scores) / SMOOTHING
         top = jnp.max(logits, axis=0)
-        total = jnp.sum(jnp.exp(logits - top[None, :]), axis=0)
-        top, total = combined_all((top, total), "img", pair_combine)
-        col_hist.append(SMOOTHING * caption_logw - SMOOTHING * (top + jnp.log(total)))
+        part = top + jnp.log(jnp.sum(jnp.exp(logits - top[None, :]), axis=0))
+        col_hist.append(SMOOTHING * caption_logw - SMOOTHING * gathered_lse(part, "img"))
     adjoint = jnp.zeros((images.shape[0], captions.shape[0]), jnp.float32)
     col_bar = caption_cot
     for level in reversed(range(ITERS)):
@@ -54,7 +49,7 @@
         col_plan = jnp.exp((row_pot[:, None] + scores) / SMOOTHING - shift_col[None, :])
         weighted = col_plan * col_bar[None, :]
         adjoint = adjoint - weighted
-        row_bar = -lax.psum(jnp.sum(weighted, axis=1), "cap")
+        row_bar = -gathered_sum(jnp.sum(weighted, axis=1), "cap")
         if level == ITERS - 1:
             row_bar = image_cot + row_bar
         shift_row = image_logw - row_pot / SMOOTHING
@@ -62,7 +57,7 @@
         weighted = row_plan * row_bar[:, None]
         adjoint = adjoint - weighted
         if level > 0:
-            col_bar = -lax.psum(jnp.sum(weighted, axis=0), "img")
+            col_bar = -gathered_sum(jnp.sum(weighted, axis=0), "img")
     rounded = adjoint.astype(jnp.bfloat16)
     image_grad = lax.psum_scatter(
         jnp.dot(rounded, captions, preferred_element_type=jnp.float32) * inv_root,

time: 767 us -> 518 us (0.68)
  blocking collectives: 445 us -> 197 us
    psum x5 -> x0, blocking collectives: 236 us -> none  [the longest x3 211 us: body(): row_bar = -lax.psum(jnp.sum(weighted, axis=1), 'cap')]
    all_gather x12 -> x11, blocking collectives: 208 us -> 197 us  [the longest x6 106 us: gathered_lse(): pieces = lax.all_gather(part, axis)]
    reduce_sum x11 -> x22, other arithmetic: 91 us -> 91.7 us  [the longest x3 24.8 us: body(): row_bar = -gathered_sum(jnp.sum(weighted, axis=1), 'cap')]
  transfers between devices with their start and end apart: 2 -> 2, of which waited for: 2 -> 2; matrix products, arithmetic and copies ran while one was open for 1% -> 2% of each run, Pallas kernels for 0% -> 0%
where the time goes in v1:
time: 518 us; the launch traced here: 510 us
  blocking collectives  197 us (38%)
  other arithmetic  162 us (31%)
  waiting for transfers between devices  109 us (21%)
  matrix products  22.4 us (4%)
  between operations  14.8 us (3%)
    all_gather x6, blocking collectives, gathered_lse(): pieces = lax.all_gather(part, axis)  106 us
    all_gather x5, blocking collectives, gathered_sum(): return jnp.sum(lax.all_gather(part, axis), axis=0)  91.1 us
    reduce_scatter x1, waiting for transfers between devices, body(): lax.psum_scatter(jnp.dot(rounded, captions, preferred_element_type=jnp.fl...  88.5 us
    convert_element_type x1, other arithmetic, body(): rounded = adjoint.astype(jnp.bfloat16)  28.6 us
    reduce_sum x3, other arithmetic, body(): row_bar = -gathered_sum(jnp.sum(weighted, axis=1), 'cap')  24.8 us
    reduce_sum x3, other arithmetic, body(): part = top + jnp.log(jnp.sum(jnp.exp(logits - top[:, None]), axis=1))  24.6 us
    reduce_max x3, other arithmetic, body(): top = jnp.max(logits, axis=0)  24.5 us
    reduce_sum x3, other arithmetic, body(): part = top + jnp.log(jnp.sum(jnp.exp(logits - top[None, :]), axis=0))  24.4 us
  transfers between devices with their start and end apart: 2, of which 2 were waited for; matrix products, arithmetic and copies ran while one was open for 2% of the time, Pallas kernels for 0%

profile of v1, /device:TPU:0, one launch (start us, length us, event | category | flops | bytes accessed | tf_op | source)
XLA Modules:
  0.0 510.1 jit_solution(12514877673017700235)
XLA Ops:
  7.2 0.9 copy-done
  8.1 10.3 %multiply_reduce_fusion = (f32[8192]{0:T(1024)S(1)}, f32[8192,512]{0,1:T(8,128)}) fusion(bf16[8192,256]{1,0:T(8,128)(2,1)} %param.6, bf16[512,256]{1,0:T(8,128)(2,1)S(1)} %copy-done), kind=kOutput, calls=%fused_computation.17 | convolution fusion | flops 2155864064 | bytes 21266432 | tf_op jit(solution)/shard_map/dot_general | solution.py:28
  18.4 8.5 %exponential_reduce_fusion.5 = f32[8192]{0:T(1024)S(1)} fusion(f32[8192,512]{0,1:T(8,128)} %get-tuple-element.13, f32[8192]{0:T(1024)S(1)} %get-tuple-element.12), kind=kLoop, calls=%fused_computation.16 | loop fusion | flops 12574720 | bytes 16842752 | tf_op jit(solution)/shard_map/reduce_sum | solution.py:36
  27.0 24.4 %all-gather = f32[131072]{0:T(1024)S(1)} all-gather(f32[8192]{0:T(1024)S(1)} %log_add_fusion.2), channel_id=2, replica_groups=mesh['img'=8,'cap'=16] {'cap'}, dimensions={0}, use_global_device_ids=true | all-gather | bytes 557056 | tf_op jit(solution)/shard_map/all_gather | solution.py:15
  51.3 0.1 reshape.137
  51.5 0.1 reduce_max.109
  51.5 0.1 exponential_reduce_fusion.8
  51.7 8.0 %fusion.5 = f32[512]{0:T(512)S(1)} fusion(f32[8192,512]{0,1:T(8,128)} %get-tuple-element.13, f32[8192]{0:T(1024)S(1)} %get-tuple-element.3), kind=kLoop, calls=%fused_computation.23 | loop fusion | flops 16776704 | bytes 16812032 | tf_op jit(solution)/shard_map/reduce_max | solution.py:40
  59.8 8.1 %exponential_reduce_fusion.4 = f32[512]{0:T(512)S(1)} fusion(f32[8192,512]{0,1:T(8,128)} %get-tuple-element.13, f32[512]{0:T(512)S(1)} %fusion.5, f32[8192]{0:T(1024)S(1)} %get-tuple-element.3), kind=kLoop, calls=%fused_computation.14 | loop fusion | flops 20971008 | bytes 16814080 | tf_op jit(solution)/shard_map/reduce_sum | solution.py:41
  67.8 13.3 %all-gather.11 = f32[8,1,512]{2,1,0:T(1,128)S(1)} all-gather(f32[1,1,512]{2,1,0:T(1,128)S(1)} %bitcast.31), channel_id=3, replica_groups=mesh['img'=8,'cap'=16] {'img'}, dimensions={0}, use_global_device_ids=true | all-gather | bytes 18432 | tf_op jit(solution)/shard_map/all_gather | solution.py:15
  81.2 8.2 %fusion.6 = f32[8192]{0:T(1024)S(1)} fusion(f32[8192,512]{0,1:T(8,128)} %get-tuple-element.13, f32[512]{0:T(512)S(1)} %get-tuple-element.5), kind=kLoop, calls=%fused_computation.24 | loop fusion | flops 16769024 | bytes 16812032 | tf_op jit(solution)/shard_map/reduce_max | solution.py:35
  89.5 8.0 %exponential_reduce_fusion.3 = f32[8192]{0:T(1024)S(1)} fusion(f32[8192,512]{0,1:T(8,128)} %get-tuple-element.13, f32[8192]{0:T(1024)S(1)} %fusion.6, f32[512]{0:T(512)S(1)} %get-tuple-element.5), kind=kLoop, calls=%fused_computation.12 | loop fusion | flops 20963328 | bytes 16844800 | tf_op jit(solution)/shard_map/reduce_sum | solution.py:36
  97.6 23.4 %all-gather.2 = f32[131072]{0:T(1024)S(1)} all-gather(f32[8192]{0:T(1024)S(1)} %log_add_fusion.1), channel_id=4, replica_groups=mesh['img'=8,'cap'=16] {'cap'}, dimensions={0}, use_global_device_ids=true | all-gather | bytes 557056 | tf_op jit(solution)/shard_map/all_gather | solution.py:15
  120.9 0.1 reshape.139
  121.0 0.1 reduce_max.113
  121.1 0.1 exponential_reduce_fusion.7
  121.3 8.2 %fusion.7 = f32[512]{0:T(512)S(1)} fusion(f32[8192,512]{0,1:T(8,128)} %get-tuple-element.13, f32[8192]{0:T(1024)S(1)} %get-tuple-element.7), kind=kLoop, calls=%fused_computation.25 | loop fusion | flops 16776704 | bytes 16812032 | tf_op jit(solution)/shard_map/reduce_max | solution.py:40
  129.5 8.2 %exponential_reduce_fusion.2 = f32[512]{0:T(512)S(1)} fusion(f32[8192,512]{0,1:T(8,128)} %get-tuple-element.13, f32[512]{0:T(512)S(1)} %fusion.7, f32[8192]{0:T(1024)S(1)} %get-tuple-element.7), kind=kLoop, calls=%fused_computation.10 | loop fusion | flops 20971008 | bytes 16814080 | tf_op jit(solution)/shard_map/reduce_sum | solution.py:41
  137.7 11.5 %all-gather.12 = f32[8,1,512]{2,1,0:T(1,128)S(1)} all-gather(f32[1,1,512]{2,1,0:T(1,128)S(1)} %bitcast.32), channel_id=5, replica_groups=mesh['img'=8,'cap'=16] {'img'}, dimensions={0}, use_global_device_ids=true | all-gather | bytes 18432 | tf_op jit(solution)/shard_map/all_gather | solution.py:15
  149.2 8.2 %fusion.8 = f32[8192]{0:T(1024)S(1)} fusion(f32[8192,512]{0,1:T(8,128)} %get-tuple-element.13, f32[512]{0:T(512)S(1)} %get-tuple-element.9), kind=kLoop, calls=%fused_computation.26 | loop fusion | flops 16769024 | bytes 16812032 | tf_op jit(solution)/shard_map/reduce_max | solution.py:35
  157.5 8.0 %exponential_reduce_fusion.1 = f32[8192]{0:T(1024)S(1)} fusion(f32[8192,512]{0,1:T(8,128)} %get-tuple-element.13, f32[8192]{0:T(1024)S(1)} %fusion.8, f32[512]{0:T(512)S(1)} %get-tuple-element.9), kind=kLoop, calls=%fused_computation.8 | loop fusion | flops 20963328 | bytes 16844800 | tf_op jit(solution)/shard_map/reduce_sum | solution.py:36
  165.6 22.0 %all-gather.4 = f32[131072]{0:T(1024)S(1)} all-gather(f32[8192]{0:T(1024)S(1)} %log_add_fusion), channel_id=6, replica_groups=mesh['img'=8,'cap'=16] {'cap'}, dimensions={0}, use_global_device_ids=true | all-gather | bytes 557056 | tf_op jit(solution)/shard_map/all_gather | solution.py:15
  187.6 0.1 reshape.141
  187.7 0.1 reduce_max.117
  187.8 0.1 exponential_reduce_fusion.6
  187.9 8.3 %fusion.9 = f32[512]{0:T(512)S(1)} fusion(f32[8192,512]{0,1:T(8,128)} %get-tuple-element.13, f32[8192]{0:T(1024)S(1)} %get-tuple-element.11), kind=kLoop, calls=%fused_computation.27 | loop fusion | flops 16776704 | bytes 16812032 | tf_op jit(solution)/shard_map/reduce_max | solution.py:40
  196.2 8.2 %exponential_reduce_fusion = f32[512]{0:T(512)S(1)} fusion(f32[8192,512]{0,1:T(8,128)} %get-tuple-element.13, f32[512]{0:T(512)S(1)} %fusion.9, f32[8192]{0:T(1024)S(1)} %get-tuple-element.11), kind=kLoop, calls=%fused_computation.6 | loop fusion | flops 20971008 | bytes 16814080 | tf_op jit(solution)/shard_map/reduce_sum | solution.py:41
  204.4 11.4 %all-gather.13 = f32[8,1,512]{2,1,0:T(1,128)S(1)} all-gather(f32[1,1,512]{2,1,0:T(1,128)S(1)} %bitcast.33), channel_id=7, replica_groups=mesh['img'=8,'cap'=16] {'img'}, dimensions={0}, use_global_device_ids=true | all-gather | bytes 18432 | tf_op jit(solution)/shard_map/all_gather | solution.py:15
  215.9 8.3 %fusion = f32[8192]{0:T(1024)S(1)} fusion(f32[8192,512]{0,1:T(8,128)} %get-tuple-element.13, f32[512]{0:T(512)S(1)} %copy-done.5, f32[512]{0:T(512)S(1)} %multiply_subtract_fusion.8, f32[8192]{0:T(1024)S(1)} %get-tuple-element.11), kind=kLoop, calls=%fused_computation.18 | loop fusion | flops 25157632 | bytes 16846848 | tf_op jit(solution)/shard_map/reduce_sum | solution.py:52
  224.2 23.0 %all-gather.6 = f32[131072]{0:T(1024)S(1)} all-gather(f32[8192]{0:T(1024)S(1)} %fusion), channel_id=8, replica_groups=mesh['img'=8,'cap'=16] {'cap'}, dimensions={0}, use_global_device_ids=true | all-gather | bytes 557056 | tf_op jit(solution)/shard_map/all_gather | solution.py:21
  247.2 0.1 reshape.143
  247.3 0.1 reduce_sum.211
  247.4 8.5 %fusion.1 = f32[512]{0:T(512)S(1)} fusion(f32[8192,512]{0,1:T(8,128)} %get-tuple-element.13, f32[8192]{0:T(1024)S(1)} %negate_add_fusion, f32[8192]{0:T(1024)S(1)} %get-tuple-element.10, f32[512]{0:T(512)S(1)} %get-tuple-element.9), kind=kLoop, calls=%fused_computation.19 | loop fusion | flops 25165312 | bytes 16846848 | tf_op jit(solution)/shard_map/reduce_sum | solution.py:60
  256.0 11.3 %all-gather.14 = f32[8,1,512]{2,1,0:T(1,128)S(1)} all-gather(f32[1,1,512]{2,1,0:T(1,128)S(1)} %bitcast.29), channel_id=9, replica_groups=mesh['img'=8,'cap'=16] {'img'}, dimensions={0}, use_global_device_ids=true | all-gather | bytes 18432 | tf_op jit(solution)/shard_map/all_gather | solution.py:21
  267.3 8.3 %fusion.2 = f32[8192]{0:T(1024)S(1)} fusion(f32[8192,512]{0,1:T(8,128)} %get-tuple-element.13, f32[512]{0:T(512)S(1)} %neg.32, f32[512]{0:T(512)S(1)} %get-tuple-element.8, f32[8192]{0:T(1024)S(1)} %get-tuple-element.7), kind=kLoop, calls=%fused_computation.20 | loop fusion | flops 25157632 | bytes 16846848 | tf_op jit(solution)/shard_map/reduce_sum | solution.py:52
  275.6 22.0 %all-gather.8 = f32[131072]{0:T(1024)S(1)} all-gather(f32[8192]{0:T(1024)S(1)} %fusion.2), channel_id=10, replica_groups=mesh['img'=8,'cap'=16] {'cap'}, dimensions={0}, use_global_device_ids=true | all-gather | bytes 557056 | tf_op jit(solution)/shard_map/all_gather | solution.py:21
  297.6 0.1 reshape.145
  297.8 8.5 %fusion.3 = f32[512]{0:T(512)S(1)} fusion(f32[8192,512]{0,1:T(8,128)} %get-tuple-element.13, f32[8192]{0:T(1024)S(1)} %neg.33, f32[8192]{0:T(1024)S(1)} %get-tuple-element.6, f32[512]{0:T(512)S(1)} %get-tuple-element.5), kind=kLoop, calls=%fused_computation.21 | loop fusion | flops 25165312 | bytes 16846848 | tf_op jit(solution)/shard_map/reduce_sum | solution.py:60
  306.4 11.4 %all-gather.15 = f32[8,1,512]{2,1,0:T(1,128)S(1)} all-gather(f32[1,1,512]{2,1,0:T(1,128)S(1)} %bitcast.30), channel_id=11, replica_groups=mesh['img'=8,'cap'=16] {'img'}, dimensions={0}, use_global_device_ids=true | all-gather | bytes 18432 | tf_op jit(solution)/shard_map/all_gather | solution.py:21
  317.8 8.3 %fusion.4 = f32[8192]{0:T(1024)S(1)} fusion(f32[8192,512]{0,1:T(8,128)} %get-tuple-element.13, f32[512]{0:T(512)S(1)} %neg.34, f32[512]{0:T(512)S(1)} %get-tuple-element.4, f32[8192]{0:T(1024)S(1)} %get-tuple-element.3), kind=kLoop, calls=%fused_computation.22 | loop fusion | flops 25157632 | bytes 16846848 | tf_op jit(solution)/shard_map/reduce_sum | solution.py:52
  326.1 23.3 %all-gather.10 = f32[131072]{0:T(1024)S(1)} all-gather(f32[8192]{0:T(1024)S(1)} %fusion.4), channel_id=12, replica_groups=mesh['img'=8,'cap'=16] {'cap'}, dimensions={0}, use_global_device_ids=true | all-gather | bytes 557056 | tf_op jit(solution)/shard_map/all_gather | solution.py:21
  349.4 0.1 reshape.147
  349.6 28.6 %subtract_convert_fusion = bf16[8192,512]{0,1:T(8,128)(2,1)S(1)} fusion(f32[8192,512]{0,1:T(8,128)} %get-tuple-element.13, f32[8192]{0:T(1024)S(1)} %neg.35, f32[8192]{0:T(1024)S(1)} %get-tuple-element.2, f32[512]{0:T(512)S(1)} %neg.34, f32[512]{0:T(512)S(1)} %get-tuple-element.4, f32[8192]{0:T(1024)S(1)} %neg.33, f32[8192]{0:T(1024)S(1)} %get-tuple-element.6, ...), kind=kLoop, calls=%fused_computation | loop fusion | flops 130023424 | bytes 25477120 | tf_op jit(solution)/shard_map/convert_element_type | solution.py:61
  378.3 3.2 copy-done.6
  381.5 3.1 convolution_multiply_fusion.1
  384.7 9.0 %convolution_multiply_fusion = f32[8192,256]{1,0:T(8,128)} fusion(bf16[8192,512]{0,1:T(8,128)(2,1)} %copy-done.6, bf16[512,256]{1,0:T(8,128)(2,1)S(1)} %copy-done), kind=kOutput, calls=%fused_computation.28 | convolution fusion | flops 2149580800 | bytes 17039360 | tf_op jit(solution)/shard_map/dot_general | solution.py:63
  393.7 20.8 %reduce-scatter.5.cloned.1.call-done = f32[64,256]{1,0:T(8,128)} async-done(((f32[512,256]{1,0:T(8,128)}), f32[64,256]{1,0:T(8,128)}) %reduce-scatter.5.cloned.1.call-update) | async-done | bytes 65552 | tf_op jit(solution)/shard_map/reduce_scatter | solution.py:68
  414.4 88.5 %reduce-scatter.3.cloned.1.call-done = f32[512,256]{1,0:T(8,128)} async-done(((f32[8192,256]{1,0:T(8,128)}), f32[512,256]{1,0:T(8,128)}) %reduce-scatter.3.cloned.1.call-update) | async-done | bytes 524304 | tf_op jit(solution)/shard_map/reduce_scatter | solution.py:62
  (43 shorter events, 0.7 us)
Async XLA Ops:
  7.2 1.0 copy-start
  7.2 407.2 %reduce-scatter.5.cloned.1.call-start = ((), (), s32[]{:S(2)}) async-start(), calls=%async_computation.3 | async-start | bytes 589824 | tf_op jit(solution)/shard_map/reduce_scatter | solution.py:68
  18.4 33.3 %copy-start.2 = (f32[8192]{0:T(1024)S(1)}, f32[8192]{0:T(1024)}, u32[]{:S(2)}) copy-start(f32[8192]{0:T(1024)} %param.8) | copy-start | bytes 98308
  51.7 29.5 %copy-start.4 = (f32[512]{0:T(512)S(1)}, f32[512]{0:T(512)}, u32[]{:S(2)}) copy-start(f32[512]{0:T(512)} %param.9) | copy-start | bytes 6148
  187.9 28.0 %copy-start.5 = (f32[512]{0:T(512)S(1)}, f32[512]{0:T(512)}, u32[]{:S(2)}) copy-start(f32[512]{0:T(512)} %param.11) | copy-start | bytes 6148
  196.2 51.2 %copy-start.3 = (f32[8192]{0:T(1024)S(1)}, f32[8192]{0:T(1024)}, u32[]{:S(2)}) copy-start(f32[8192]{0:T(1024)} %param.10) | copy-start | bytes 98308
  349.6 31.9 %copy-start.1 = (bf16[8192,256]{1,0:T(8,128)(2,1)S(1)}, bf16[8192,256]{1,0:T(8,128)(2,1)}, u32[]{:S(2)}) copy-start(bf16[8192,256]{1,0:T(8,128)(2,1)} %param.6) | copy-start | bytes 12582916
  378.2 3.2 copy-start.6
  384.6 118.3 %reduce-scatter.3.cloned.1.call-start = ((), (), s32[]{:S(2)}) async-start(), calls=%async_computation.2 | async-start | bytes 8912896 | tf_op jit(solution)/shard_map/reduce_scatter | solution.py:62
Sparse Core Ops, SparseCore 0:
  384.7 29.6 reduce-scatter.4
  418.4 84.4 reduce-scatter.2

commit v2 on v1

--- a/solution.py
+++ b/solution.py
@@ -1,8 +1,76 @@
+import functools
 import math
 
 import jax
 import jax.numpy as jnp
 from jax import lax
+from jax.experimental import pallas as pl
+from jax.experimental.pallas import tpu as pltpu
+
+MESH = pl.DeviceIdType.MESH
+
+
+def _peer(axis, k, n):
+    me_img = lax.axis_index("img")
+    me_cap = lax.axis_index("cap")
+    if axis == "cap":
+        return (me_img, lax.rem(me_cap + k, n))
+    return (lax.rem(me_img + k, n), me_cap)
+
+
+def _combine_kernel(axis, n, mode, x_ref, o_ref, buf, send_sem, recv_sem):
+    barrier = pltpu.get_barrier_semaphore()
+    for k in range(1, n):
+        pl.semaphore_signal(barrier, inc=1, device_id=_peer(axis, k, n), device_id_type=MESH)
+    pl.semaphore_wait(barrier, n - 1)
+    copies = []
+    for k in range(1, n):
+        copy = pltpu.make_async_remote_copy(
+            src_ref=x_ref,
+            dst_ref=buf.at[k],
+            send_sem=send_sem.at[k],
+            recv_sem=recv_sem.at[k],
+            device_id=_peer(axis, k, n),
+            device_id_type=MESH,
+        )
+        copy.start()
+        copies.append(copy)
+    for copy in copies:
+        copy.wait()
+    x = x_ref[...]
+    if mode == "sum":
+        acc = x
+        for k in range(1, n):
+            acc = acc + buf[k]
+    else:
+        top = x
+        for k in range(1, n):
+            top = jnp.maximum(top, buf[k])
+        tot = jnp.exp(x - top)
+        for k in range(1, n):
+            tot = tot + jnp.exp(buf[k] - top)
+        acc = top + jnp.log(tot)
+    o_ref[...] = acc
+
+
+def combine(x, axis, n, mode, cid):
+    size = x.shape[0]
+    rows = size // 128
+    x2 = x.reshape(rows, 128)
+    out = pl.pallas_call(
+        functools.partial(_combine_kernel, axis, n, mode),
+        out_shape=jax.ShapeDtypeStruct((rows, 128), jnp.float32),
+        in_specs=[pl.BlockSpec(memory_space=pltpu.VMEM)],
+        out_specs=pl.BlockSpec(memory_space=pltpu.VMEM),
+        scratch_shapes=[
+            pltpu.VMEM((n, rows, 128), jnp.float32),
+            pltpu.SemaphoreType.DMA((n,)),
+            pltpu.SemaphoreType.DMA((n,)),
+        ],
+        compiler_params=pltpu.CompilerParams(collective_id=cid, has_side_effects=True),
+    )(x2)
+    return out.reshape(size)
+
 from jax.sharding import PartitionSpec as P
 
 ITERS = 3
@@ -11,14 +79,15 @@
 SMOOTHING = 0.25
 
 
+_IDS = {("cap", "lse"): 0, ("img", "lse"): 1, ("cap", "sum"): 2, ("img", "sum"): 3}
+
+
 def gathered_lse(part, axis):
-    pieces = lax.all_gather(part, axis)
-    top = jnp.max(pieces, axis=0)
-    return top + jnp.log(jnp.sum(jnp.exp(pieces - top[None]), axis=0))
+    return combine(part, axis, lax.axis_size(axis), "lse", _IDS[(axis, "lse")])
 
 
 def gathered_sum(part, axis):
-    return jnp.sum(lax.all_gather(part, axis), axis=0)
+    return combine(part, axis, lax.axis_size(axis), "sum", _IDS[(axis, "sum")])
 
 
 def body(images, captions, image_logw, caption_logw, image_cot, caption_cot):

time: 518 us -> 453 us (0.87)
  blocking collectives: 197 us -> 0 us
  Pallas kernels: 0 us -> 119 us
  other arithmetic: 162 us -> 175 us
    all_gather x11 -> x0, blocking collectives: 197 us -> none  [the longest x6 106 us: gathered_lse(): pieces = lax.all_gather(part, axis)]
    pallas_call x0 -> x11, Pallas kernels: none -> 119 us  [combine(): pl.pallas_call(functools.partial(_combine_kernel, axis, n, mode), out_sha...]
where the time goes in v2:
time: 453 us; the launch traced here: 445 us
  other arithmetic  175 us (39%)
  Pallas kernels  119 us (26%)
  waiting for transfers between devices  110 us (24%)
  matrix products  22.4 us (5%)
  between operations  14.5 us (3%)
    pallas_call x11, Pallas kernels, combine(): pl.pallas_call(functools.partial(_combine_kernel, axis, n, mode), out_sha...  119 us
    reduce_scatter x1, waiting for transfers between devices, body(): lax.psum_scatter(jnp.dot(rounded, captions, preferred_element_type=jnp.fl...  88.2 us
    convert_element_type x1, other arithmetic, body(): rounded = adjoint.astype(jnp.bfloat16)  28.5 us
    reduce_sum x3, other arithmetic, body(): row_bar = -gathered_sum(jnp.sum(weighted, axis=1), 'cap')  26.8 us
    reduce_sum x3, other arithmetic, body(): part = top + jnp.log(jnp.sum(jnp.exp(logits - top[:, None]), axis=1))  24.8 us
    reduce_sum x3, other arithmetic, body(): part = top + jnp.log(jnp.sum(jnp.exp(logits - top[None, :]), axis=0))  24.7 us
    reduce_max x3, other arithmetic, body(): top = jnp.max(logits, axis=0)  24.1 us
    reduce_scatter x1, waiting for transfers between devices, body(): lax.psum_scatter(lax.dot_general(rounded, images, (((0,), (0,)), ((), ())...  21.5 us
  transfers between devices with their start and end apart: 2, of which 2 were waited for; matrix products, arithmetic and copies ran while one was open for 2% of the time, Pallas kernels for 0%

profile of v2, /device:TPU:0, one launch (start us, length us, event | category | flops | bytes accessed | tf_op | source)
XLA Modules:
  0.0 445.2 jit_solution(16796325085513549026)
XLA Ops:
  7.2 0.9 copy-done
  8.1 10.3 %multiply_reduce_fusion = (f32[8192]{0:T(1024)S(1)}, f32[8192,512]{0,1:T(8,128)}) fusion(bf16[8192,256]{1,0:T(8,128)(2,1)} %param.6, bf16[512,256]{1,0:T(8,128)(2,1)S(1)} %copy-done), kind=kOutput, calls=%fused_computation.17 | convolution fusion | flops 2155864064 | bytes 21266432 | tf_op jit(solution)/shard_map/dot_general | solution.py:97
  18.4 8.5 %exponential_reduce_fusion.5 = f32[8192]{0:T(1024)S(1)} fusion(f32[8192,512]{0,1:T(8,128)} %get-tuple-element.13, f32[8192]{0:T(1024)S(1)} %get-tuple-element.12), kind=kLoop, calls=%fused_computation.16 | loop fusion | flops 12574720 | bytes 16842752 | tf_op jit(solution)/shard_map/reduce_sum | solution.py:105
  26.9 0.6 add_bitcast_fusion.2.x_ref
  27.6 14.9 %shard_map.77 = f32[64,128]{1,0:T(8,128)} custom-call(f32[64,128]{1,0:T(8,128)} %add_bitcast_fusion.2.x_ref), custom_call_target="tpu_custom_call" | custom-call | tf_op jit(solution)/shard_map/pallas_call | solution.py:60
  42.4 0.8 multiply_subtract_fusion
  43.2 8.0 %fusion.5 = f32[512]{0:T(512)S(1)} fusion(f32[8192,512]{0,1:T(8,128)} %get-tuple-element.13, f32[8192]{0:T(1024)S(1)} %get-tuple-element.3), kind=kLoop, calls=%fused_computation.23 | loop fusion | flops 16776704 | bytes 16812032 | tf_op jit(solution)/shard_map/reduce_max | solution.py:109
  51.2 8.6 %exponential_reduce_fusion.4 = f32[512]{0:T(512)S(1)} fusion(f32[8192,512]{0,1:T(8,128)} %get-tuple-element.13, f32[512]{0:T(512)S(1)} %fusion.5, f32[8192]{0:T(1024)S(1)} %get-tuple-element.3), kind=kLoop, calls=%fused_computation.14 | loop fusion | flops 20971008 | bytes 16814080 | tf_op jit(solution)/shard_map/reduce_sum | solution.py:110
  60.4 8.6 %shard_map.78 = f32[4,128]{1,0:T(4,128)} custom-call(f32[4,128]{1,0:T(4,128)} %add_bitcast_fusion.5.x_ref), custom_call_target="tpu_custom_call" | custom-call | tf_op jit(solution)/shard_map/pallas_call | solution.py:60
  69.0 0.7 multiply_subtract_fusion.3
  69.7 8.2 %fusion.6 = f32[8192]{0:T(1024)S(1)} fusion(f32[8192,512]{0,1:T(8,128)} %get-tuple-element.13, f32[512]{0:T(512)S(1)} %get-tuple-element.9), kind=kLoop, calls=%fused_computation.24 | loop fusion | flops 16769024 | bytes 16812032 | tf_op jit(solution)/shard_map/reduce_max | solution.py:104
  77.9 8.0 %exponential_reduce_fusion.3 = f32[8192]{0:T(1024)S(1)} fusion(f32[8192,512]{0,1:T(8,128)} %get-tuple-element.13, f32[8192]{0:T(1024)S(1)} %fusion.6, f32[512]{0:T(512)S(1)} %get-tuple-element.9), kind=kLoop, calls=%fused_computation.12 | loop fusion | flops 20963328 | bytes 16844800 | tf_op jit(solution)/shard_map/reduce_sum | solution.py:105
  86.6 13.9 %shard_map.79 = f32[64,128]{1,0:T(8,128)} custom-call(f32[64,128]{1,0:T(8,128)} %add_bitcast_fusion.1.x_ref), custom_call_target="tpu_custom_call" | custom-call | tf_op jit(solution)/shard_map/pallas_call | solution.py:60
  100.5 0.8 multiply_subtract_fusion.1
  101.3 8.0 %fusion.7 = f32[512]{0:T(512)S(1)} fusion(f32[8192,512]{0,1:T(8,128)} %get-tuple-element.13, f32[8192]{0:T(1024)S(1)} %get-tuple-element.5), kind=kLoop, calls=%fused_computation.25 | loop fusion | flops 16776704 | bytes 16812032 | tf_op jit(solution)/shard_map/reduce_max | solution.py:109
  109.3 8.1 %exponential_reduce_fusion.2 = f32[512]{0:T(512)S(1)} fusion(f32[8192,512]{0,1:T(8,128)} %get-tuple-element.13, f32[512]{0:T(512)S(1)} %fusion.7, f32[8192]{0:T(1024)S(1)} %get-tuple-element.5), kind=kLoop, calls=%fused_computation.10 | loop fusion | flops 20971008 | bytes 16814080 | tf_op jit(solution)/shard_map/reduce_sum | solution.py:110
  118.0 6.6 %shard_map.80 = f32[4,128]{1,0:T(4,128)} custom-call(f32[4,128]{1,0:T(4,128)} %add_bitcast_fusion.4.x_ref), custom_call_target="tpu_custom_call" | custom-call | tf_op jit(solution)/shard_map/pallas_call | solution.py:60
  124.5 0.7 multiply_subtract_fusion.4
  125.2 8.2 %fusion.8 = f32[8192]{0:T(1024)S(1)} fusion(f32[8192,512]{0,1:T(8,128)} %get-tuple-element.13, f32[512]{0:T(512)S(1)} %get-tuple-element.11), kind=kLoop, calls=%fused_computation.26 | loop fusion | flops 16769024 | bytes 16812032 | tf_op jit(solution)/shard_map/reduce_max | solution.py:104
  133.5 8.2 %exponential_reduce_fusion.1 = f32[8192]{0:T(1024)S(1)} fusion(f32[8192,512]{0,1:T(8,128)} %get-tuple-element.13, f32[8192]{0:T(1024)S(1)} %fusion.8, f32[512]{0:T(512)S(1)} %get-tuple-element.11), kind=kLoop, calls=%fused_computation.8 | loop fusion | flops 20963328 | bytes 16844800 | tf_op jit(solution)/shard_map/reduce_sum | solution.py:105
  141.7 0.6 add_bitcast_fusion.x_ref
  142.3 14.0 %shard_map.81 = f32[64,128]{1,0:T(8,128)} custom-call(f32[64,128]{1,0:T(8,128)} %add_bitcast_fusion.x_ref), custom_call_target="tpu_custom_call" | custom-call | tf_op jit(solution)/shard_map/pallas_call | solution.py:60
  156.3 0.8 multiply_subtract_fusion.2
  157.1 8.0 %fusion.9 = f32[512]{0:T(512)S(1)} fusion(f32[8192,512]{0,1:T(8,128)} %get-tuple-element.13, f32[8192]{0:T(1024)S(1)} %get-tuple-element.7), kind=kLoop, calls=%fused_computation.27 | loop fusion | flops 16776704 | bytes 16812032 | tf_op jit(solution)/shard_map/reduce_max | solution.py:109
  165.1 8.1 %exponential_reduce_fusion = f32[512]{0:T(512)S(1)} fusion(f32[8192,512]{0,1:T(8,128)} %get-tuple-element.13, f32[512]{0:T(512)S(1)} %fusion.9, f32[8192]{0:T(1024)S(1)} %get-tuple-element.7), kind=kLoop, calls=%fused_computation.6 | loop fusion | flops 20971008 | bytes 16814080 | tf_op jit(solution)/shard_map/reduce_sum | solution.py:110
  173.8 6.6 %shard_map.82 = f32[4,128]{1,0:T(4,128)} custom-call(f32[4,128]{1,0:T(4,128)} %add_bitcast_fusion.3.x_ref), custom_call_target="tpu_custom_call" | custom-call | tf_op jit(solution)/shard_map/pallas_call | solution.py:60
  180.4 0.7 fusion.11
  181.1 8.9 %fusion = f32[8192]{0:T(1024)} fusion(f32[8192,512]{0,1:T(8,128)} %get-tuple-element.13, f32[512]{0:T(512)S(1)} %copy-done.5, f32[512]{0:T(512)S(1)} %fusion.11, f32[8192]{0:T(1024)S(1)} %get-tuple-element.7), kind=kLoop, calls=%fused_computation.18 | loop fusion | flops 25157632 | bytes 16846848 | tf_op jit(solution)/shard_map/reduce_sum | solution.py:121
  189.9 13.9 %shard_map.83 = f32[64,128]{1,0:T(8,128)} custom-call(f32[64,128]{1,0:T(8,128)} %bitcast.59), custom_call_target="tpu_custom_call" | custom-call | tf_op jit(solution)/shard_map/pallas_call | solution.py:60
  203.8 0.8 bitcast_add_fusion
  204.6 8.9 %fusion.1 = f32[512]{0:T(512)} fusion(f32[8192,512]{0,1:T(8,128)} %get-tuple-element.13, f32[8192]{0:T(1024)S(1)} %bitcast_add_fusion, f32[8192]{0:T(1024)S(1)} %get-tuple-element.6, f32[512]{0:T(512)S(1)} %get-tuple-element.11), kind=kLoop, calls=%fused_computation.19 | loop fusion | flops 25165312 | bytes 16846848 | tf_op jit(solution)/shard_map/reduce_sum | solution.py:129
  213.5 6.6 %shard_map.84 = f32[4,128]{1,0:T(4,128)} custom-call(f32[4,128]{1,0:T(4,128)} %bitcast.62), custom_call_target="tpu_custom_call" | custom-call | tf_op jit(solution)/shard_map/pallas_call | solution.py:60
  220.1 0.7 negate_bitcast_fusion.3
  220.8 8.9 %fusion.2 = f32[8192]{0:T(1024)} fusion(f32[8192,512]{0,1:T(8,128)} %get-tuple-element.13, f32[512]{0:T(512)S(1)} %negate_bitcast_fusion.3, f32[512]{0:T(512)S(1)} %get-tuple-element.10, f32[8192]{0:T(1024)S(1)} %get-tuple-element.5), kind=kLoop, calls=%fused_computation.20 | loop fusion | flops 25157632 | bytes 16846848 | tf_op jit(solution)/shard_map/reduce_sum | solution.py:121
  229.7 13.9 %shard_map.85 = f32[64,128]{1,0:T(8,128)} custom-call(f32[64,128]{1,0:T(8,128)} %bitcast.60), custom_call_target="tpu_custom_call" | custom-call | tf_op jit(solution)/shard_map/pallas_call | solution.py:60
  243.5 0.8 negate_bitcast_fusion.1
  244.3 8.9 %fusion.3 = f32[512]{0:T(512)} fusion(f32[8192,512]{0,1:T(8,128)} %get-tuple-element.13, f32[8192]{0:T(1024)S(1)} %negate_bitcast_fusion.1, f32[8192]{0:T(1024)S(1)} %get-tuple-element.4, f32[512]{0:T(512)S(1)} %get-tuple-element.9), kind=kLoop, calls=%fused_computation.21 | loop fusion | flops 25165312 | bytes 16846848 | tf_op jit(solution)/shard_map/reduce_sum | solution.py:129
  253.2 6.6 %shard_map.86 = f32[4,128]{1,0:T(4,128)} custom-call(f32[4,128]{1,0:T(4,128)} %bitcast.63), custom_call_target="tpu_custom_call" | custom-call | tf_op jit(solution)/shard_map/pallas_call | solution.py:60
  259.8 0.7 negate_bitcast_fusion.2
  260.5 9.1 %fusion.4 = f32[8192]{0:T(1024)} fusion(f32[8192,512]{0,1:T(8,128)} %get-tuple-element.13, f32[512]{0:T(512)S(1)} %negate_bitcast_fusion.2, f32[512]{0:T(512)S(1)} %get-tuple-element.8, f32[8192]{0:T(1024)S(1)} %get-tuple-element.3), kind=kLoop, calls=%fused_computation.22 | loop fusion | flops 25157632 | bytes 16846848 | tf_op jit(solution)/shard_map/reduce_sum | solution.py:121
  269.5 13.9 %shard_map.87 = f32[64,128]{1,0:T(8,128)} custom-call(f32[64,128]{1,0:T(8,128)} %bitcast.61), custom_call_target="tpu_custom_call" | custom-call | tf_op jit(solution)/shard_map/pallas_call | solution.py:60
  283.4 0.8 negate_bitcast_fusion
  284.2 28.5 %subtract_convert_fusion = bf16[8192,512]{0,1:T(8,128)(2,1)S(1)} fusion(f32[8192,512]{0,1:T(8,128)} %get-tuple-element.13, f32[8192]{0:T(1024)S(1)} %negate_bitcast_fusion, f32[8192]{0:T(1024)S(1)} %get-tuple-element.2, f32[512]{0:T(512)S(1)} %negate_bitcast_fusion.2, f32[512]{0:T(512)S(1)} %get-tuple-element.8, f32[8192]{0:T(1024)S(1)} %negate_bitcast_fusion.1, ...), kind=kLoop, calls=%fused_computation | loop fusion | flops 130023424 | bytes 25477120 | tf_op jit(solution)/shard_map/convert_element_type | solution.py:130
  312.7 3.2 copy-done.6
  315.9 3.1 convolution_multiply_fusion.1
  319.4 9.0 %convolution_multiply_fusion = f32[8192,256]{1,0:T(8,128)} fusion(bf16[8192,512]{0,1:T(8,128)(2,1)} %copy-done.6, bf16[512,256]{1,0:T(8,128)(2,1)S(1)} %copy-done), kind=kOutput, calls=%fused_computation.28 | convolution fusion | flops 2149580800 | bytes 17039360 | tf_op jit(solution)/shard_map/dot_general | solution.py:132
  328.3 21.5 %reduce-scatter.5.cloned.1.call-done = f32[64,256]{1,0:T(8,128)} async-done(((f32[512,256]{1,0:T(8,128)}), f32[64,256]{1,0:T(8,128)}) %reduce-scatter.5.cloned.1.call-update) | async-done | bytes 65552 | tf_op jit(solution)/shard_map/reduce_scatter | solution.py:137
  349.9 88.2 %reduce-scatter.3.cloned.1.call-done = f32[512,256]{1,0:T(8,128)} async-done(((f32[8192,256]{1,0:T(8,128)}), f32[512,256]{1,0:T(8,128)}) %reduce-scatter.3.cloned.1.call-update) | async-done | bytes 524304 | tf_op jit(solution)/shard_map/reduce_scatter | solution.py:131
  (20 shorter events, 2.8 us)
Async XLA Ops:
  7.2 1.0 copy-start
  7.2 35.3 %copy-start.2 = (f32[8192]{0:T(1024)S(1)}, f32[8192]{0:T(1024)}, u32[]{:S(2)}) copy-start(f32[8192]{0:T(1024)} %param.8) | copy-start | bytes 98308
  7.2 342.7 %reduce-scatter.5.cloned.1.call-start = ((), (), s32[]{:S(2)}) async-start(), calls=%async_computation.3 | async-start | bytes 589824 | tf_op jit(solution)/shard_map/reduce_scatter | solution.py:137
  43.2 25.8 %copy-start.4 = (f32[512]{0:T(512)S(1)}, f32[512]{0:T(512)}, u32[]{:S(2)}) copy-start(f32[512]{0:T(512)} %param.9) | copy-start | bytes 6148
  157.1 24.0 %copy-start.5 = (f32[512]{0:T(512)S(1)}, f32[512]{0:T(512)}, u32[]{:S(2)}) copy-start(f32[512]{0:T(512)} %param.11) | copy-start | bytes 6148
  165.1 38.7 %copy-start.3 = (f32[8192]{0:T(1024)S(1)}, f32[8192]{0:T(1024)}, u32[]{:S(2)}) copy-start(f32[8192]{0:T(1024)} %param.10) | copy-start | bytes 98308
  284.2 31.7 %copy-start.1 = (bf16[8192,256]{1,0:T(8,128)(2,1)S(1)}, bf16[8192,256]{1,0:T(8,128)(2,1)}, u32[]{:S(2)}) copy-start(bf16[8192,256]{1,0:T(8,128)(2,1)} %param.6) | copy-start | bytes 12582916
  312.7 3.2 copy-start.6
  319.0 119.1 %reduce-scatter.3.cloned.1.call-start = ((), (), s32[]{:S(2)}) async-start(), calls=%async_computation.2 | async-start | bytes 8912896 | tf_op jit(solution)/shard_map/reduce_scatter | solution.py:131
Sparse Core Ops, SparseCore 0:
  319.2 30.6 reduce-scatter.4
  353.8 84.2 reduce-scatter.2

commit v3 on v2

--- a/solution.py
+++ b/solution.py
@@ -90,59 +90,196 @@
     return combine(part, axis, lax.axis_size(axis), "sum", _IDS[(axis, "sum")])
 
 
+TM = 512
+
+
+def _scores(img_ref, cap_ref, inv_root):
+    return lax.dot_general(
+        img_ref[...], cap_ref[...], (((1,), (1,)), ((), ())), preferred_element_type=jnp.float32
+    ) * inv_root
+
+
+def _row_kernel(mode, inv_root, img_ref, cap_ref, a_ref, b_ref, w_ref, o_ref):
+    s = _scores(img_ref, cap_ref, inv_root)
+    if mode == "lse":
+        x = (b_ref[...] + s) / SMOOTHING
+        top = jnp.max(x, axis=1, keepdims=True)
+        o_ref[...] = top + jnp.log(jnp.sum(jnp.exp(x - top), axis=1, keepdims=True))
+    else:
+        plan = jnp.exp((a_ref[...] + s) / SMOOTHING - b_ref[...])
+        o_ref[...] = jnp.sum(plan * w_ref[...], axis=1, keepdims=True)
+
+
+def row_pass(mode, images, captions, a, b, w):
+    n, e = images.shape
+    c = captions.shape[0]
+    inv_root = 1.0 / math.sqrt(e)
+    out = pl.pallas_call(
+        functools.partial(_row_kernel, mode, inv_root),
+        out_shape=jax.ShapeDtypeStruct((n, 1), jnp.float32),
+        grid=(n // TM,),
+        in_specs=[
+            pl.BlockSpec((TM, e), lambda i: (i, 0)),
+            pl.BlockSpec((c, e), lambda i: (0, 0)),
+            pl.BlockSpec((TM, 1), lambda i: (i, 0)),
+            pl.BlockSpec((1, c), lambda i: (0, 0)),
+            pl.BlockSpec((1, c), lambda i: (0, 0)),
+        ],
+        out_specs=pl.BlockSpec((TM, 1), lambda i: (i, 0)),
+        cost_estimate=pl.CostEstimate(
+            flops=2 * n * c * e, transcendentals=n * c, bytes_accessed=n * e * 2 + c * e * 2
+        ),
+    )(images, captions, a.reshape(n, 1), b.reshape(1, c), w.reshape(1, c))
+    return out.reshape(n)
+
+
+def _col_kernel(mode, inv_root, img_ref, cap_ref, a_ref, b_ref, w_ref, o_ref, top_ref, tot_ref):
+    step = pl.program_id(0)
+    s = _scores(img_ref, cap_ref, inv_root)
+    if mode == "lse":
+        x = (a_ref[...] + s) / SMOOTHING
+
+        @pl.when(step == 0)
+        def _():
+            top_ref[...] = jnp.full(top_ref.shape, -jnp.inf, jnp.float32)
+            tot_ref[...] = jnp.zeros(tot_ref.shape, jnp.float32)
+
+        old = top_ref[...]
+        top = jnp.maximum(old, jnp.max(x, axis=0, keepdims=True))
+        tot_ref[...] = tot_ref[...] * jnp.exp(old - top) + jnp.sum(jnp.exp(x - top), axis=0, keepdims=True)
+        top_ref[...] = top
+
+        @pl.when(step == pl.num_programs(0) - 1)
+        def _():
+            o_ref[...] = top_ref[...] + jnp.log(tot_ref[...])
+    else:
+        plan = jnp.exp((b_ref[...] + s) / SMOOTHING - a_ref[...])
+
+        @pl.when(step == 0)
+        def _():
+            tot_ref[...] = jnp.zeros(tot_ref.shape, jnp.float32)
+
+        tot_ref[...] += jnp.sum(plan * w_ref[...], axis=0, keepdims=True)
+
+        @pl.when(step == pl.num_programs(0) - 1)
+        def _():
+            o_ref[...] = tot_ref[...]
+
+
+def col_pass(mode, images, captions, a, w, b):
+    n, e = images.shape
+    c = captions.shape[0]
+    inv_root = 1.0 / math.sqrt(e)
+    out = pl.pallas_call(
+        functools.partial(_col_kernel, mode, inv_root),
+        out_shape=jax.ShapeDtypeStruct((1, c), jnp.float32),
+        grid=(n // TM,),
+        in_specs=[
+            pl.BlockSpec((TM, e), lambda i: (i, 0)),
+            pl.BlockSpec((c, e), lambda i: (0, 0)),
+            pl.BlockSpec((TM, 1), lambda i: (i, 0)),
+            pl.BlockSpec((1, c), lambda i: (0, 0)),
+            pl.BlockSpec((TM, 1), lambda i: (i, 0)),
+        ],
+        out_specs=pl.BlockSpec((1, c), lambda i: (0, 0)),
+        scratch_shapes=[pltpu.VMEM((1, c), jnp.float32), pltpu.VMEM((1, c), jnp.float32)],
+        cost_estimate=pl.CostEstimate(
+            flops=2 * n * c * e, transcendentals=n * c, bytes_accessed=n * e * 2 + c * e * 2
+        ),
+    )(images, captions, a.reshape(n, 1), b.reshape(1, c), w.reshape(n, 1))
+    return out.reshape(c)
+
+
+def _final_kernel(inv_root, img_ref, cap_ref, rows_ref, cols_ref, ig_ref, cg_ref):
+    step = pl.program_id(0)
+    s = _scores(img_ref, cap_ref, inv_root)
+    rows = rows_ref[...]
+    cols = cols_ref[...]
+    logw_r = rows[:, 6:7]
+    logw_c = cols[7:8, :]
+    adjoint = jnp.zeros(s.shape, jnp.float32)
+    for level in reversed(range(ITERS)):
+        f = rows[:, level:level + 1]
+        fb = rows[:, 3 + level:4 + level]
+        g_prev = cols[level:level + 1, :]
+        g = cols[level + 1:level + 2, :]
+        gb = cols[4 + level:5 + level, :]
+        col_plan = jnp.exp((f + s) / SMOOTHING - (logw_c - g / SMOOTHING))
+        adjoint = adjoint - col_plan * gb
+        row_plan = jnp.exp((g_prev + s) / SMOOTHING - (logw_r - f / SMOOTHING))
+        adjoint = adjoint - row_plan * fb
+    rounded = adjoint.astype(jnp.bfloat16)
+    ig_ref[...] = jnp.dot(rounded, cap_ref[...], preferred_element_type=jnp.float32) * inv_root
+
+    @pl.when(step == 0)
+    def _():
+        cg_ref[...] = jnp.zeros(cg_ref.shape, jnp.float32)
+
+    cg_ref[...] += lax.dot_general(
+        rounded, img_ref[...], (((0,), (0,)), ((), ())), preferred_element_type=jnp.float32
+    ) * inv_root
+
+
+def final_pass(images, captions, rows, cols):
+    n, e = images.shape
+    c = captions.shape[0]
+    inv_root = 1.0 / math.sqrt(e)
+    return pl.pallas_call(
+        functools.partial(_final_kernel, inv_root),
+        out_shape=(
+            jax.ShapeDtypeStruct((n, e), jnp.float32),
+            jax.ShapeDtypeStruct((c, e), jnp.float32),
+        ),
+        grid=(n // TM,),
+        in_specs=[
+            pl.BlockSpec((TM, e), lambda i: (i, 0)),
+            pl.BlockSpec((c, e), lambda i: (0, 0)),
+            pl.BlockSpec((TM, 8), lambda i: (i, 0)),
+            pl.BlockSpec((8, c), lambda i: (0, 0)),
+        ],
+        out_specs=(
+            pl.BlockSpec((TM, e), lambda i: (i, 0)),
+            pl.BlockSpec((c, e), lambda i: (0, 0)),
+        ),
+        cost_estimate=pl.CostEstimate(
+            flops=6 * n * c * e, transcendentals=6 * n * c, bytes_accessed=n * e * 6 + c * e * 6
+        ),
+    )(images, captions, rows, cols)
+
+
 def body(images, captions, image_logw, caption_logw, image_cot, caption_cot):
-    inv_root = 1.0 / math.sqrt(images.shape[1])
-
-    def get_tile():
-        return jnp.dot(images, captions.T, preferred_element_type=jnp.float32) * inv_root
-
-    col_hist = [jnp.zeros((captions.shape[0],), jnp.float32)]
+    n = images.shape[0]
+    c = captions.shape[0]
+    zeros_r = jnp.zeros((n,), jnp.float32)
+    zeros_c = jnp.zeros((c,), jnp.float32)
+    col_hist = [zeros_c]
     row_hist = []
     for level in range(ITERS):
-        scores = get_tile()
-        logits = (col_hist[-1][None, :] + scores) / SMOOTHING
-        top = jnp.max(logits, axis=1)
-        part = top + jnp.log(jnp.sum(jnp.exp(logits - top[:, None]), axis=1))
+        part = row_pass("lse", images, captions, zeros_r, col_hist[-1], zeros_c)
         row_pot = SMOOTHING * image_logw - SMOOTHING * gathered_lse(part, "cap")
         row_hist.append(row_pot)
-        logits = (row_pot[:, None] + scores) / SMOOTHING
-        top = jnp.max(logits, axis=0)
-        part = top + jnp.log(jnp.sum(jnp.exp(logits - top[None, :]), axis=0))
+        part = col_pass("lse", images, captions, row_pot, zeros_r, zeros_c)
         col_hist.append(SMOOTHING * caption_logw - SMOOTHING * gathered_lse(part, "img"))
-    adjoint = jnp.zeros((images.shape[0], captions.shape[0]), jnp.float32)
     col_bar = caption_cot
+    row_bars = [None] * ITERS
+    col_bars = [None] * ITERS
     for level in reversed(range(ITERS)):
-        scores = get_tile()
-        row_pot = row_hist[level]
+        col_bars[level] = col_bar
         shift_col = caption_logw - col_hist[level + 1] / SMOOTHING
-        col_plan = jnp.exp((row_pot[:, None] + scores) / SMOOTHING - shift_col[None, :])
-        weighted = col_plan * col_bar[None, :]
-        adjoint = adjoint - weighted
-        row_bar = -gathered_sum(jnp.sum(weighted, axis=1), "cap")
+        part = row_pass("wsum", images, captions, row_hist[level], shift_col, col_bar)
+        row_bar = -gathered_sum(part, "cap")
         if level == ITERS - 1:
             row_bar = image_cot + row_bar
-        shift_row = image_logw - row_pot / SMOOTHING
-        row_plan = jnp.exp((col_hist[level][None, :] + scores) / SMOOTHING - shift_row[:, None])
-        weighted = row_plan * row_bar[:, None]
-        adjoint = adjoint - weighted
+        row_bars[level] = row_bar
         if level > 0:
-            col_bar = -gathered_sum(jnp.sum(weighted, axis=0), "img")
-    rounded = adjoint.astype(jnp.bfloat16)
-    image_grad = lax.psum_scatter(
-        jnp.dot(rounded, captions, preferred_element_type=jnp.float32) * inv_root,
-        "cap",
-        scatter_dimension=0,
-        tiled=True,
-    )
-    caption_grad = lax.psum_scatter(
-        lax.dot_general(
-            rounded, images, (((0,), (0,)), ((), ())), preferred_element_type=jnp.float32
-        )
-        * inv_root,
-        "img",
-        scatter_dimension=0,
-        tiled=True,
-    )
+            shift_row = image_logw - row_hist[level] / SMOOTHING
+            part = col_pass("wsum", images, captions, shift_row, row_bar, col_hist[level])
+            col_bar = -gathered_sum(part, "img")
+    rows = jnp.stack(row_hist + row_bars + [image_logw, zeros_r], axis=1)
+    cols = jnp.stack(col_hist + col_bars + [caption_logw], axis=0)
+    ig_part, cg_part = final_pass(images, captions, rows, cols)
+    image_grad = lax.psum_scatter(ig_part, "cap", scatter_dimension=0, tiled=True)
+    caption_grad = lax.psum_scatter(cg_part, "img", scatter_dimension=0, tiled=True)
     return (image_grad, caption_grad)
 
 

time: 453 us -> 551 us (1.22)
  Pallas kernels: 119 us -> 330 us
  other arithmetic: 175 us -> 34.5 us
  local copies, waits for them, and re-layouts: 4.13 us -> 48.4 us
  matrix products: 22.4 us -> 0 us
  waiting for transfers between devices: 110 us -> 119 us
    pallas_call x0 -> x12, Pallas kernels: none -> 211 us  [the longest x6 91.1 us: row_pass(): pl.pallas_call(functools.partial(_row_kernel, mode, inv_root), out_shape=...]
    reduce_sum x11 -> x0, other arithmetic: 94.2 us -> none  [the longest x3 26.8 us: body(): row_bar = -gathered_sum(jnp.sum(weighted, axis=1), 'cap')]
    reduce_max x5 -> x0, other arithmetic: 40.6 us -> none  [the longest x3 24.1 us: body(): top = jnp.max(logits, axis=0)]
    another operation x0 -> x8, local copies, waits for them, and re-layouts: none -> 35.2 us  [the longest x5 31.8 us: body(): rows = jnp.stack(row_hist + row_bars + [image_logw, zeros_r], axis=1)]
    convert_element_type x1 -> x0, other arithmetic: 28.5 us -> none  [body(): rounded = adjoint.astype(jnp.bfloat16)]
    pallas_call x0 -> x6, other arithmetic: none -> 23.8 us  [row_pass(): pl.pallas_call(functools.partial(_row_kernel, mode, inv_root), out_shape=...]
    dot_general x3 -> x0, matrix products: 22.4 us -> none  [the longest x1 10.3 us: get_tile(): jnp.dot(images, captions.T, preferred_element_type=jnp.float32) * inv_root]
    reduce_scatter x2, waiting for transfers between devices: 110 us -> 118 us  [the longest x1 88.1 us: body(): lax.psum_scatter(ig_part, 'cap', scatter_dimension=0, tiled=True)]
  transfers between devices with their start and end apart: 2 -> 2, of which waited for: 2 -> 2; matrix products, arithmetic and copies ran while one was open for 2% -> 0% of each run, Pallas kernels for 0% -> 0%
where the time goes in v3:
time: 551 us; the launch traced here: 546 us
  Pallas kernels  330 us (60%)
  waiting for transfers between devices  119 us (22%)
  local copies, waits for them, and re-layouts  48.4 us (9%)
  other arithmetic  34.5 us (6%)
  between operations  14.2 us (3%)
    pallas_call x11, Pallas kernels, combine(): pl.pallas_call(functools.partial(_combine_kernel, axis, n, mode), out_sha...  119 us
    pallas_call x6, Pallas kernels, row_pass(): pl.pallas_call(functools.partial(_row_kernel, mode, inv_root), out_shape=...  91.1 us
    reduce_scatter x1, waiting for transfers between devices, body(): lax.psum_scatter(ig_part, 'cap', scatter_dimension=0, tiled=True)  88.1 us
    pallas_call x5, Pallas kernels, col_pass(): pl.pallas_call(functools.partial(_col_kernel, mode, inv_root), out_shape=...  76.7 us
    pallas_call x1, Pallas kernels, final_pass(): pl.pallas_call(functools.partial(_final_kernel, inv_root), out_shape=(jax...  42.8 us
    another operation x5, local copies, waits for them, and re-layouts, body(): rows = jnp.stack(row_hist + row_bars + [image_logw, zeros_r], axis=1)  31.8 us
    reduce_scatter x1, waiting for transfers between devices, body(): lax.psum_scatter(cg_part, 'img', scatter_dimension=0, tiled=True)  30.2 us
    pallas_call x6, other arithmetic, row_pass(): pl.pallas_call(functools.partial(_row_kernel, mode, inv_root), out_shape=...  23.8 us
  transfers between devices with their start and end apart: 2, of which 2 were waited for; matrix products, arithmetic and copies ran while one was open for 0% of the time, Pallas kernels for 0%

profile of v3, /device:TPU:0, one launch (start us, length us, event | category | flops | bytes accessed | tf_op | source)
XLA Modules:
  0.0 545.9 jit_solution(17467531330588896634)
XLA Ops:
  7.2 2.2 broadcast_6_a_ref_w_ref.2.a_ref.w_ref
  10.0 15.4 %shard_map.77 = f32[8192,1]{1,0:T(8,128)} custom-call(bf16[8192,256]{1,0:T(8,128)(2,1)} %img_ref.23, bf16[512,256]{1,0:T(8,128)(2,1)} %cap_ref.23, f32[8192,1]{1,0:T(8,128)} %broadcast_6_a_ref_w_ref.2.a_ref.w_ref, f32[1,512]{1,0:T(1,128)} %broadcast_7_b_ref_w_ref.2.b_ref.w_ref, f32[1,512]{1,0:T(1,128)} %broadcast_7_b_ref_w_ref.2.b_ref.w_ref), custom_call_target="tpu_custom_call" | custom-call | flops 2147483648 | bytes 4456448 | tf_op jit(solution)/shard_map/pallas_call | solution.py:117
  25.4 4.0 reduce
  29.4 14.9 %shard_map.78 = f32[64,128]{1,0:T(8,128)} custom-call(f32[64,128]{1,0:T(8,128)} %bitcast.58), custom_call_target="tpu_custom_call" | custom-call | tf_op jit(solution)/shard_map/pallas_call | solution.py:60
  45.0 2.7 copy.47.a_ref
  47.7 15.5 %shard_map.79 = f32[1,512]{1,0:T(1,128)} custom-call(bf16[8192,256]{1,0:T(8,128)(2,1)} %img_ref.23, bf16[512,256]{1,0:T(8,128)(2,1)} %cap_ref.23, f32[8192,1]{1,0:T(8,128)} %copy.47.a_ref, f32[1,512]{1,0:T(1,128)} %broadcast_7_b_ref_w_ref.2.b_ref.w_ref, f32[8192,1]{1,0:T(8,128)} %broadcast_6_a_ref_w_ref.2.a_ref.w_ref), custom_call_target="tpu_custom_call" | custom-call | flops 2147483648 | bytes 4456448 | tf_op jit(solution)/shard_map/pallas_call | solution.py:173
  63.2 8.6 %shard_map.80 = f32[4,128]{1,0:T(4,128)} custom-call(f32[4,128]{1,0:T(4,128)} %bitcast.84), custom_call_target="tpu_custom_call" | custom-call | tf_op jit(solution)/shard_map/pallas_call | solution.py:60
  71.8 1.3 multiply_subtract_fusion.4
  73.0 15.4 %shard_map.81 = f32[8192,1]{1,0:T(8,128)} custom-call(bf16[8192,256]{1,0:T(8,128)(2,1)} %img_ref.23, bf16[512,256]{1,0:T(8,128)(2,1)} %cap_ref.23, f32[8192,1]{1,0:T(8,128)} %broadcast_6_a_ref_w_ref.2.a_ref.w_ref, f32[1,512]{1,0:T(1,128)} %bitcast.69, f32[1,512]{1,0:T(1,128)} %broadcast_7_b_ref_w_ref.2.b_ref.w_ref), custom_call_target="tpu_custom_call" | custom-call | flops 2147483648 | bytes 4456448 | tf_op jit(solution)/shard_map/pallas_call | solution.py:117
  88.5 4.0 reduce.1
  92.4 13.9 %shard_map.82 = f32[64,128]{1,0:T(8,128)} custom-call(f32[64,128]{1,0:T(8,128)} %bitcast.59), custom_call_target="tpu_custom_call" | custom-call | tf_op jit(solution)/shard_map/pallas_call | solution.py:60
  106.3 0.8 multiply_subtract_fusion.1
  107.1 2.6 copy.48.a_ref
  109.7 15.5 %shard_map.83 = f32[1,512]{1,0:T(1,128)} custom-call(bf16[8192,256]{1,0:T(8,128)(2,1)} %img_ref.23, bf16[512,256]{1,0:T(8,128)(2,1)} %cap_ref.23, f32[8192,1]{1,0:T(8,128)} %copy.48.a_ref, f32[1,512]{1,0:T(1,128)} %broadcast_7_b_ref_w_ref.2.b_ref.w_ref, f32[8192,1]{1,0:T(8,128)} %broadcast_6_a_ref_w_ref.2.a_ref.w_ref), custom_call_target="tpu_custom_call" | custom-call | flops 2147483648 | bytes 4456448 | tf_op jit(solution)/shard_map/pallas_call | solution.py:173
  125.2 6.6 %shard_map.84 = f32[4,128]{1,0:T(4,128)} custom-call(f32[4,128]{1,0:T(4,128)} %bitcast.85), custom_call_target="tpu_custom_call" | custom-call | tf_op jit(solution)/shard_map/pallas_call | solution.py:60
  131.8 1.3 multiply_subtract_fusion.3
  133.1 15.4 %shard_map.85 = f32[8192,1]{1,0:T(8,128)} custom-call(bf16[8192,256]{1,0:T(8,128)(2,1)} %img_ref.23, bf16[512,256]{1,0:T(8,128)(2,1)} %cap_ref.23, f32[8192,1]{1,0:T(8,128)} %broadcast_6_a_ref_w_ref.2.a_ref.w_ref, f32[1,512]{1,0:T(1,128)} %bitcast.72, f32[1,512]{1,0:T(1,128)} %broadcast_7_b_ref_w_ref.2.b_ref.w_ref), custom_call_target="tpu_custom_call" | custom-call | flops 2147483648 | bytes 4456448 | tf_op jit(solution)/shard_map/pallas_call | solution.py:117
  148.4 4.0 reduce.2
  152.4 14.0 %shard_map.86 = f32[64,128]{1,0:T(8,128)} custom-call(f32[64,128]{1,0:T(8,128)} %bitcast.60), custom_call_target="tpu_custom_call" | custom-call | tf_op jit(solution)/shard_map/pallas_call | solution.py:60
  167.2 2.6 copy.49.a_ref
  169.8 2.6 copy.44.a_ref
  172.5 2.6 copy.41.a_ref
  175.1 15.5 %shard_map.87 = f32[1,512]{1,0:T(1,128)} custom-call(bf16[8192,256]{1,0:T(8,128)(2,1)} %img_ref.23, bf16[512,256]{1,0:T(8,128)(2,1)} %cap_ref.23, f32[8192,1]{1,0:T(8,128)} %copy.49.a_ref, f32[1,512]{1,0:T(1,128)} %broadcast_7_b_ref_w_ref.2.b_ref.w_ref, f32[8192,1]{1,0:T(8,128)} %broadcast_6_a_ref_w_ref.2.a_ref.w_ref), custom_call_target="tpu_custom_call" | custom-call | flops 2147483648 | bytes 4456448 | tf_op jit(solution)/shard_map/pallas_call | solution.py:173
  190.5 6.6 %shard_map.88 = f32[4,128]{1,0:T(4,128)} custom-call(f32[4,128]{1,0:T(4,128)} %bitcast.86), custom_call_target="tpu_custom_call" | custom-call | tf_op jit(solution)/shard_map/pallas_call | solution.py:60
  197.1 1.3 bitcast_subtract_fusion.3
  198.4 15.0 %shard_map.89 = f32[8192,1]{1,0:T(8,128)} custom-call(bf16[8192,256]{1,0:T(8,128)(2,1)} %img_ref.23, bf16[512,256]{1,0:T(8,128)(2,1)} %cap_ref.23, f32[8192,1]{1,0:T(8,128)} %copy.49.a_ref, f32[1,512]{1,0:T(1,128)} %bitcast.89, f32[1,512]{1,0:T(1,128)} %bitcast.80), custom_call_target="tpu_custom_call" | custom-call | flops 2147483648 | bytes 4456448 | tf_op jit(solution)/shard_map/pallas_call | solution.py:117
  213.4 4.0 reduce.3
  217.3 13.9 %shard_map.90 = f32[64,128]{1,0:T(8,128)} custom-call(f32[64,128]{1,0:T(8,128)} %bitcast.61), custom_call_target="tpu_custom_call" | custom-call | tf_op jit(solution)/shard_map/pallas_call | solution.py:60
  232.0 2.6 copy.42.w_ref
  234.6 15.1 %shard_map.91 = f32[1,512]{1,0:T(1,128)} custom-call(bf16[8192,256]{1,0:T(8,128)(2,1)} %img_ref.23, bf16[512,256]{1,0:T(8,128)(2,1)} %cap_ref.23, f32[8192,1]{1,0:T(8,128)} %copy.41.a_ref, f32[1,512]{1,0:T(1,128)} %bitcast.73, f32[8192,1]{1,0:T(8,128)} %copy.42.w_ref), custom_call_target="tpu_custom_call" | custom-call | flops 2147483648 | bytes 4456448 | tf_op jit(solution)/shard_map/pallas_call | solution.py:173
  249.7 6.5 %shard_map.92 = f32[4,128]{1,0:T(4,128)} custom-call(f32[4,128]{1,0:T(4,128)} %bitcast.82), custom_call_target="tpu_custom_call" | custom-call | tf_op jit(solution)/shard_map/pallas_call | solution.py:60
  256.2 1.2 neg.60
  257.4 15.0 %shard_map.93 = f32[8192,1]{1,0:T(8,128)} custom-call(bf16[8192,256]{1,0:T(8,128)(2,1)} %img_ref.23, bf16[512,256]{1,0:T(8,128)(2,1)} %cap_ref.23, f32[8192,1]{1,0:T(8,128)} %copy.48.a_ref, f32[1,512]{1,0:T(1,128)} %bitcast.88, f32[1,512]{1,0:T(1,128)} %bitcast.76), custom_call_target="tpu_custom_call" | custom-call | flops 2147483648 | bytes 4456448 | tf_op jit(solution)/shard_map/pallas_call | solution.py:117
  272.4 4.0 reduce.4
  276.3 13.9 %shard_map.94 = f32[64,128]{1,0:T(8,128)} custom-call(f32[64,128]{1,0:T(8,128)} %bitcast.62), custom_call_target="tpu_custom_call" | custom-call | tf_op jit(solution)/shard_map/pallas_call | solution.py:60
  291.0 2.6 copy.45.w_ref
  293.6 15.1 %shard_map.95 = f32[1,512]{1,0:T(1,128)} custom-call(bf16[8192,256]{1,0:T(8,128)(2,1)} %img_ref.23, bf16[512,256]{1,0:T(8,128)(2,1)} %cap_ref.23, f32[8192,1]{1,0:T(8,128)} %copy.44.a_ref, f32[1,512]{1,0:T(1,128)} %bitcast.70, f32[8192,1]{1,0:T(8,128)} %copy.45.w_ref), custom_call_target="tpu_custom_call" | custom-call | flops 2147483648 | bytes 4456448 | tf_op jit(solution)/shard_map/pallas_call | solution.py:173
  308.8 6.5 %shard_map.96 = f32[4,128]{1,0:T(4,128)} custom-call(f32[4,128]{1,0:T(4,128)} %bitcast.83), custom_call_target="tpu_custom_call" | custom-call | tf_op jit(solution)/shard_map/pallas_call | solution.py:60
  315.3 1.1 neg.64
  316.4 14.9 %shard_map.97 = f32[8192,1]{1,0:T(8,128)} custom-call(bf16[8192,256]{1,0:T(8,128)(2,1)} %img_ref.23, bf16[512,256]{1,0:T(8,128)(2,1)} %cap_ref.23, f32[8192,1]{1,0:T(8,128)} %copy.47.a_ref, f32[1,512]{1,0:T(1,128)} %bitcast.87, f32[1,512]{1,0:T(1,128)} %bitcast.78), custom_call_target="tpu_custom_call" | custom-call | flops 2147483648 | bytes 4456448 | tf_op jit(solution)/shard_map/pallas_call | solution.py:117
  331.4 4.0 reduce.5
  335.3 13.9 %shard_map.98 = f32[64,128]{1,0:T(8,128)} custom-call(f32[64,128]{1,0:T(8,128)} %bitcast.57), custom_call_target="tpu_custom_call" | custom-call | tf_op jit(solution)/shard_map/pallas_call | solution.py:60
  350.0 2.6 copy.50
  352.6 2.7 copy.53
  355.3 21.2 %stack.36.rows_ref = f32[8192,8]{1,0:T(8,128)} concatenate(f32[8192,1]{1,0:T(8,128)} %copy.47.a_ref, f32[8192,1]{1,0:T(8,128)} %copy.48.a_ref, f32[8192,1]{1,0:T(8,128)} %copy.49.a_ref, f32[8192,1]{1,0:T(8,128)} %copy.50, f32[8192,1]{1,0:T(8,128)} %copy.45.w_ref, f32[8192,1]{1,0:T(8,128)} %copy.42.w_ref, f32[8192,1]{1,0:T(8,128)} %copy.53, ...), dimensions={1} | concatenate | bytes 524288 | tf_op jit(solution)/shard_map/stack | solution.py:278
  377.2 42.8 %shard_map.99 = (f32[8192,256]{1,0:T(8,128)}, f32[512,256]{1,0:T(8,128)}) custom-call(bf16[8192,256]{1,0:T(8,128)(2,1)} %img_ref.23, bf16[512,256]{1,0:T(8,128)(2,1)} %cap_ref.23, f32[8192,8]{1,0:T(8,128)} %stack.36.rows_ref, f32[8,512]{1,0:T(8,128)} %stack.39.cols_ref), custom_call_target="tpu_custom_call" | custom-call | flops 6442450944 | bytes 13369344 | tf_op jit(solution)/shard_map/pallas_call | solution.py:227
  420.8 30.2 %reduce-scatter.5.cloned.1.call-done = f32[64,256]{1,0:T(8,128)} async-done(((f32[512,256]{1,0:T(8,128)}), f32[64,256]{1,0:T(8,128)}) %reduce-scatter.5.cloned.1.call-update) | async-done | bytes 65552 | tf_op jit(solution)/shard_map/reduce_scatter | solution.py:282
  450.9 88.1 %reduce-scatter.3.cloned.1.call-done = f32[512,256]{1,0:T(8,128)} async-done(((f32[8192,256]{1,0:T(8,128)}), f32[512,256]{1,0:T(8,128)}) %reduce-scatter.3.cloned.1.call-update) | async-done | bytes 524304 | tf_op jit(solution)/shard_map/reduce_scatter | solution.py:281
  (29 shorter events, 5.9 us)
Async XLA Ops:
  7.2 443.8 %reduce-scatter.5.cloned.1.call-start = ((), (), s32[]{:S(2)}) async-start(), calls=%async_computation.3 | async-start | bytes 589824 | tf_op jit(solution)/shard_map/reduce_scatter | solution.py:282
  25.4 18.8 %copy-start = (f32[8192]{0:T(1024)S(1)}, f32[8192]{0:T(1024)}, u32[]{:S(2)}) copy-start(f32[8192]{0:T(1024)} %param.8) | copy-start | bytes 98308
  47.7 24.1 %copy-start.5 = (f32[512]{0:T(512)S(1)}, f32[512]{0:T(512)}, u32[]{:S(2)}) copy-start(f32[512]{0:T(512)} %param.9) | copy-start | bytes 6148
  213.4 17.9 %copy-start.4 = (f32[8192]{0:T(1024)S(1)}, f32[8192]{0:T(1024)}, u32[]{:S(2)}) copy-start(f32[8192]{0:T(1024)} %param.10) | copy-start | bytes 98308
  355.3 21.2 %copy-start.1 = (f32[1,512]{1,0:T(1,128)S(1)}, f32[1,512]{1,0:T(1,128)}, u32[]{:S(2)}) copy-start(f32[1,512]{1,0:T(1,128)} %broadcast_7_b_ref_w_ref.2.b_ref.w_ref) | copy-start | bytes 6148
  355.3 21.2 %copy-start.2 = (f32[512]{0:T(512)S(1)}, f32[512]{0:T(512)}, u32[]{:S(2)}) copy-start(f32[512]{0:T(512)} %get-tuple-element.15) | copy-start | bytes 6148
  355.3 21.2 %copy-start.3 = (f32[512]{0:T(512)S(1)}, f32[512]{0:T(512)}, u32[]{:S(2)}) copy-start(f32[512]{0:T(512)} %get-tuple-element.13) | copy-start | bytes 6148
  355.3 21.2 %copy-start.6 = (f32[4,128]{1,0:T(4,128)S(1)}, f32[4,128]{1,0:T(4,128)}, u32[]{:S(2)}) copy-start(f32[4,128]{1,0:T(4,128)} %neg.60) | copy-start | bytes 6148
  355.3 21.2 %copy-start.7 = (f32[4,128]{1,0:T(4,128)S(1)}, f32[4,128]{1,0:T(4,128)}, u32[]{:S(2)}) copy-start(f32[4,128]{1,0:T(4,128)} %neg.64) | copy-start | bytes 6148
  355.3 21.2 %copy-start.8 = (f32[512]{0:T(512)S(1)}, f32[512]{0:T(512)}, u32[]{:S(2)}) copy-start(f32[512]{0:T(512)} %param.11) | copy-start | bytes 6148
  420.0 119.1 %reduce-scatter.3.cloned.1.call-start = ((), (), s32[]{:S(2)}) async-start(), calls=%async_computation.2 | async-start | bytes 8912896 | tf_op jit(solution)/shard_map/reduce_scatter | solution.py:281
Sparse Core Ops, SparseCore 0:
  420.1 30.7 reduce-scatter.4
  454.9 84.1 reduce-scatter.2

commit v4 on v3

--- a/solution.py
+++ b/solution.py
@@ -90,24 +90,38 @@
     return combine(part, axis, lax.axis_size(axis), "sum", _IDS[(axis, "sum")])
 
 
-TM = 512
-
-
-def _scores(img_ref, cap_ref, inv_root):
+TM = 1024
+INV_EPS = 1.0 / SMOOTHING
+
+
+def _scores_t(img_ref, cap_ref, inv_root):
     return lax.dot_general(
-        img_ref[...], cap_ref[...], (((1,), (1,)), ((), ())), preferred_element_type=jnp.float32
+        cap_ref[...], img_ref[...], (((1,), (1,)), ((), ())), preferred_element_type=jnp.float32
     ) * inv_root
 
 
+def _lane_chunks(x):
+    return [x[:, k * 128:(k + 1) * 128] for k in range(x.shape[1] // 128)]
+
+
 def _row_kernel(mode, inv_root, img_ref, cap_ref, a_ref, b_ref, w_ref, o_ref):
-    s = _scores(img_ref, cap_ref, inv_root)
+    s = _scores_t(img_ref, cap_ref, inv_root)
     if mode == "lse":
-        x = (b_ref[...] + s) / SMOOTHING
-        top = jnp.max(x, axis=1, keepdims=True)
-        o_ref[...] = top + jnp.log(jnp.sum(jnp.exp(x - top), axis=1, keepdims=True))
+        x = (b_ref[...] + s) * INV_EPS
+        top = jnp.max(x, axis=0, keepdims=True)
+        o_ref[...] = top + jnp.log(jnp.sum(jnp.exp(x - top), axis=0, keepdims=True))
     else:
-        plan = jnp.exp((a_ref[...] + s) / SMOOTHING - b_ref[...])
-        o_ref[...] = jnp.sum(plan * w_ref[...], axis=1, keepdims=True)
+        plan = jnp.exp((a_ref[...] + s) * INV_EPS - b_ref[...])
+        o_ref[...] = jnp.sum(plan * w_ref[...], axis=0, keepdims=True)
+
+
+def _specs(n, c, e):
+    return [
+        pl.BlockSpec((TM, e), lambda i: (i, 0)),
+        pl.BlockSpec((c, e), lambda i: (0, 0)),
+        pl.BlockSpec((1, TM), lambda i: (0, i)),
+        pl.BlockSpec((c, 1), lambda i: (0, 0)),
+    ]
 
 
 def row_pass(mode, images, captions, a, b, w):
@@ -116,54 +130,60 @@
     inv_root = 1.0 / math.sqrt(e)
     out = pl.pallas_call(
         functools.partial(_row_kernel, mode, inv_root),
-        out_shape=jax.ShapeDtypeStruct((n, 1), jnp.float32),
+        out_shape=jax.ShapeDtypeStruct((1, n), jnp.float32),
         grid=(n // TM,),
-        in_specs=[
-            pl.BlockSpec((TM, e), lambda i: (i, 0)),
-            pl.BlockSpec((c, e), lambda i: (0, 0)),
-            pl.BlockSpec((TM, 1), lambda i: (i, 0)),
-            pl.BlockSpec((1, c), lambda i: (0, 0)),
-            pl.BlockSpec((1, c), lambda i: (0, 0)),
-        ],
-        out_specs=pl.BlockSpec((TM, 1), lambda i: (i, 0)),
+        in_specs=_specs(n, c, e) + [pl.BlockSpec((c, 1), lambda i: (0, 0))],
+        out_specs=pl.BlockSpec((1, TM), lambda i: (0, i)),
         cost_estimate=pl.CostEstimate(
             flops=2 * n * c * e, transcendentals=n * c, bytes_accessed=n * e * 2 + c * e * 2
         ),
-    )(images, captions, a.reshape(n, 1), b.reshape(1, c), w.reshape(1, c))
+    )(images, captions, a.reshape(1, n), b.reshape(c, 1), w.reshape(c, 1))
     return out.reshape(n)
 
 
 def _col_kernel(mode, inv_root, img_ref, cap_ref, a_ref, b_ref, w_ref, o_ref, top_ref, tot_ref):
     step = pl.program_id(0)
-    s = _scores(img_ref, cap_ref, inv_root)
+    s = _scores_t(img_ref, cap_ref, inv_root)
     if mode == "lse":
-        x = (a_ref[...] + s) / SMOOTHING
+        chunks = _lane_chunks((a_ref[...] + s) * INV_EPS)
 
         @pl.when(step == 0)
         def _():
             top_ref[...] = jnp.full(top_ref.shape, -jnp.inf, jnp.float32)
             tot_ref[...] = jnp.zeros(tot_ref.shape, jnp.float32)
 
+        cmax = chunks[0]
+        for piece in chunks[1:]:
+            cmax = jnp.maximum(cmax, piece)
         old = top_ref[...]
-        top = jnp.maximum(old, jnp.max(x, axis=0, keepdims=True))
-        tot_ref[...] = tot_ref[...] * jnp.exp(old - top) + jnp.sum(jnp.exp(x - top), axis=0, keepdims=True)
+        top = jnp.maximum(old, cmax)
+        tot = tot_ref[...] * jnp.exp(old - top)
+        for piece in chunks:
+            tot = tot + jnp.exp(piece - top)
+        tot_ref[...] = tot
         top_ref[...] = top
 
         @pl.when(step == pl.num_programs(0) - 1)
         def _():
-            o_ref[...] = top_ref[...] + jnp.log(tot_ref[...])
+            t = top_ref[...]
+            m = jnp.max(t, axis=1, keepdims=True)
+            o_ref[...] = m + jnp.log(jnp.sum(tot_ref[...] * jnp.exp(t - m), axis=1, keepdims=True))
     else:
-        plan = jnp.exp((b_ref[...] + s) / SMOOTHING - a_ref[...])
+        plan = jnp.exp((b_ref[...] + s) * INV_EPS - a_ref[...])
+        chunks = _lane_chunks(plan * w_ref[...])
 
         @pl.when(step == 0)
         def _():
             tot_ref[...] = jnp.zeros(tot_ref.shape, jnp.float32)
 
-        tot_ref[...] += jnp.sum(plan * w_ref[...], axis=0, keepdims=True)
+        acc = chunks[0]
+        for piece in chunks[1:]:
+            acc = acc + piece
+        tot_ref[...] += acc
 
         @pl.when(step == pl.num_programs(0) - 1)
         def _():
-            o_ref[...] = tot_ref[...]
+            o_ref[...] = jnp.sum(tot_ref[...], axis=1, keepdims=True)
 
 
 def col_pass(mode, images, captions, a, w, b):
@@ -172,52 +192,46 @@
     inv_root = 1.0 / math.sqrt(e)
     out = pl.pallas_call(
         functools.partial(_col_kernel, mode, inv_root),
-        out_shape=jax.ShapeDtypeStruct((1, c), jnp.float32),
+        out_shape=jax.ShapeDtypeStruct((c, 1), jnp.float32),
         grid=(n // TM,),
-        in_specs=[
-            pl.BlockSpec((TM, e), lambda i: (i, 0)),
-            pl.BlockSpec((c, e), lambda i: (0, 0)),
-            pl.BlockSpec((TM, 1), lambda i: (i, 0)),
-            pl.BlockSpec((1, c), lambda i: (0, 0)),
-            pl.BlockSpec((TM, 1), lambda i: (i, 0)),
-        ],
-        out_specs=pl.BlockSpec((1, c), lambda i: (0, 0)),
-        scratch_shapes=[pltpu.VMEM((1, c), jnp.float32), pltpu.VMEM((1, c), jnp.float32)],
+        in_specs=_specs(n, c, e) + [pl.BlockSpec((1, TM), lambda i: (0, i))],
+        out_specs=pl.BlockSpec((c, 1), lambda i: (0, 0)),
+        scratch_shapes=[pltpu.VMEM((c, 128), jnp.float32), pltpu.VMEM((c, 128), jnp.float32)],
         cost_estimate=pl.CostEstimate(
             flops=2 * n * c * e, transcendentals=n * c, bytes_accessed=n * e * 2 + c * e * 2
         ),
-    )(images, captions, a.reshape(n, 1), b.reshape(1, c), w.reshape(n, 1))
+    )(images, captions, a.reshape(1, n), b.reshape(c, 1), w.reshape(1, n))
     return out.reshape(c)
 
 
 def _final_kernel(inv_root, img_ref, cap_ref, rows_ref, cols_ref, ig_ref, cg_ref):
     step = pl.program_id(0)
-    s = _scores(img_ref, cap_ref, inv_root)
+    s = _scores_t(img_ref, cap_ref, inv_root)
     rows = rows_ref[...]
     cols = cols_ref[...]
-    logw_r = rows[:, 6:7]
-    logw_c = cols[7:8, :]
+    logw_r = rows[6:7, :]
+    logw_c = cols[:, 7:8]
     adjoint = jnp.zeros(s.shape, jnp.float32)
     for level in reversed(range(ITERS)):
-        f = rows[:, level:level + 1]
-        fb = rows[:, 3 + level:4 + level]
-        g_prev = cols[level:level + 1, :]
-        g = cols[level + 1:level + 2, :]
-        gb = cols[4 + level:5 + level, :]
-        col_plan = jnp.exp((f + s) / SMOOTHING - (logw_c - g / SMOOTHING))
+        f = rows[level:level + 1, :]
+        fb = rows[3 + level:4 + level, :]
+        g_prev = cols[:, level:level + 1]
+        g = cols[:, level + 1:level + 2]
+        gb = cols[:, 4 + level:5 + level]
+        col_plan = jnp.exp((f + s) * INV_EPS - (logw_c - g * INV_EPS))
         adjoint = adjoint - col_plan * gb
-        row_plan = jnp.exp((g_prev + s) / SMOOTHING - (logw_r - f / SMOOTHING))
+        row_plan = jnp.exp((g_prev + s) * INV_EPS - (logw_r - f * INV_EPS))
         adjoint = adjoint - row_plan * fb
     rounded = adjoint.astype(jnp.bfloat16)
-    ig_ref[...] = jnp.dot(rounded, cap_ref[...], preferred_element_type=jnp.float32) * inv_root
+    ig_ref[...] = lax.dot_general(
+        rounded, cap_ref[...], (((0,), (0,)), ((), ())), preferred_element_type=jnp.float32
+    ) * inv_root
 
     @pl.when(step == 0)
     def _():
         cg_ref[...] = jnp.zeros(cg_ref.shape, jnp.float32)
 
-    cg_ref[...] += lax.dot_general(
-        rounded, img_ref[...], (((0,), (0,)), ((), ())), preferred_element_type=jnp.float32
-    ) * inv_root
+    cg_ref[...] += jnp.dot(rounded, img_ref[...], preferred_element_type=jnp.float32) * inv_root
 
 
 def final_pass(images, captions, rows, cols):
@@ -234,8 +248,8 @@
         in_specs=[
             pl.BlockSpec((TM, e), lambda i: (i, 0)),
             pl.BlockSpec((c, e), lambda i: (0, 0)),
-            pl.BlockSpec((TM, 8), lambda i: (i, 0)),
-            pl.BlockSpec((8, c), lambda i: (0, 0)),
+            pl.BlockSpec((8, TM), lambda i: (0, i)),
+            pl.BlockSpec((c, 8), lambda i: (0, 0)),
         ],
         out_specs=(
             pl.BlockSpec((TM, e), lambda i: (i, 0)),
@@ -275,8 +289,8 @@
             shift_row = image_logw - row_hist[level] / SMOOTHING
             part = col_pass("wsum", images, captions, shift_row, row_bar, col_hist[level])
             col_bar = -gathered_sum(part, "img")
-    rows = jnp.stack(row_hist + row_bars + [image_logw, zeros_r], axis=1)
-    cols = jnp.stack(col_hist + col_bars + [caption_logw], axis=0)
+    rows = jnp.stack(row_hist + row_bars + [image_logw, zeros_r], axis=0)
+    cols = jnp.stack(col_hist + col_bars + [caption_logw], axis=1)
     ig_part, cg_part = final_pass(images, captions, rows, cols)
     image_grad = lax.psum_scatter(ig_part, "cap", scatter_dimension=0, tiled=True)
     caption_grad = lax.psum_scatter(cg_part, "img", scatter_dimension=0, tiled=True)

time: 551 us -> 434 us (0.79)
  Pallas kernels: 330 us -> 266 us
  local copies, waits for them, and re-layouts: 48.4 us -> 11.8 us
  other arithmetic: 34.5 us -> 19.5 us
    pallas_call x6, Pallas kernels: 91.1 us -> 57 us  [row_pass(): pl.pallas_call(functools.partial(_row_kernel, mode, inv_root), out_shape=...]
    another operation x8 -> x6, local copies, waits for them, and re-layouts: 35.2 us -> 4.18 us  [the longest x3 1.73 us: body(): cols = jnp.stack(col_hist + col_bars + [caption_logw], axis=1)]
    pallas_call x5, Pallas kernels: 76.7 us -> 49.9 us  [col_pass(): pl.pallas_call(functools.partial(_col_kernel, mode, inv_root), out_shape=...]
    pallas_call x6 -> x5, other arithmetic: 23.8 us -> 8.38 us  [col_pass(): pl.pallas_call(functools.partial(_col_kernel, mode, inv_root), out_shape=...]
where the time goes in v4:
time: 434 us; the launch traced here: 430 us
  Pallas kernels  266 us (61%)
  waiting for transfers between devices  119 us (27%)
  other arithmetic  19.5 us (4%)
  between operations  14.3 us (3%)
  local copies, waits for them, and re-layouts  11.8 us (3%)
    pallas_call x11, Pallas kernels, combine(): pl.pallas_call(functools.partial(_combine_kernel, axis, n, mode), out_sha...  119 us
    reduce_scatter x1, waiting for transfers between devices, body(): lax.psum_scatter(ig_part, 'cap', scatter_dimension=0, tiled=True)  88.2 us
    pallas_call x6, Pallas kernels, row_pass(): pl.pallas_call(functools.partial(_row_kernel, mode, inv_root), out_shape=...  57 us
    pallas_call x5, Pallas kernels, col_pass(): pl.pallas_call(functools.partial(_col_kernel, mode, inv_root), out_shape=...  49.9 us
    pallas_call x1, Pallas kernels, final_pass(): pl.pallas_call(functools.partial(_final_kernel, inv_root), out_shape=(jax...  39.7 us
    reduce_scatter x1, waiting for transfers between devices, body(): lax.psum_scatter(cg_part, 'img', scatter_dimension=0, tiled=True)  30.1 us
  transfers between devices with their start and end apart: 2, of which 2 were waited for; matrix products, arithmetic and copies ran while one was open for 0% of the time, Pallas kernels for 0%

profile of v4, /device:TPU:0, one launch (start us, length us, event | category | flops | bytes accessed | tf_op | source)
XLA Modules:
  0.0 430.4 jit_solution(15181287355237278994)
XLA Ops:
  7.9 0.7 broadcast_7_b_ref_w_ref.2.b_ref.w_ref
  8.6 10.0 %shard_map.77 = f32[1,8192]{1,0:T(1,128)} custom-call(bf16[8192,256]{1,0:T(8,128)(2,1)} %img_ref.23, bf16[512,256]{1,0:T(8,128)(2,1)} %cap_ref.23, f32[1,8192]{1,0:T(1,128)} %broadcast_6_a_ref_w_ref.2.a_ref.w_ref, f32[512,1]{1,0:T(8,128)} %broadcast_7_b_ref_w_ref.2.b_ref.w_ref, f32[512,1]{1,0:T(8,128)} %broadcast_7_b_ref_w_ref.2.b_ref.w_ref), custom_call_target="tpu_custom_call" | custom-call | flops 2147483648 | bytes 4456448 | tf_op jit(solution)/shard_map/pallas_call | solution.py:131
  18.6 14.9 %shard_map.78 = f32[64,128]{1,0:T(8,128)} custom-call(f32[64,128]{1,0:T(8,128)} %bitcast.73), custom_call_target="tpu_custom_call" | custom-call | tf_op jit(solution)/shard_map/pallas_call | solution.py:60
  33.5 1.5 copy.40.w_ref
  35.0 1.4 bitcast_subtract_fusion.2
  36.4 10.3 %shard_map.79 = f32[512,1]{1,0:T(8,128)} custom-call(bf16[8192,256]{1,0:T(8,128)(2,1)} %img_ref.23, bf16[512,256]{1,0:T(8,128)(2,1)} %cap_ref.23, f32[1,8192]{1,0:T(1,128)} %bitcast.55, f32[512,1]{1,0:T(8,128)} %broadcast_7_b_ref_w_ref.2.b_ref.w_ref, f32[1,8192]{1,0:T(1,128)} %broadcast_6_a_ref_w_ref.2.a_ref.w_ref), custom_call_target="tpu_custom_call" | custom-call | flops 2147483648 | bytes 4456448 | tf_op jit(solution)/shard_map/pallas_call | solution.py:193
  46.7 1.7 reduce
  48.4 8.5 %shard_map.80 = f32[4,128]{1,0:T(4,128)} custom-call(f32[4,128]{1,0:T(4,128)} %bitcast.79), custom_call_target="tpu_custom_call" | custom-call | tf_op jit(solution)/shard_map/pallas_call | solution.py:60
  57.7 0.9 copy.37.b_ref
  58.5 9.9 %shard_map.81 = f32[1,8192]{1,0:T(1,128)} custom-call(bf16[8192,256]{1,0:T(8,128)(2,1)} %img_ref.23, bf16[512,256]{1,0:T(8,128)(2,1)} %cap_ref.23, f32[1,8192]{1,0:T(1,128)} %broadcast_6_a_ref_w_ref.2.a_ref.w_ref, f32[512,1]{1,0:T(8,128)} %copy.37.b_ref, f32[512,1]{1,0:T(8,128)} %broadcast_7_b_ref_w_ref.2.b_ref.w_ref), custom_call_target="tpu_custom_call" | custom-call | flops 2147483648 | bytes 4456448 | tf_op jit(solution)/shard_map/pallas_call | solution.py:131
  68.4 13.9 %shard_map.82 = f32[64,128]{1,0:T(8,128)} custom-call(f32[64,128]{1,0:T(8,128)} %bitcast.74), custom_call_target="tpu_custom_call" | custom-call | tf_op jit(solution)/shard_map/pallas_call | solution.py:60
  82.4 1.4 multiply_subtract_fusion.1
  83.8 0.9 copy.45.b_ref
  84.6 10.4 %shard_map.83 = f32[512,1]{1,0:T(8,128)} custom-call(bf16[8192,256]{1,0:T(8,128)(2,1)} %img_ref.23, bf16[512,256]{1,0:T(8,128)(2,1)} %cap_ref.23, f32[1,8192]{1,0:T(1,128)} %bitcast.63, f32[512,1]{1,0:T(8,128)} %broadcast_7_b_ref_w_ref.2.b_ref.w_ref, f32[1,8192]{1,0:T(1,128)} %broadcast_6_a_ref_w_ref.2.a_ref.w_ref), custom_call_target="tpu_custom_call" | custom-call | flops 2147483648 | bytes 4456448 | tf_op jit(solution)/shard_map/pallas_call | solution.py:193
  95.0 1.7 reduce.1
  96.7 6.6 %shard_map.84 = f32[4,128]{1,0:T(4,128)} custom-call(f32[4,128]{1,0:T(4,128)} %bitcast.80), custom_call_target="tpu_custom_call" | custom-call | tf_op jit(solution)/shard_map/pallas_call | solution.py:60
  103.9 0.9 copy.38.b_ref
  104.8 9.9 %shard_map.85 = f32[1,8192]{1,0:T(1,128)} custom-call(bf16[8192,256]{1,0:T(8,128)(2,1)} %img_ref.23, bf16[512,256]{1,0:T(8,128)(2,1)} %cap_ref.23, f32[1,8192]{1,0:T(1,128)} %broadcast_6_a_ref_w_ref.2.a_ref.w_ref, f32[512,1]{1,0:T(8,128)} %copy.38.b_ref, f32[512,1]{1,0:T(8,128)} %broadcast_7_b_ref_w_ref.2.b_ref.w_ref), custom_call_target="tpu_custom_call" | custom-call | flops 2147483648 | bytes 4456448 | tf_op jit(solution)/shard_map/pallas_call | solution.py:131
  114.7 14.0 %shard_map.86 = f32[64,128]{1,0:T(8,128)} custom-call(f32[64,128]{1,0:T(8,128)} %bitcast.75), custom_call_target="tpu_custom_call" | custom-call | tf_op jit(solution)/shard_map/pallas_call | solution.py:60
  128.7 1.4 multiply_subtract_fusion
  130.1 0.9 copy.42.b_ref
  130.9 10.4 %shard_map.87 = f32[512,1]{1,0:T(8,128)} custom-call(bf16[8192,256]{1,0:T(8,128)(2,1)} %img_ref.23, bf16[512,256]{1,0:T(8,128)(2,1)} %cap_ref.23, f32[1,8192]{1,0:T(1,128)} %bitcast.66, f32[512,1]{1,0:T(8,128)} %broadcast_7_b_ref_w_ref.2.b_ref.w_ref, f32[1,8192]{1,0:T(1,128)} %broadcast_6_a_ref_w_ref.2.a_ref.w_ref), custom_call_target="tpu_custom_call" | custom-call | flops 2147483648 | bytes 4456448 | tf_op jit(solution)/shard_map/pallas_call | solution.py:193
  141.3 1.7 reduce.2
  143.0 6.6 %shard_map.88 = f32[4,128]{1,0:T(4,128)} custom-call(f32[4,128]{1,0:T(4,128)} %bitcast.81), custom_call_target="tpu_custom_call" | custom-call | tf_op jit(solution)/shard_map/pallas_call | solution.py:60
  150.3 0.9 copy.39.b_ref
  151.1 9.0 %shard_map.89 = f32[1,8192]{1,0:T(1,128)} custom-call(bf16[8192,256]{1,0:T(8,128)(2,1)} %img_ref.23, bf16[512,256]{1,0:T(8,128)(2,1)} %cap_ref.23, f32[1,8192]{1,0:T(1,128)} %bitcast.67, f32[512,1]{1,0:T(8,128)} %copy.39.b_ref, f32[512,1]{1,0:T(8,128)} %copy.40.w_ref), custom_call_target="tpu_custom_call" | custom-call | flops 2147483648 | bytes 4456448 | tf_op jit(solution)/shard_map/pallas_call | solution.py:131
  160.2 13.9 %shard_map.90 = f32[64,128]{1,0:T(8,128)} custom-call(f32[64,128]{1,0:T(8,128)} %bitcast.70), custom_call_target="tpu_custom_call" | custom-call | tf_op jit(solution)/shard_map/pallas_call | solution.py:60
  174.1 1.4 bitcast_add_fusion
  175.5 9.4 %shard_map.91 = f32[512,1]{1,0:T(8,128)} custom-call(bf16[8192,256]{1,0:T(8,128)(2,1)} %img_ref.23, bf16[512,256]{1,0:T(8,128)(2,1)} %cap_ref.23, f32[1,8192]{1,0:T(1,128)} %bitcast.77, f32[512,1]{1,0:T(8,128)} %copy.38.b_ref, f32[1,8192]{1,0:T(1,128)} %bitcast.58), custom_call_target="tpu_custom_call" | custom-call | flops 2147483648 | bytes 4456448 | tf_op jit(solution)/shard_map/pallas_call | solution.py:193
  184.8 1.7 reduce.3
  186.5 6.5 %shard_map.92 = f32[4,128]{1,0:T(4,128)} custom-call(f32[4,128]{1,0:T(4,128)} %bitcast.82), custom_call_target="tpu_custom_call" | custom-call | tf_op jit(solution)/shard_map/pallas_call | solution.py:60
  193.7 0.9 copy.43.w_ref
  194.6 9.0 %shard_map.93 = f32[1,8192]{1,0:T(1,128)} custom-call(bf16[8192,256]{1,0:T(8,128)(2,1)} %img_ref.23, bf16[512,256]{1,0:T(8,128)(2,1)} %cap_ref.23, f32[1,8192]{1,0:T(1,128)} %bitcast.64, f32[512,1]{1,0:T(8,128)} %copy.42.b_ref, f32[512,1]{1,0:T(8,128)} %copy.43.w_ref), custom_call_target="tpu_custom_call" | custom-call | flops 2147483648 | bytes 4456448 | tf_op jit(solution)/shard_map/pallas_call | solution.py:131
  203.6 13.9 %shard_map.94 = f32[64,128]{1,0:T(8,128)} custom-call(f32[64,128]{1,0:T(8,128)} %bitcast.71), custom_call_target="tpu_custom_call" | custom-call | tf_op jit(solution)/shard_map/pallas_call | solution.py:60
  217.5 1.4 neg.62
  219.0 9.5 %shard_map.95 = f32[512,1]{1,0:T(8,128)} custom-call(bf16[8192,256]{1,0:T(8,128)(2,1)} %img_ref.23, bf16[512,256]{1,0:T(8,128)(2,1)} %cap_ref.23, f32[1,8192]{1,0:T(1,128)} %bitcast.76, f32[512,1]{1,0:T(8,128)} %copy.37.b_ref, f32[1,8192]{1,0:T(1,128)} %bitcast.60), custom_call_target="tpu_custom_call" | custom-call | flops 2147483648 | bytes 4456448 | tf_op jit(solution)/shard_map/pallas_call | solution.py:193
  228.4 1.6 reduce.4
  230.1 6.5 %shard_map.96 = f32[4,128]{1,0:T(4,128)} custom-call(f32[4,128]{1,0:T(4,128)} %bitcast.78), custom_call_target="tpu_custom_call" | custom-call | tf_op jit(solution)/shard_map/pallas_call | solution.py:60
  237.3 0.9 copy.46.w_ref
  238.2 9.1 %shard_map.97 = f32[1,8192]{1,0:T(1,128)} custom-call(bf16[8192,256]{1,0:T(8,128)(2,1)} %img_ref.23, bf16[512,256]{1,0:T(8,128)(2,1)} %cap_ref.23, f32[1,8192]{1,0:T(1,128)} %bitcast.56, f32[512,1]{1,0:T(8,128)} %copy.45.b_ref, f32[512,1]{1,0:T(8,128)} %copy.46.w_ref), custom_call_target="tpu_custom_call" | custom-call | flops 2147483648 | bytes 4456448 | tf_op jit(solution)/shard_map/pallas_call | solution.py:131
  247.2 13.9 %shard_map.98 = f32[64,128]{1,0:T(8,128)} custom-call(f32[64,128]{1,0:T(8,128)} %bitcast.72), custom_call_target="tpu_custom_call" | custom-call | tf_op jit(solution)/shard_map/pallas_call | solution.py:60
  261.1 0.8 neg.66
  262.3 1.1 stack.36.rows_ref
  263.4 1.4 stack.39.cols_ref
  264.8 39.7 %shard_map.99 = (f32[8192,256]{1,0:T(8,128)}, f32[512,256]{1,0:T(8,128)}) custom-call(bf16[8192,256]{1,0:T(8,128)(2,1)} %img_ref.23, bf16[512,256]{1,0:T(8,128)(2,1)} %cap_ref.23, f32[8,8192]{1,0:T(8,128)} %stack.36.rows_ref, f32[512,8]{1,0:T(8,128)} %stack.39.cols_ref), custom_call_target="tpu_custom_call" | custom-call | flops 6442450944 | bytes 13369344 | tf_op jit(solution)/shard_map/pallas_call | solution.py:241
  304.6 0.7 reduce-scatter.3.cloned.1.call-update
  305.3 30.1 %reduce-scatter.5.cloned.1.call-done = f32[64,256]{1,0:T(8,128)} async-done(((f32[512,256]{1,0:T(8,128)}), f32[64,256]{1,0:T(8,128)}) %reduce-scatter.5.cloned.1.call-update) | async-done | bytes 65552 | tf_op jit(solution)/shard_map/reduce_scatter | solution.py:296
  335.4 88.2 %reduce-scatter.3.cloned.1.call-done = f32[512,256]{1,0:T(8,128)} async-done(((f32[8192,256]{1,0:T(8,128)}), f32[512,256]{1,0:T(8,128)}) %reduce-scatter.3.cloned.1.call-update) | async-done | bytes 524304 | tf_op jit(solution)/shard_map/reduce_scatter | solution.py:295
  (41 shorter events, 4.5 us)
Async XLA Ops:
  7.2 27.8 %copy-start.6 = (f32[8192]{0:T(1024)S(1)}, f32[8192]{0:T(1024)}, u32[]{:S(2)}) copy-start(f32[8192]{0:T(1024)} %param.8) | copy-start | bytes 98308
  7.2 328.2 %reduce-scatter.5.cloned.1.call-start = ((), (), s32[]{:S(2)}) async-start(), calls=%async_computation.3 | async-start | bytes 589824 | tf_op jit(solution)/shard_map/reduce_scatter | solution.py:296
  7.9 49.1 %copy-start.13 = (f32[512]{0:T(512)S(1)}, f32[512]{0:T(512)}, u32[]{:S(2)}) copy-start(f32[512]{0:T(512)} %param.9) | copy-start | bytes 6148
  130.1 44.0 %copy-start.14 = (f32[8192]{0:T(1024)S(1)}, f32[8192]{0:T(1024)}, u32[]{:S(2)}) copy-start(f32[8192]{0:T(1024)} %param.10) | copy-start | bytes 98308
  218.9 43.3 %copy-start.7 = (f32[8192]{0:T(1024)S(1)}, f32[8192]{0:T(1024)}, u32[]{:S(2)}) copy-start(f32[8192]{0:T(1024)} %bitcast_subtract_fusion.2) | copy-start | bytes 98308
  218.9 43.3 %copy-start.8 = (f32[8192]{0:T(1024)S(1)}, f32[8192]{0:T(1024)}, u32[]{:S(2)}) copy-start(f32[8192]{0:T(1024)} %bitcast_add_fusion) | copy-start | bytes 98308
  218.9 43.4 %copy-start.9 = (f32[1,8192]{1,0:T(1,128)S(1)}, f32[1,8192]{1,0:T(1,128)}, u32[]{:S(2)}) copy-start(f32[1,8192]{1,0:T(1,128)} %broadcast_6_a_ref_w_ref.2.a_ref.w_ref) | copy-start | bytes 98308
  218.9 43.4 %copy-start.10 = (f32[64,128]{1,0:T(8,128)S(1)}, f32[64,128]{1,0:T(8,128)}, u32[]{:S(2)}) copy-start(f32[64,128]{1,0:T(8,128)} %neg.62) | copy-start | bytes 98308
  218.9 43.4 %copy-start.11 = (f32[8192]{0:T(1024)S(1)}, f32[8192]{0:T(1024)}, u32[]{:S(2)}) copy-start(f32[8192]{0:T(1024)} %get-tuple-element.9) | copy-start | bytes 98308
  218.9 43.4 %copy-start.12 = (f32[8192]{0:T(1024)S(1)}, f32[8192]{0:T(1024)}, u32[]{:S(2)}) copy-start(f32[8192]{0:T(1024)} %get-tuple-element.7) | copy-start | bytes 98308
  218.9 44.5 %copy-start = (f32[512,1]{1,0:T(8,128)S(1)}, f32[512,1]{1,0:T(8,128)}, u32[]{:S(2)}) copy-start(f32[512,1]{1,0:T(8,128)} %broadcast_7_b_ref_w_ref.2.b_ref.w_ref) | copy-start | bytes 6148
  218.9 44.5 %copy-start.1 = (f32[512,1]{1,0:T(8,128)S(1)}, f32[512,1]{1,0:T(8,128)}, u32[]{:S(2)}) copy-start(f32[512,1]{1,0:T(8,128)} %copy.40.w_ref) | copy-start | bytes 6148
  218.9 44.4 %copy-start.2 = (f32[512,1]{1,0:T(8,128)S(1)}, f32[512,1]{1,0:T(8,128)}, u32[]{:S(2)}) copy-start(f32[512,1]{1,0:T(8,128)} %copy.37.b_ref) | copy-start | bytes 6148
  218.9 44.4 %copy-start.3 = (f32[512,1]{1,0:T(8,128)S(1)}, f32[512,1]{1,0:T(8,128)}, u32[]{:S(2)}) copy-start(f32[512,1]{1,0:T(8,128)} %copy.38.b_ref) | copy-start | bytes 6148
  219.0 44.4 %copy-start.4 = (f32[512,1]{1,0:T(8,128)S(1)}, f32[512,1]{1,0:T(8,128)}, u32[]{:S(2)}) copy-start(f32[512,1]{1,0:T(8,128)} %copy.43.w_ref) | copy-start | bytes 6148
  238.1 25.3 %copy-start.5 = (f32[512,1]{1,0:T(8,128)S(1)}, f32[512,1]{1,0:T(8,128)}, u32[]{:S(2)}) copy-start(f32[512,1]{1,0:T(8,128)} %copy.46.w_ref) | copy-start | bytes 6148
  304.6 119.0 %reduce-scatter.3.cloned.1.call-start = ((), (), s32[]{:S(2)}) async-start(), calls=%async_computation.2 | async-start | bytes 8912896 | tf_op jit(solution)/shard_map/reduce_scatter | solution.py:295
Sparse Core Ops, SparseCore 0:
  304.7 30.6 reduce-scatter.4
  339.4 84.1 reduce-scatter.2

commit v5 on v4

--- a/solution.py
+++ b/solution.py
@@ -8,20 +8,27 @@
 from jax.experimental.pallas import tpu as pltpu
 
 MESH = pl.DeviceIdType.MESH
-
-
-def _peer(axis, k, n):
-    me_img = lax.axis_index("img")
-    me_cap = lax.axis_index("cap")
-    if axis == "cap":
-        return (me_img, lax.rem(me_cap + k, n))
-    return (lax.rem(me_img + k, n), me_cap)
-
-
-def _combine_kernel(axis, n, mode, x_ref, o_ref, buf, send_sem, recv_sem):
+AXES = ("img", "cy", "cx")
+
+
+def _peer(group, k):
+    idx = {name: lax.axis_index(name) for name in AXES}
+    total = 1
+    lin = 0
+    for name, size in group:
+        lin = lin * size + idx[name]
+        total *= size
+    lin = lax.rem(lin + k, total)
+    for name, size in reversed(group):
+        idx[name] = lax.rem(lin, size)
+        lin = lin // size
+    return tuple(idx[name] for name in AXES)
+
+
+def _combine_kernel(group, n, mode, x_ref, o_ref, buf, send_sem, recv_sem):
     barrier = pltpu.get_barrier_semaphore()
     for k in range(1, n):
-        pl.semaphore_signal(barrier, inc=1, device_id=_peer(axis, k, n), device_id_type=MESH)
+        pl.semaphore_signal(barrier, inc=1, device_id=_peer(group, k), device_id_type=MESH)
     pl.semaphore_wait(barrier, n - 1)
     copies = []
     for k in range(1, n):
@@ -30,7 +37,7 @@
             dst_ref=buf.at[k],
             send_sem=send_sem.at[k],
             recv_sem=recv_sem.at[k],
-            device_id=_peer(axis, k, n),
+            device_id=_peer(group, k),
             device_id_type=MESH,
         )
         copy.start()
@@ -53,12 +60,15 @@
     o_ref[...] = acc
 
 
-def combine(x, axis, n, mode, cid):
+def combine(x, group, mode, cid):
+    n = 1
+    for _, size in group:
+        n *= size
     size = x.shape[0]
     rows = size // 128
     x2 = x.reshape(rows, 128)
     out = pl.pallas_call(
-        functools.partial(_combine_kernel, axis, n, mode),
+        functools.partial(_combine_kernel, group, n, mode),
         out_shape=jax.ShapeDtypeStruct((rows, 128), jnp.float32),
         in_specs=[pl.BlockSpec(memory_space=pltpu.VMEM)],
         out_specs=pl.BlockSpec(memory_space=pltpu.VMEM),
@@ -71,7 +81,7 @@
     )(x2)
     return out.reshape(size)
 
-from jax.sharding import PartitionSpec as P
+from jax.sharding import Mesh, PartitionSpec as P
 
 ITERS = 3
 
@@ -79,18 +89,15 @@
 SMOOTHING = 0.25
 
 
-_IDS = {("cap", "lse"): 0, ("img", "lse"): 1, ("cap", "sum"): 2, ("img", "sum"): 3}
-
-
-def gathered_lse(part, axis):
-    return combine(part, axis, lax.axis_size(axis), "lse", _IDS[(axis, "lse")])
-
-
-def gathered_sum(part, axis):
-    return combine(part, axis, lax.axis_size(axis), "sum", _IDS[(axis, "sum")])
-
-
-TM = 1024
+def gathered_lse(part, group, cid):
+    return combine(part, group, "lse", cid)
+
+
+def gathered_sum(part, group, cid):
+    return combine(part, group, "sum", cid)
+
+
+TM = 256
 INV_EPS = 1.0 / SMOOTHING
 
 
@@ -261,7 +268,18 @@
     )(images, captions, rows, cols)
 
 
-def body(images, captions, image_logw, caption_logw, image_cot, caption_cot):
+def body(images, captions, image_logw, caption_logw, image_cot, caption_cot, *, n_img, ny, nx):
+    rows_here = images.shape[0] // ny
+    start = lax.axis_index("cy") * rows_here
+    images = lax.dynamic_slice_in_dim(images, start, rows_here, 0)
+    image_logw = lax.dynamic_slice_in_dim(image_logw, start, rows_here, 0)
+    image_cot = lax.dynamic_slice_in_dim(image_cot, start, rows_here, 0)
+    captions = lax.all_gather(captions, "cy", tiled=True)
+    vecs = lax.all_gather(jnp.stack([caption_logw, caption_cot]), "cy", axis=1, tiled=True)
+    caption_logw = vecs[0]
+    caption_cot = vecs[1]
+    row_group = (("cx", nx),)
+    col_group = (("cy", ny), ("img", n_img))
     n = images.shape[0]
     c = captions.shape[0]
     zeros_r = jnp.zeros((n,), jnp.float32)
@@ -270,10 +288,10 @@
     row_hist = []
     for level in range(ITERS):
         part = row_pass("lse", images, captions, zeros_r, col_hist[-1], zeros_c)
-        row_pot = SMOOTHING * image_logw - SMOOTHING * gathered_lse(part, "cap")
+        row_pot = SMOOTHING * image_logw - SMOOTHING * gathered_lse(part, row_group, 0)
         row_hist.append(row_pot)
         part = col_pass("lse", images, captions, row_pot, zeros_r, zeros_c)
-        col_hist.append(SMOOTHING * caption_logw - SMOOTHING * gathered_lse(part, "img"))
+        col_hist.append(SMOOTHING * caption_logw - SMOOTHING * gathered_lse(part, col_group, 1))
     col_bar = caption_cot
     row_bars = [None] * ITERS
     col_bars = [None] * ITERS
@@ -281,23 +299,43 @@
         col_bars[level] = col_bar
         shift_col = caption_logw - col_hist[level + 1] / SMOOTHING
         part = row_pass("wsum", images, captions, row_hist[level], shift_col, col_bar)
-        row_bar = -gathered_sum(part, "cap")
+        row_bar = -gathered_sum(part, row_group, 2)
         if level == ITERS - 1:
             row_bar = image_cot + row_bar
         row_bars[level] = row_bar
         if level > 0:
             shift_row = image_logw - row_hist[level] / SMOOTHING
             part = col_pass("wsum", images, captions, shift_row, row_bar, col_hist[level])
-            col_bar = -gathered_sum(part, "img")
+            col_bar = -gathered_sum(part, col_group, 3)
     rows = jnp.stack(row_hist + row_bars + [image_logw, zeros_r], axis=0)
     cols = jnp.stack(col_hist + col_bars + [caption_logw], axis=1)
     ig_part, cg_part = final_pass(images, captions, rows, cols)
-    image_grad = lax.psum_scatter(ig_part, "cap", scatter_dimension=0, tiled=True)
-    caption_grad = lax.psum_scatter(cg_part, "img", scatter_dimension=0, tiled=True)
+    image_grad = lax.psum_scatter(ig_part, "cx", scatter_dimension=0, tiled=True)
+    caption_grad = lax.psum_scatter(cg_part, ("cy", "img"), scatter_dimension=0, tiled=True)
     return (image_grad, caption_grad)
 
 
 def solution(mesh):
-    in_specs = (P("img", None), P("cap", None), P("img"), P("cap"), P("img"), P("cap"))
-    out_specs = (P(("img", "cap"), None), P(("cap", "img"), None))
-    return jax.shard_map(body, mesh=mesh, in_specs=in_specs, out_specs=out_specs, check_vma=False)
+    n_img = mesh.shape["img"]
+    n_cap = mesh.shape["cap"]
+    nx = int(math.isqrt(n_cap))
+    while n_cap % nx:
+        nx -= 1
+    ny = n_cap // nx
+    grid = Mesh(mesh.devices.reshape(n_img, ny, nx), AXES)
+    in_specs = (
+        P("img", None),
+        P(("cy", "cx"), None),
+        P("img"),
+        P(("cy", "cx")),
+        P("img"),
+        P(("cy", "cx")),
+    )
+    out_specs = (P(("img", "cy", "cx"), None), P(("cy", "cx", "img"), None))
+    return jax.shard_map(
+        functools.partial(body, n_img=n_img, ny=ny, nx=nx),
+        mesh=grid,
+        in_specs=in_specs,
+        out_specs=out_specs,
+        check_vma=False,
+    )

time: 434 us -> 460 us (1.060)
  blocking collectives: 0 us -> 12.6 us
  other arithmetic: 19.5 us -> 26.7 us
  local copies, waits for them, and re-layouts: 11.8 us -> 16.6 us
    pallas_call x11, Pallas kernels: 119 us -> 98.7 us  [combine(): pl.pallas_call(functools.partial(_combine_kernel, group, n, mode), out_sh...]
    all_gather x0 -> x1, blocking collectives: none -> 12.6 us  [body(): lax.all_gather(jnp.stack([caption_logw, caption_cot]), 'cy', axis=1, tile...]
    all_gather x0 -> x1, waiting for transfers between devices: none -> 10.9 us  [body(): captions = lax.all_gather(captions, 'cy', tiled=True)]
    pallas_call x1, Pallas kernels: 39.7 us -> 48.9 us  [final_pass(): pl.pallas_call(functools.partial(_final_kernel, inv_root), out_shape=(jax...]
    reduce_scatter x2, waiting for transfers between devices: 118 us -> 110 us  [the longest x1 77.7 us: body(): lax.psum_scatter(cg_part, ('cy', 'img'), scatter_dimension=0, tiled=True)]
    pallas_call x5, Pallas kernels: 49.9 us -> 57 us  [col_pass(): pl.pallas_call(functools.partial(_col_kernel, mode, inv_root), out_shape=...]
    reshape x6 -> x0, local copies, waits for them, and re-layouts: 5.82 us -> none  [the longest x5 4.29 us: row_pass(): b.reshape(c, 1)]
    another operation x3 -> x1, local copies, waits for them, and re-layouts: 1.73 us -> 6.34 us  [body(): cols = jnp.stack(col_hist + col_bars + [caption_logw], axis=1)]
  transfers between devices with their start and end apart: 2 -> 3, of which waited for: 2 -> 3; matrix products, arithmetic and copies ran while one was open for 0% -> 1% of each run, Pallas kernels for 0% -> 0%
where the time goes in v5:
time: 460 us; the launch traced here: 457 us
  Pallas kernels  265 us (58%)
  waiting for transfers between devices  122 us (27%)
  other arithmetic  26.7 us (6%)
  local copies, waits for them, and re-layouts  16.6 us (4%)
  between operations  14 us (3%)
  blocking collectives  12.6 us (3%)
    pallas_call x11, Pallas kernels, combine(): pl.pallas_call(functools.partial(_combine_kernel, group, n, mode), out_sh...  98.7 us
    reduce_scatter x1, waiting for transfers between devices, body(): lax.psum_scatter(cg_part, ('cy', 'img'), scatter_dimension=0, tiled=True)  77.7 us
    pallas_call x6, Pallas kernels, row_pass(): pl.pallas_call(functools.partial(_row_kernel, mode, inv_root), out_shape=...  60.4 us
    pallas_call x5, Pallas kernels, col_pass(): pl.pallas_call(functools.partial(_col_kernel, mode, inv_root), out_shape=...  57 us
    pallas_call x1, Pallas kernels, final_pass(): pl.pallas_call(functools.partial(_final_kernel, inv_root), out_shape=(jax...  48.9 us
    reduce_scatter x1, waiting for transfers between devices, body(): lax.psum_scatter(ig_part, 'cx', scatter_dimension=0, tiled=True)  31.9 us
    all_gather x1, blocking collectives, body(): lax.all_gather(jnp.stack([caption_logw, caption_cot]), 'cy', axis=1, tile...  12.6 us
    all_gather x1, waiting for transfers between devices, body(): captions = lax.all_gather(captions, 'cy', tiled=True)  10.9 us
  transfers between devices with their start and end apart: 3, of which 3 were waited for; matrix products, arithmetic and copies ran while one was open for 1% of the time, Pallas kernels for 0%

profile of v5, /device:TPU:0, one launch (start us, length us, event | category | flops | bytes accessed | tf_op | source)
XLA Modules:
  0.0 457.1 jit_solution(6900381564820938374)
XLA Ops:
  8.0 0.7 pad_maximum_fusion
  8.7 12.6 %all_gather.7 = f32[2,2048]{1,0:T(2,128)S(1)} all-gather(f32[2,512]{1,0:T(2,128)S(1)} %pad_maximum_fusion), channel_id=1, replica_groups=mesh['img'=8,'cy'=4,'cx'=4] {'cy'}, dimensions={1}, use_global_device_ids=true | all-gather | bytes 20480 | tf_op jit(solution)/shard_map/all_gather | solution.py:278
  21.7 1.3 copy.59.w_ref
  23.0 2.3 constant_dynamic-slice_fusion.img_ref
  25.3 10.9 %all-gather.2.cloned.1.call-done.cap_ref = bf16[2048,256]{1,0:T(8,128)(2,1)} async-done(((bf16[512,256]{1,0:T(8,128)(2,1)}), bf16[2048,256]{1,0:T(8,128)(2,1)}) %all-gather.2.cloned.1.call-update) | async-done | bytes 1048592 | tf_op jit(solution)/shard_map/all_gather | solution.py:277
  36.9 1.1 broadcast_4_b_ref_w_ref.2.b_ref.w_ref
  38.0 10.5 %shard_map.77 = f32[1,2048]{1,0:T(1,128)} custom-call(bf16[2048,256]{1,0:T(8,128)(2,1)} %constant_dynamic-slice_fusion.img_ref, bf16[2048,256]{1,0:T(8,128)(2,1)} %all-gather.2.cloned.1.call-done.cap_ref, f32[1,2048]{1,0:T(1,128)} %broadcast_5_a_ref_w_ref.2.a_ref.w_ref, f32[2048,1]{1,0:T(8,128)} %broadcast_4_b_ref_w_ref.2.b_ref.w_ref, ...), custom_call_target="tpu_custom_call" | custom-call | flops 2147483648 | bytes 2097152 | tf_op jit(solution)/shard_map/pallas_call | solution.py:138
  48.5 7.3 %shard_map.78 = f32[16,128]{1,0:T(8,128)} custom-call(f32[16,128]{1,0:T(8,128)} %bitcast.71), custom_call_target="tpu_custom_call" | custom-call | tf_op jit(solution)/shard_map/pallas_call | solution.py:70
  55.8 1.3 bitcast_subtract_fusion.2
  57.1 12.3 %shard_map.79 = f32[2048,1]{1,0:T(8,128)} custom-call(bf16[2048,256]{1,0:T(8,128)(2,1)} %constant_dynamic-slice_fusion.img_ref, bf16[2048,256]{1,0:T(8,128)(2,1)} %all-gather.2.cloned.1.call-done.cap_ref, f32[1,2048]{1,0:T(1,128)} %bitcast.59, f32[2048,1]{1,0:T(8,128)} %broadcast_4_b_ref_w_ref.2.b_ref.w_ref, f32[1,2048]{1,0:T(1,128)} %broadcast_5_a_ref_w_ref.2.a_ref.w_ref), custom_call_target="tpu_custom_call" | custom-call | flops 2147483648 | bytes 2097152 | tf_op jit(solution)/shard_map/pallas_call | solution.py:200
  69.4 2.1 reduce
  71.5 12.0 %shard_map.80 = f32[16,128]{1,0:T(8,128)} custom-call(f32[16,128]{1,0:T(8,128)} %bitcast.45), custom_call_target="tpu_custom_call" | custom-call | tf_op jit(solution)/shard_map/pallas_call | solution.py:70
  84.6 1.5 multiply_subtract_fusion.2
  86.0 10.5 %shard_map.81 = f32[1,2048]{1,0:T(1,128)} custom-call(bf16[2048,256]{1,0:T(8,128)(2,1)} %constant_dynamic-slice_fusion.img_ref, bf16[2048,256]{1,0:T(8,128)(2,1)} %all-gather.2.cloned.1.call-done.cap_ref, f32[1,2048]{1,0:T(1,128)} %broadcast_5_a_ref_w_ref.2.a_ref.w_ref, f32[2048,1]{1,0:T(8,128)} %get-tuple-element.13.b_ref, ...), custom_call_target="tpu_custom_call" | custom-call | flops 2147483648 | bytes 2097152 | tf_op jit(solution)/shard_map/pallas_call | solution.py:138
  96.6 6.6 %shard_map.82 = f32[16,128]{1,0:T(8,128)} custom-call(f32[16,128]{1,0:T(8,128)} %bitcast.72), custom_call_target="tpu_custom_call" | custom-call | tf_op jit(solution)/shard_map/pallas_call | solution.py:70
  103.2 1.3 multiply_subtract_fusion.7
  104.5 12.3 %shard_map.83 = f32[2048,1]{1,0:T(8,128)} custom-call(bf16[2048,256]{1,0:T(8,128)(2,1)} %constant_dynamic-slice_fusion.img_ref, bf16[2048,256]{1,0:T(8,128)(2,1)} %all-gather.2.cloned.1.call-done.cap_ref, f32[1,2048]{1,0:T(1,128)} %bitcast.62, f32[2048,1]{1,0:T(8,128)} %broadcast_4_b_ref_w_ref.2.b_ref.w_ref, f32[1,2048]{1,0:T(1,128)} %broadcast_5_a_ref_w_ref.2.a_ref.w_ref), custom_call_target="tpu_custom_call" | custom-call | flops 2147483648 | bytes 2097152 | tf_op jit(solution)/shard_map/pallas_call | solution.py:200
  116.8 2.2 reduce.1
  118.9 11.7 %shard_map.84 = f32[16,128]{1,0:T(8,128)} custom-call(f32[16,128]{1,0:T(8,128)} %bitcast.47), custom_call_target="tpu_custom_call" | custom-call | tf_op jit(solution)/shard_map/pallas_call | solution.py:70
  131.7 1.5 multiply_subtract_fusion.1
  133.2 10.5 %shard_map.85 = f32[1,2048]{1,0:T(1,128)} custom-call(bf16[2048,256]{1,0:T(8,128)(2,1)} %constant_dynamic-slice_fusion.img_ref, bf16[2048,256]{1,0:T(8,128)(2,1)} %all-gather.2.cloned.1.call-done.cap_ref, f32[1,2048]{1,0:T(1,128)} %broadcast_5_a_ref_w_ref.2.a_ref.w_ref, f32[2048,1]{1,0:T(8,128)} %get-tuple-element.11.b_ref, ...), custom_call_target="tpu_custom_call" | custom-call | flops 2147483648 | bytes 2097152 | tf_op jit(solution)/shard_map/pallas_call | solution.py:138
  143.7 6.6 %shard_map.86 = f32[16,128]{1,0:T(8,128)} custom-call(f32[16,128]{1,0:T(8,128)} %bitcast.73), custom_call_target="tpu_custom_call" | custom-call | tf_op jit(solution)/shard_map/pallas_call | solution.py:70
  150.4 1.3 multiply_subtract_fusion.6
  151.7 12.3 %shard_map.87 = f32[2048,1]{1,0:T(8,128)} custom-call(bf16[2048,256]{1,0:T(8,128)(2,1)} %constant_dynamic-slice_fusion.img_ref, bf16[2048,256]{1,0:T(8,128)(2,1)} %all-gather.2.cloned.1.call-done.cap_ref, f32[1,2048]{1,0:T(1,128)} %bitcast.65, f32[2048,1]{1,0:T(8,128)} %broadcast_4_b_ref_w_ref.2.b_ref.w_ref, f32[1,2048]{1,0:T(1,128)} %broadcast_5_a_ref_w_ref.2.a_ref.w_ref), custom_call_target="tpu_custom_call" | custom-call | flops 2147483648 | bytes 2097152 | tf_op jit(solution)/shard_map/pallas_call | solution.py:200
  163.9 2.2 reduce.2
  166.1 11.6 %shard_map.88 = f32[16,128]{1,0:T(8,128)} custom-call(f32[16,128]{1,0:T(8,128)} %bitcast.49), custom_call_target="tpu_custom_call" | custom-call | tf_op jit(solution)/shard_map/pallas_call | solution.py:70
  178.8 1.5 multiply_subtract_fusion.3
  180.2 9.6 %shard_map.89 = f32[1,2048]{1,0:T(1,128)} custom-call(bf16[2048,256]{1,0:T(8,128)(2,1)} %constant_dynamic-slice_fusion.img_ref, bf16[2048,256]{1,0:T(8,128)(2,1)} %all-gather.2.cloned.1.call-done.cap_ref, f32[1,2048]{1,0:T(1,128)} %bitcast.66, f32[2048,1]{1,0:T(8,128)} %get-tuple-element.9.b_ref, f32[2048,1]{1,0:T(8,128)} %copy.59.w_ref), custom_call_target="tpu_custom_call" | custom-call | flops 2147483648 | bytes 2097152 | tf_op jit(solution)/shard_map/pallas_call | solution.py:138
  189.8 6.6 %shard_map.90 = f32[16,128]{1,0:T(8,128)} custom-call(f32[16,128]{1,0:T(8,128)} %bitcast.68), custom_call_target="tpu_custom_call" | custom-call | tf_op jit(solution)/shard_map/pallas_call | solution.py:70
  196.5 1.3 bitcast_add_fusion
  197.8 10.0 %shard_map.91 = f32[2048,1]{1,0:T(8,128)} custom-call(bf16[2048,256]{1,0:T(8,128)(2,1)} %constant_dynamic-slice_fusion.img_ref, bf16[2048,256]{1,0:T(8,128)(2,1)} %all-gather.2.cloned.1.call-done.cap_ref, f32[1,2048]{1,0:T(1,128)} %bitcast.75, f32[2048,1]{1,0:T(8,128)} %get-tuple-element.11.b_ref, f32[1,2048]{1,0:T(1,128)} %bitcast.54), custom_call_target="tpu_custom_call" | custom-call | flops 2147483648 | bytes 2097152 | tf_op jit(solution)/shard_map/pallas_call | solution.py:200
  207.8 2.2 reduce.3
  210.0 11.6 %shard_map.92 = f32[16,128]{1,0:T(8,128)} custom-call(f32[16,128]{1,0:T(8,128)} %bitcast.51), custom_call_target="tpu_custom_call" | custom-call | tf_op jit(solution)/shard_map/pallas_call | solution.py:70
  222.3 1.3 copy.60.w_ref
  223.6 9.6 %shard_map.93 = f32[1,2048]{1,0:T(1,128)} custom-call(bf16[2048,256]{1,0:T(8,128)(2,1)} %constant_dynamic-slice_fusion.img_ref, bf16[2048,256]{1,0:T(8,128)(2,1)} %all-gather.2.cloned.1.call-done.cap_ref, f32[1,2048]{1,0:T(1,128)} %bitcast.63, f32[2048,1]{1,0:T(8,128)} %get-tuple-element.10.b_ref, f32[2048,1]{1,0:T(8,128)} %copy.60.w_ref), custom_call_target="tpu_custom_call" | custom-call | flops 2147483648 | bytes 2097152 | tf_op jit(solution)/shard_map/pallas_call | solution.py:138
  233.2 6.6 %shard_map.94 = f32[16,128]{1,0:T(8,128)} custom-call(f32[16,128]{1,0:T(8,128)} %bitcast.69), custom_call_target="tpu_custom_call" | custom-call | tf_op jit(solution)/shard_map/pallas_call | solution.py:70
  239.8 1.3 neg.62
  241.1 10.1 %shard_map.95 = f32[2048,1]{1,0:T(8,128)} custom-call(bf16[2048,256]{1,0:T(8,128)(2,1)} %constant_dynamic-slice_fusion.img_ref, bf16[2048,256]{1,0:T(8,128)(2,1)} %all-gather.2.cloned.1.call-done.cap_ref, f32[1,2048]{1,0:T(1,128)} %bitcast.74, f32[2048,1]{1,0:T(8,128)} %get-tuple-element.13.b_ref, f32[1,2048]{1,0:T(1,128)} %bitcast.56), custom_call_target="tpu_custom_call" | custom-call | flops 2147483648 | bytes 2097152 | tf_op jit(solution)/shard_map/pallas_call | solution.py:200
  251.2 2.2 reduce.4
  253.4 11.5 %shard_map.96 = f32[16,128]{1,0:T(8,128)} custom-call(f32[16,128]{1,0:T(8,128)} %bitcast.44), custom_call_target="tpu_custom_call" | custom-call | tf_op jit(solution)/shard_map/pallas_call | solution.py:70
  265.6 1.4 copy.61.w_ref
  267.0 9.7 %shard_map.97 = f32[1,2048]{1,0:T(1,128)} custom-call(bf16[2048,256]{1,0:T(8,128)(2,1)} %constant_dynamic-slice_fusion.img_ref, bf16[2048,256]{1,0:T(8,128)(2,1)} %all-gather.2.cloned.1.call-done.cap_ref, f32[1,2048]{1,0:T(1,128)} %bitcast.60, f32[2048,1]{1,0:T(8,128)} %get-tuple-element.12.b_ref, f32[2048,1]{1,0:T(8,128)} %copy.61.w_ref), custom_call_target="tpu_custom_call" | custom-call | flops 2147483648 | bytes 2097152 | tf_op jit(solution)/shard_map/pallas_call | solution.py:138
  276.7 6.6 %shard_map.98 = f32[16,128]{1,0:T(8,128)} custom-call(f32[16,128]{1,0:T(8,128)} %bitcast.70), custom_call_target="tpu_custom_call" | custom-call | tf_op jit(solution)/shard_map/pallas_call | solution.py:70
  284.1 6.3 %stack.43.cols_ref = f32[2048,8]{1,0:T(8,128)} concatenate(f32[2048,1]{1,0:T(8,128)S(1)} %copy-done.1, f32[2048,1]{1,0:T(8,128)} %get-tuple-element.13.b_ref, f32[2048,1]{1,0:T(8,128)} %get-tuple-element.11.b_ref, f32[2048,1]{1,0:T(8,128)} %get-tuple-element.8, f32[2048,1]{1,0:T(8,128)} %copy.61.w_ref, f32[2048,1]{1,0:T(8,128)} %copy.60.w_ref, f32[2048,1]{1,0:T(8,128)S(1)} %copy-done, ...), dimensions={1} | concatenate | bytes 131072 | tf_op jit(solution)/shard_map/stack | solution.py:311
  290.5 0.7 stack.42.rows_ref
  291.2 48.9 %shard_map.99 = (f32[2048,256]{1,0:T(8,128)}, f32[2048,256]{1,0:T(8,128)}) custom-call(bf16[2048,256]{1,0:T(8,128)(2,1)} %constant_dynamic-slice_fusion.img_ref, bf16[2048,256]{1,0:T(8,128)(2,1)} %all-gather.2.cloned.1.call-done.cap_ref, f32[8,2048]{1,0:T(8,128)} %stack.42.rows_ref, f32[2048,8]{1,0:T(8,128)} %stack.43.cols_ref), custom_call_target="tpu_custom_call" | custom-call | flops 6442450944 | bytes 6291456 | tf_op jit(solution)/shard_map/pallas_call | solution.py:248
  340.9 77.7 %reduce-scatter.5.cloned.1.call-done = f32[64,256]{1,0:T(8,128)} async-done(((f32[2048,256]{1,0:T(8,128)}), f32[64,256]{1,0:T(8,128)}) %reduce-scatter.5.cloned.1.call-update) | async-done | bytes 65552 | tf_op jit(solution)/shard_map/reduce_scatter | solution.py:314
  418.6 31.9 %reduce-scatter.3.cloned.1.call-done = f32[512,256]{1,0:T(8,128)} async-done(((f32[2048,256]{1,0:T(8,128)}), f32[512,256]{1,0:T(8,128)}) %reduce-scatter.3.cloned.1.call-update) | async-done | bytes 524304 | tf_op jit(solution)/shard_map/reduce_scatter | solution.py:313
  (34 shorter events, 7.8 us)
Async XLA Ops:
  7.2 29.1 %all-gather.2.cloned.1.call-start = ((), (), s32[]{:S(2)}) async-start(), calls=%async_computation.2 | async-start | bytes 1310720 | tf_op jit(solution)/shard_map/all_gather | solution.py:277
  7.9 410.7 %reduce-scatter.5.cloned.1.call-start = ((), (), s32[]{:S(2)}) async-start(), calls=%async_computation.4 | async-start | bytes 2162688 | tf_op jit(solution)/shard_map/reduce_scatter | solution.py:314
  267.0 17.0 %copy-start = (f32[2048,1]{1,0:T(8,128)S(1)}, f32[2048,1]{1,0:T(8,128)}, u32[]{:S(2)}) copy-start(f32[2048,1]{1,0:T(8,128)} %copy.59.w_ref) | copy-start | bytes 24580
  267.0 17.0 %copy-start.1 = (f32[2048,1]{1,0:T(8,128)S(1)}, f32[2048,1]{1,0:T(8,128)}, u32[]{:S(2)}) copy-start(f32[2048,1]{1,0:T(8,128)} %broadcast_4_b_ref_w_ref.2.b_ref.w_ref) | copy-start | bytes 24580
  284.0 6.4 %copy-start.2 = (f32[2048]{0:T(1024)S(1)}, f32[2048]{0:T(1024)}, u32[]{:S(2)}) copy-start(f32[2048]{0:T(1024)} %bitcast_add_fusion) | copy-start | bytes 24580
  284.0 6.4 %copy-start.3 = (f32[1,2048]{1,0:T(1,128)S(1)}, f32[1,2048]{1,0:T(1,128)}, u32[]{:S(2)}) copy-start(f32[1,2048]{1,0:T(1,128)} %broadcast_5_a_ref_w_ref.2.a_ref.w_ref) | copy-start | bytes 24580
  284.0 6.4 %copy-start.4 = (f32[16,128]{1,0:T(8,128)S(1)}, f32[16,128]{1,0:T(8,128)}, u32[]{:S(2)}) copy-start(f32[16,128]{1,0:T(8,128)} %neg.62) | copy-start | bytes 24580
  284.0 6.4 %copy-start.5 = (f32[2048]{0:T(1024)S(1)}, f32[2048]{0:T(1024)}, u32[]{:S(2)}) copy-start(f32[2048]{0:T(1024)} %get-tuple-element.6) | copy-start | bytes 24580
  284.1 6.4 %copy-start.6 = (f32[2048]{0:T(1024)S(1)}, f32[2048]{0:T(1024)}, u32[]{:S(2)}) copy-start(f32[2048]{0:T(1024)} %get-tuple-element.19) | copy-start | bytes 24580
  284.1 6.4 %copy-start.7 = (f32[2048]{0:T(1024)S(1)}, f32[2048]{0:T(1024)}, u32[]{:S(2)}) copy-start(f32[2048]{0:T(1024)} %get-tuple-element.17) | copy-start | bytes 24580
  340.2 110.4 %reduce-scatter.3.cloned.1.call-start = ((), (), s32[]{:S(2)}) async-start(), calls=%async_computation.3 | async-start | bytes 2621440 | tf_op jit(solution)/shard_map/reduce_scatter | solution.py:313
Sparse Core Ops, SparseCore 0:
  9.6 26.5 all-gather.1
  340.3 78.2 reduce-scatter.4
  421.6 28.8 reduce-scatter.2

commit v6 on v5

--- a/solution.py
+++ b/solution.py
@@ -274,10 +274,14 @@
     images = lax.dynamic_slice_in_dim(images, start, rows_here, 0)
     image_logw = lax.dynamic_slice_in_dim(image_logw, start, rows_here, 0)
     image_cot = lax.dynamic_slice_in_dim(image_cot, start, rows_here, 0)
-    captions = lax.all_gather(captions, "cy", tiled=True)
-    vecs = lax.all_gather(jnp.stack([caption_logw, caption_cot]), "cy", axis=1, tiled=True)
-    caption_logw = vecs[0]
-    caption_cot = vecs[1]
+    e = captions.shape[1]
+    joined = jnp.concatenate(
+        [captions.astype(jnp.float32), jnp.stack([caption_logw, caption_cot], axis=1)], axis=1
+    )
+    joined = lax.all_gather(joined, "cy", tiled=True)
+    captions = joined[:, :e].astype(jnp.bfloat16)
+    caption_logw = joined[:, e]
+    caption_cot = joined[:, e + 1]
     row_group = (("cx", nx),)
     col_group = (("cy", ny), ("img", n_img))
     n = images.shape[0]
@@ -311,7 +315,10 @@
     cols = jnp.stack(col_hist + col_bars + [caption_logw], axis=1)
     ig_part, cg_part = final_pass(images, captions, rows, cols)
     image_grad = lax.psum_scatter(ig_part, "cx", scatter_dimension=0, tiled=True)
-    caption_grad = lax.psum_scatter(cg_part, ("cy", "img"), scatter_dimension=0, tiled=True)
+    piece = c // (ny * n_img)
+    staged = cg_part.reshape(ny, n_img, piece, e).transpose(1, 0, 2, 3).reshape(c, e)
+    staged = lax.psum_scatter(staged, "img", scatter_dimension=0, tiled=True)
+    caption_grad = lax.psum_scatter(staged, "cy", scatter_dimension=0, tiled=True)
     return (image_grad, caption_grad)
 
 

time: 460 us -> 468 us (1.017)
  blocking collectives: 12.6 us -> 0 us
  local copies, waits for them, and re-layouts: 16.6 us -> 25.7 us
  other arithmetic: 26.7 us -> 32.7 us
  waiting for transfers between devices: 122 us -> 128 us
    all_gather x1, waiting for transfers between devices: 10.9 us -> 39.8 us  [body(): joined = lax.all_gather(joined, 'cy', tiled=True)]
    reduce_scatter x1 -> x2, waiting for transfers between devices: 77.7 us -> 55.9 us  [the longest x1 32.4 us: body(): staged = lax.psum_scatter(staged, 'img', scatter_dimension=0, tiled=True)]
    all_gather x1 -> x0, blocking collectives: 12.6 us -> none  [body(): lax.all_gather(jnp.stack([caption_logw, caption_cot]), 'cy', axis=1, tile...]
  transfers between devices with their start and end apart: 3 -> 4, of which waited for: 3 -> 4; matrix products, arithmetic and copies ran while one was open for 1% -> 0% of each run, Pallas kernels for 0% -> 0%
where the time goes in v6:
time: 468 us; the launch traced here: 466 us
  Pallas kernels  265 us (57%)
  waiting for transfers between devices  128 us (27%)
  other arithmetic  32.7 us (7%)
  local copies, waits for them, and re-layouts  25.7 us (5%)
  between operations  14 us (3%)
    pallas_call x11, Pallas kernels, combine(): pl.pallas_call(functools.partial(_combine_kernel, group, n, mode), out_sh...  98.7 us
    pallas_call x6, Pallas kernels, row_pass(): pl.pallas_call(functools.partial(_row_kernel, mode, inv_root), out_shape=...  60.5 us
    pallas_call x5, Pallas kernels, col_pass(): pl.pallas_call(functools.partial(_col_kernel, mode, inv_root), out_shape=...  57.1 us
    pallas_call x1, Pallas kernels, final_pass(): pl.pallas_call(functools.partial(_final_kernel, inv_root), out_shape=(jax...  48.9 us
    all_gather x1, waiting for transfers between devices, body(): joined = lax.all_gather(joined, 'cy', tiled=True)  39.8 us
    reduce_scatter x1, waiting for transfers between devices, body(): staged = lax.psum_scatter(staged, 'img', scatter_dimension=0, tiled=True)  32.4 us
    reduce_scatter x1, waiting for transfers between devices, body(): lax.psum_scatter(ig_part, 'cx', scatter_dimension=0, tiled=True)  31.3 us
    reduce_scatter x1, waiting for transfers between devices, body(): lax.psum_scatter(staged, 'cy', scatter_dimension=0, tiled=True)  23.4 us
  transfers between devices with their start and end apart: 4, of which 4 were waited for; matrix products, arithmetic and copies ran while one was open for 0% of the time, Pallas kernels for 0%

profile of v6, /device:TPU:0, one launch (start us, length us, event | category | flops | bytes accessed | tf_op | source)
XLA Modules:
  0.0 465.5 jit_solution(15673558112049845456)
XLA Ops:
  11.0 2.3 constant_dynamic-slice_fusion.img_ref
  13.2 39.8 %all-gather.2.cloned.1.call-done = f32[2048,258]{1,0:T(8,128)} async-done(((f32[512,258]{1,0:T(8,128)}), f32[2048,258]{1,0:T(8,128)}) %all-gather.2.cloned.1.call-update) | async-done | bytes 2113552 | tf_op jit(solution)/shard_map/all_gather | solution.py:281
  53.0 2.7 slice.23.cap_ref
  57.4 10.5 %shard_map.77 = f32[1,2048]{1,0:T(1,128)} custom-call(bf16[2048,256]{1,0:T(8,128)(2,1)} %constant_dynamic-slice_fusion.img_ref, bf16[2048,256]{1,0:T(8,128)(2,1)} %slice.23.cap_ref, f32[1,2048]{1,0:T(1,128)} %broadcast_5_a_ref_w_ref.2.a_ref.w_ref, f32[2048,1]{1,0:T(8,128)} %broadcast_4_b_ref_w_ref.2.b_ref.w_ref, f32[2048,1]{1,0:T(8,128)} %broadcast_4_b_ref_w_ref.2.b_ref.w_ref), custom_call_target="tpu_custom_call" | custom-call | flops 2147483648 | bytes 2097152 | tf_op jit(solution)/shard_map/pallas_call | solution.py:138
  67.9 7.3 %shard_map.78 = f32[16,128]{1,0:T(8,128)} custom-call(f32[16,128]{1,0:T(8,128)} %bitcast.73), custom_call_target="tpu_custom_call" | custom-call | tf_op jit(solution)/shard_map/pallas_call | solution.py:70
  75.2 1.3 bitcast_subtract_fusion.2
  76.5 12.4 %shard_map.79 = f32[2048,1]{1,0:T(8,128)} custom-call(bf16[2048,256]{1,0:T(8,128)(2,1)} %constant_dynamic-slice_fusion.img_ref, bf16[2048,256]{1,0:T(8,128)(2,1)} %slice.23.cap_ref, f32[1,2048]{1,0:T(1,128)} %bitcast.61, f32[2048,1]{1,0:T(8,128)} %broadcast_4_b_ref_w_ref.2.b_ref.w_ref, f32[1,2048]{1,0:T(1,128)} %broadcast_5_a_ref_w_ref.2.a_ref.w_ref), custom_call_target="tpu_custom_call" | custom-call | flops 2147483648 | bytes 2097152 | tf_op jit(solution)/shard_map/pallas_call | solution.py:200
  88.9 2.2 reduce
  91.1 11.9 %shard_map.80 = f32[16,128]{1,0:T(8,128)} custom-call(f32[16,128]{1,0:T(8,128)} %bitcast.47), custom_call_target="tpu_custom_call" | custom-call | tf_op jit(solution)/shard_map/pallas_call | solution.py:70
  103.7 1.4 copy.47
  105.1 3.1 multiply_subtract_fusion.2
  108.2 10.5 %shard_map.81 = f32[1,2048]{1,0:T(1,128)} custom-call(bf16[2048,256]{1,0:T(8,128)(2,1)} %constant_dynamic-slice_fusion.img_ref, bf16[2048,256]{1,0:T(8,128)(2,1)} %slice.23.cap_ref, f32[1,2048]{1,0:T(1,128)} %broadcast_5_a_ref_w_ref.2.a_ref.w_ref, f32[2048,1]{1,0:T(8,128)} %get-tuple-element.13.b_ref, f32[2048,1]{1,0:T(8,128)} %broadcast_4_b_ref_w_ref.2.b_ref.w_ref), custom_call_target="tpu_custom_call" | custom-call | flops 2147483648 | bytes 2097152 | tf_op jit(solution)/shard_map/pallas_call | solution.py:138
  118.7 6.7 %shard_map.82 = f32[16,128]{1,0:T(8,128)} custom-call(f32[16,128]{1,0:T(8,128)} %bitcast.74), custom_call_target="tpu_custom_call" | custom-call | tf_op jit(solution)/shard_map/pallas_call | solution.py:70
  125.4 1.3 multiply_subtract_fusion.7
  126.7 12.3 %shard_map.83 = f32[2048,1]{1,0:T(8,128)} custom-call(bf16[2048,256]{1,0:T(8,128)(2,1)} %constant_dynamic-slice_fusion.img_ref, bf16[2048,256]{1,0:T(8,128)(2,1)} %slice.23.cap_ref, f32[1,2048]{1,0:T(1,128)} %bitcast.64, f32[2048,1]{1,0:T(8,128)} %broadcast_4_b_ref_w_ref.2.b_ref.w_ref, f32[1,2048]{1,0:T(1,128)} %broadcast_5_a_ref_w_ref.2.a_ref.w_ref), custom_call_target="tpu_custom_call" | custom-call | flops 2147483648 | bytes 2097152 | tf_op jit(solution)/shard_map/pallas_call | solution.py:200
  139.0 2.2 reduce.1
  141.1 11.7 %shard_map.84 = f32[16,128]{1,0:T(8,128)} custom-call(f32[16,128]{1,0:T(8,128)} %bitcast.49), custom_call_target="tpu_custom_call" | custom-call | tf_op jit(solution)/shard_map/pallas_call | solution.py:70
  153.5 1.3 copy.48
  154.8 2.7 multiply_subtract_fusion.1
  157.6 10.5 %shard_map.85 = f32[1,2048]{1,0:T(1,128)} custom-call(bf16[2048,256]{1,0:T(8,128)(2,1)} %constant_dynamic-slice_fusion.img_ref, bf16[2048,256]{1,0:T(8,128)(2,1)} %slice.23.cap_ref, f32[1,2048]{1,0:T(1,128)} %broadcast_5_a_ref_w_ref.2.a_ref.w_ref, f32[2048,1]{1,0:T(8,128)} %get-tuple-element.11.b_ref, f32[2048,1]{1,0:T(8,128)} %broadcast_4_b_ref_w_ref.2.b_ref.w_ref), custom_call_target="tpu_custom_call" | custom-call | flops 2147483648 | bytes 2097152 | tf_op jit(solution)/shard_map/pallas_call | solution.py:138
  168.1 6.6 %shard_map.86 = f32[16,128]{1,0:T(8,128)} custom-call(f32[16,128]{1,0:T(8,128)} %bitcast.75), custom_call_target="tpu_custom_call" | custom-call | tf_op jit(solution)/shard_map/pallas_call | solution.py:70
  174.7 1.3 multiply_subtract_fusion.6
  176.0 12.3 %shard_map.87 = f32[2048,1]{1,0:T(8,128)} custom-call(bf16[2048,256]{1,0:T(8,128)(2,1)} %constant_dynamic-slice_fusion.img_ref, bf16[2048,256]{1,0:T(8,128)(2,1)} %slice.23.cap_ref, f32[1,2048]{1,0:T(1,128)} %bitcast.67, f32[2048,1]{1,0:T(8,128)} %broadcast_4_b_ref_w_ref.2.b_ref.w_ref, f32[1,2048]{1,0:T(1,128)} %broadcast_5_a_ref_w_ref.2.a_ref.w_ref), custom_call_target="tpu_custom_call" | custom-call | flops 2147483648 | bytes 2097152 | tf_op jit(solution)/shard_map/pallas_call | solution.py:200
  188.3 2.2 reduce.2
  190.4 11.6 %shard_map.88 = f32[16,128]{1,0:T(8,128)} custom-call(f32[16,128]{1,0:T(8,128)} %bitcast.51), custom_call_target="tpu_custom_call" | custom-call | tf_op jit(solution)/shard_map/pallas_call | solution.py:70
  202.8 1.4 copy.49
  204.2 3.3 multiply_subtract_fusion.3
  207.5 9.5 %shard_map.89 = f32[1,2048]{1,0:T(1,128)} custom-call(bf16[2048,256]{1,0:T(8,128)(2,1)} %constant_dynamic-slice_fusion.img_ref, bf16[2048,256]{1,0:T(8,128)(2,1)} %slice.23.cap_ref, f32[1,2048]{1,0:T(1,128)} %bitcast.68, f32[2048,1]{1,0:T(8,128)} %get-tuple-element.9.b_ref, f32[2048,1]{1,0:T(8,128)} %get-tuple-element.15.w_ref), custom_call_target="tpu_custom_call" | custom-call | flops 2147483648 | bytes 2097152 | tf_op jit(solution)/shard_map/pallas_call | solution.py:138
  217.0 6.6 %shard_map.90 = f32[16,128]{1,0:T(8,128)} custom-call(f32[16,128]{1,0:T(8,128)} %bitcast.70), custom_call_target="tpu_custom_call" | custom-call | tf_op jit(solution)/shard_map/pallas_call | solution.py:70
  223.6 1.3 bitcast_add_fusion
  225.0 10.1 %shard_map.91 = f32[2048,1]{1,0:T(8,128)} custom-call(bf16[2048,256]{1,0:T(8,128)(2,1)} %constant_dynamic-slice_fusion.img_ref, bf16[2048,256]{1,0:T(8,128)(2,1)} %slice.23.cap_ref, f32[1,2048]{1,0:T(1,128)} %bitcast.77, f32[2048,1]{1,0:T(8,128)} %get-tuple-element.11.b_ref, f32[1,2048]{1,0:T(1,128)} %bitcast.56), custom_call_target="tpu_custom_call" | custom-call | flops 2147483648 | bytes 2097152 | tf_op jit(solution)/shard_map/pallas_call | solution.py:200
  235.1 2.2 reduce.3
  237.2 11.6 %shard_map.92 = f32[16,128]{1,0:T(8,128)} custom-call(f32[16,128]{1,0:T(8,128)} %bitcast.53), custom_call_target="tpu_custom_call" | custom-call | tf_op jit(solution)/shard_map/pallas_call | solution.py:70
  249.5 1.4 copy.50.w_ref
  250.9 9.5 %shard_map.93 = f32[1,2048]{1,0:T(1,128)} custom-call(bf16[2048,256]{1,0:T(8,128)(2,1)} %constant_dynamic-slice_fusion.img_ref, bf16[2048,256]{1,0:T(8,128)(2,1)} %slice.23.cap_ref, f32[1,2048]{1,0:T(1,128)} %bitcast.65, f32[2048,1]{1,0:T(8,128)} %get-tuple-element.10.b_ref, f32[2048,1]{1,0:T(8,128)} %copy.50.w_ref), custom_call_target="tpu_custom_call" | custom-call | flops 2147483648 | bytes 2097152 | tf_op jit(solution)/shard_map/pallas_call | solution.py:138
  260.5 6.6 %shard_map.94 = f32[16,128]{1,0:T(8,128)} custom-call(f32[16,128]{1,0:T(8,128)} %bitcast.71), custom_call_target="tpu_custom_call" | custom-call | tf_op jit(solution)/shard_map/pallas_call | solution.py:70
  268.4 10.1 %shard_map.95 = f32[2048,1]{1,0:T(8,128)} custom-call(bf16[2048,256]{1,0:T(8,128)(2,1)} %constant_dynamic-slice_fusion.img_ref, bf16[2048,256]{1,0:T(8,128)(2,1)} %slice.23.cap_ref, f32[1,2048]{1,0:T(1,128)} %bitcast.76, f32[2048,1]{1,0:T(8,128)} %get-tuple-element.13.b_ref, f32[1,2048]{1,0:T(1,128)} %bitcast.58), custom_call_target="tpu_custom_call" | custom-call | flops 2147483648 | bytes 2097152 | tf_op jit(solution)/shard_map/pallas_call | solution.py:200
  278.4 2.2 reduce.4
  280.6 11.5 %shard_map.96 = f32[16,128]{1,0:T(8,128)} custom-call(f32[16,128]{1,0:T(8,128)} %bitcast.46), custom_call_target="tpu_custom_call" | custom-call | tf_op jit(solution)/shard_map/pallas_call | solution.py:70
  292.9 1.3 copy.51.w_ref
  294.2 9.9 %shard_map.97 = f32[1,2048]{1,0:T(1,128)} custom-call(bf16[2048,256]{1,0:T(8,128)(2,1)} %constant_dynamic-slice_fusion.img_ref, bf16[2048,256]{1,0:T(8,128)(2,1)} %slice.23.cap_ref, f32[1,2048]{1,0:T(1,128)} %bitcast.62, f32[2048,1]{1,0:T(8,128)} %get-tuple-element.12.b_ref, f32[2048,1]{1,0:T(8,128)} %copy.51.w_ref), custom_call_target="tpu_custom_call" | custom-call | flops 2147483648 | bytes 2097152 | tf_op jit(solution)/shard_map/pallas_call | solution.py:138
  304.1 6.6 %shard_map.98 = f32[16,128]{1,0:T(8,128)} custom-call(f32[16,128]{1,0:T(8,128)} %bitcast.72), custom_call_target="tpu_custom_call" | custom-call | tf_op jit(solution)/shard_map/pallas_call | solution.py:70
  311.5 6.6 %stack.39.cols_ref = f32[2048,8]{1,0:T(8,128)} concatenate(f32[2048,1]{1,0:T(8,128)S(1)} %copy-done.3, f32[2048,1]{1,0:T(8,128)S(1)} %copy-done.1, f32[2048,1]{1,0:T(8,128)} %get-tuple-element.11.b_ref, f32[2048,1]{1,0:T(8,128)} %get-tuple-element.8, f32[2048,1]{1,0:T(8,128)} %copy.51.w_ref, f32[2048,1]{1,0:T(8,128)} %copy.50.w_ref, f32[2048,1]{1,0:T(8,128)} %get-tuple-element.15.w_ref, ...), dimensions={1} | concatenate | bytes 131072 | tf_op jit(solution)/shard_map/stack | solution.py:315
  318.9 48.9 %shard_map.99 = (f32[2048,256]{1,0:T(8,128)}, f32[2048,256]{1,0:T(8,128)}) custom-call(bf16[2048,256]{1,0:T(8,128)(2,1)} %constant_dynamic-slice_fusion.img_ref, bf16[2048,256]{1,0:T(8,128)(2,1)} %slice.23.cap_ref, f32[8,2048]{1,0:T(8,128)} %stack.38.rows_ref, f32[2048,8]{1,0:T(8,128)} %stack.39.cols_ref), custom_call_target="tpu_custom_call" | custom-call | flops 6442450944 | bytes 6291456 | tf_op jit(solution)/shard_map/pallas_call | solution.py:248
  367.8 3.1 copy.54
  371.8 32.4 %reduce-scatter.6.cloned.1.call-done = f32[256,256]{1,0:T(8,128)} async-done(((f32[2048,256]{1,0:T(8,128)}), f32[256,256]{1,0:T(8,128)}) %reduce-scatter.6.cloned.1.call-update) | async-done | bytes 262160 | tf_op jit(solution)/shard_map/reduce_scatter | solution.py:320
  404.2 31.3 %reduce-scatter.4.cloned.1.call-done = f32[512,256]{1,0:T(8,128)} async-done(((f32[2048,256]{1,0:T(8,128)}), f32[512,256]{1,0:T(8,128)}) %reduce-scatter.4.cloned.1.call-update) | async-done | bytes 524304 | tf_op jit(solution)/shard_map/reduce_scatter | solution.py:317
  435.6 23.4 %reduce-scatter.8.cloned.1.call-done = f32[64,256]{1,0:T(8,128)} async-done(((f32[256,256]{1,0:T(8,128)}), f32[64,256]{1,0:T(8,128)}) %reduce-scatter.8.cloned.1.call-update) | async-done | bytes 65552 | tf_op jit(solution)/shard_map/reduce_scatter | solution.py:321
  (42 shorter events, 12.4 us)
Async XLA Ops:
  7.2 45.9 %all-gather.2.cloned.1.call-start = ((), (), s32[]{:S(2)}) async-start(), calls=%async_computation.3 | async-start | bytes 3932160 | tf_op jit(solution)/shard_map/all_gather | solution.py:281
  10.9 393.3 %reduce-scatter.6.cloned.1.call-start = ((), (), s32[]{:S(2)}) async-start(), calls=%async_computation.5 | async-start | bytes 2359296 | tf_op jit(solution)/shard_map/reduce_scatter | solution.py:320
  76.5 28.6 %copy-start = (f32[2048,258]{1,0:T(8,128)S(1)}, f32[2048,258]{1,0:T(8,128)}, u32[]{:S(2)}) copy-start(f32[2048,258]{1,0:T(8,128)} %all-gather.2.cloned.1.call-done) | copy-start | bytes 6340612
  294.2 17.2 %copy-start.1 = (f32[2048,1]{1,0:T(8,128)S(1)}, f32[2048,1]{1,0:T(8,128)}, u32[]{:S(2)}) copy-start(f32[2048,1]{1,0:T(8,128)} %get-tuple-element.13.b_ref) | copy-start | bytes 24580
  294.2 17.2 %copy-start.2 = (f32[2048,1]{1,0:T(8,128)S(1)}, f32[2048,1]{1,0:T(8,128)}, u32[]{:S(2)}) copy-start(f32[2048,1]{1,0:T(8,128)} %get-tuple-element.14) | copy-start | bytes 24580
  294.2 17.2 %copy-start.3 = (f32[2048,1]{1,0:T(8,128)S(1)}, f32[2048,1]{1,0:T(8,128)}, u32[]{:S(2)}) copy-start(f32[2048,1]{1,0:T(8,128)} %broadcast_4_b_ref_w_ref.2.b_ref.w_ref) | copy-start | bytes 24580
  311.4 6.7 %copy-start.4 = (f32[2048]{0:T(1024)S(1)}, f32[2048]{0:T(1024)}, u32[]{:S(2)}) copy-start(f32[2048]{0:T(1024)} %bitcast_add_fusion) | copy-start | bytes 24580
  311.4 6.7 %copy-start.5 = (f32[1,2048]{1,0:T(1,128)S(1)}, f32[1,2048]{1,0:T(1,128)}, u32[]{:S(2)}) copy-start(f32[1,2048]{1,0:T(1,128)} %broadcast_5_a_ref_w_ref.2.a_ref.w_ref) | copy-start | bytes 24580
  311.4 6.7 %copy-start.6 = (f32[16,128]{1,0:T(8,128)S(1)}, f32[16,128]{1,0:T(8,128)}, u32[]{:S(2)}) copy-start(f32[16,128]{1,0:T(8,128)} %neg.62) | copy-start | bytes 24580
  311.5 6.7 %copy-start.7 = (f32[2048]{0:T(1024)S(1)}, f32[2048]{0:T(1024)}, u32[]{:S(2)}) copy-start(f32[2048]{0:T(1024)} %get-tuple-element.6) | copy-start | bytes 24580
  311.5 6.7 %copy-start.8 = (f32[2048]{0:T(1024)S(1)}, f32[2048]{0:T(1024)}, u32[]{:S(2)}) copy-start(f32[2048]{0:T(1024)} %get-tuple-element.19) | copy-start | bytes 24580
  311.5 6.7 %copy-start.9 = (f32[2048]{0:T(1024)S(1)}, f32[2048]{0:T(1024)}, u32[]{:S(2)}) copy-start(f32[2048]{0:T(1024)} %get-tuple-element.17) | copy-start | bytes 24580
  371.0 64.6 %reduce-scatter.4.cloned.1.call-start = ((), (), s32[]{:S(2)}) async-start(), calls=%async_computation.4 | async-start | bytes 2621440 | tf_op jit(solution)/shard_map/reduce_scatter | solution.py:317
  371.7 87.3 %reduce-scatter.8.cloned.1.call-start = ((), (), s32[]{:S(2)}) async-start(), calls=%async_computation.6 | async-start | bytes 327680 | tf_op jit(solution)/shard_map/reduce_scatter | solution.py:321
Sparse Core Ops, SparseCore 0:
  11.0 41.9 all-gather.1
  371.1 33.0 reduce-scatter.5
  407.2 28.3 reduce-scatter.3
  438.4 20.5 reduce-scatter.7

commit v7 on v4

--- a/solution.py
+++ b/solution.py
@@ -261,7 +261,20 @@
     )(images, captions, rows, cols)
 
 
+CHUNKS = 2
+
+
+def _interleave(x, owners):
+    rest = x.shape[1:]
+    x = x.reshape((owners, CHUNKS, x.shape[0] // (owners * CHUNKS)) + rest)
+    return jnp.swapaxes(x, 0, 1).reshape((-1,) + rest)
+
+
 def body(images, captions, image_logw, caption_logw, image_cot, caption_cot):
+    owners = lax.axis_size("cap")
+    images = _interleave(images, owners)
+    image_logw = _interleave(image_logw, owners)
+    image_cot = _interleave(image_cot, owners)
     n = images.shape[0]
     c = captions.shape[0]
     zeros_r = jnp.zeros((n,), jnp.float32)
@@ -291,9 +304,17 @@
             col_bar = -gathered_sum(part, "img")
     rows = jnp.stack(row_hist + row_bars + [image_logw, zeros_r], axis=0)
     cols = jnp.stack(col_hist + col_bars + [caption_logw], axis=1)
-    ig_part, cg_part = final_pass(images, captions, rows, cols)
-    image_grad = lax.psum_scatter(ig_part, "cap", scatter_dimension=0, tiled=True)
-    caption_grad = lax.psum_scatter(cg_part, "img", scatter_dimension=0, tiled=True)
+    span = n // CHUNKS
+    grads = []
+    cg_total = None
+    for h in range(CHUNKS):
+        ig_part, cg_part = final_pass(
+            images[h * span:(h + 1) * span], captions, rows[:, h * span:(h + 1) * span], cols
+        )
+        grads.append(lax.psum_scatter(ig_part, "cap", scatter_dimension=0, tiled=True))
+        cg_total = cg_part if cg_total is None else cg_total + cg_part
+    image_grad = jnp.concatenate(grads, axis=0)
+    caption_grad = lax.psum_scatter(cg_total, "img", scatter_dimension=0, tiled=True)
     return (image_grad, caption_grad)
 
 

time: 434 us -> 500 us (1.15)
  waiting for transfers between devices: 119 us -> 167 us
  local copies, waits for them, and re-layouts: 11.8 us -> 24.7 us
    reduce_scatter x1 -> x2, waiting for transfers between devices: 88.2 us -> 135 us  [body(): lax.psum_scatter(ig_part, 'cap', scatter_dimension=0, tiled=True)]
    reshape x0 -> x5, local copies, waits for them, and re-layouts: none -> 6.21 us  [the longest x3 6.14 us: _interleave(): x = x.reshape((owners, CHUNKS, x.shape[0] // (owners * CHUNKS)) + rest)]
    slice x0 -> x2, local copies, waits for them, and re-layouts: none -> 5.56 us  [the longest x1 4.84 us: body(): images[h * span:(h + 1) * span]]
    pallas_call x1 -> x2, Pallas kernels: 39.7 us -> 41.9 us  [final_pass(): pl.pallas_call(functools.partial(_final_kernel, inv_root), out_shape=(jax...]
  transfers between devices with their start and end apart: 2 -> 3, of which waited for: 2 -> 3; matrix products, arithmetic and copies ran while one was open for 0% -> 1% of each run, Pallas kernels for 0% -> 4%
where the time goes in v7:
time: 500 us; the launch traced here: 496 us
  Pallas kernels  268 us (54%)
  waiting for transfers between devices  167 us (33%)
  local copies, waits for them, and re-layouts  24.7 us (5%)
  other arithmetic  22.4 us (4%)
  between operations  14.1 us (3%)
    reduce_scatter x2, waiting for transfers between devices, body(): lax.psum_scatter(ig_part, 'cap', scatter_dimension=0, tiled=True)  135 us
    pallas_call x11, Pallas kernels, combine(): pl.pallas_call(functools.partial(_combine_kernel, axis, n, mode), out_sha...  119 us
    pallas_call x6, Pallas kernels, row_pass(): pl.pallas_call(functools.partial(_row_kernel, mode, inv_root), out_shape=...  57 us
    pallas_call x5, Pallas kernels, col_pass(): pl.pallas_call(functools.partial(_col_kernel, mode, inv_root), out_shape=...  49.8 us
    pallas_call x2, Pallas kernels, final_pass(): pl.pallas_call(functools.partial(_final_kernel, inv_root), out_shape=(jax...  41.9 us
    reduce_scatter x1, waiting for transfers between devices, body(): lax.psum_scatter(cg_total, 'img', scatter_dimension=0, tiled=True)  31.8 us
  transfers between devices with their start and end apart: 3, of which 3 were waited for; matrix products, arithmetic and copies ran while one was open for 1% of the time, Pallas kernels for 4%

profile of v7, /device:TPU:0, one launch (start us, length us, event | category | flops | bytes accessed | tf_op | source)
XLA Modules:
  0.0 496.5 jit_solution(9449214536159414614)
XLA Ops:
  8.9 1.5 copy.51.w_ref
  10.4 0.8 copy.64
  11.2 4.6 copy.67
  17.2 10.0 %shard_map.77 = f32[1,8192]{1,0:T(1,128)} custom-call(bf16[8192,256]{1,0:T(8,128)(2,1)} %bitcast.48, bf16[512,256]{1,0:T(8,128)(2,1)} %cap_ref.25, f32[1,8192]{1,0:T(1,128)} %broadcast_7_a_ref_w_ref.2.a_ref.w_ref, f32[512,1]{1,0:T(8,128)} %broadcast_6_b_ref_w_ref.2.b_ref.w_ref, f32[512,1]{1,0:T(8,128)} %broadcast_6_b_ref_w_ref.2.b_ref.w_ref), custom_call_target="tpu_custom_call" | custom-call | flops 2147483648 | bytes 4456448 | tf_op jit(solution)/shard_map/pallas_call | solution.py:131
  27.2 14.9 %shard_map.78 = f32[64,128]{1,0:T(8,128)} custom-call(f32[64,128]{1,0:T(8,128)} %bitcast.76), custom_call_target="tpu_custom_call" | custom-call | tf_op jit(solution)/shard_map/pallas_call | solution.py:60
  43.5 10.3 %shard_map.79 = f32[512,1]{1,0:T(8,128)} custom-call(bf16[8192,256]{1,0:T(8,128)(2,1)} %bitcast.49, bf16[512,256]{1,0:T(8,128)(2,1)} %cap_ref.25, f32[1,8192]{1,0:T(1,128)} %fusion.2.a_ref, f32[512,1]{1,0:T(8,128)} %broadcast_6_b_ref_w_ref.2.b_ref.w_ref, f32[1,8192]{1,0:T(1,128)} %broadcast_7_a_ref_w_ref.2.a_ref.w_ref), custom_call_target="tpu_custom_call" | custom-call | flops 2147483648 | bytes 4456448 | tf_op jit(solution)/shard_map/pallas_call | solution.py:193
  53.8 1.7 reduce
  55.5 8.6 %shard_map.80 = f32[4,128]{1,0:T(4,128)} custom-call(f32[4,128]{1,0:T(4,128)} %bitcast.80), custom_call_target="tpu_custom_call" | custom-call | tf_op jit(solution)/shard_map/pallas_call | solution.py:60
  64.8 0.9 copy.47.b_ref
  65.6 9.9 %shard_map.81 = f32[1,8192]{1,0:T(1,128)} custom-call(bf16[8192,256]{1,0:T(8,128)(2,1)} %bitcast.50, bf16[512,256]{1,0:T(8,128)(2,1)} %cap_ref.25, f32[1,8192]{1,0:T(1,128)} %broadcast_7_a_ref_w_ref.2.a_ref.w_ref, f32[512,1]{1,0:T(8,128)} %copy.47.b_ref, f32[512,1]{1,0:T(8,128)} %broadcast_6_b_ref_w_ref.2.b_ref.w_ref), custom_call_target="tpu_custom_call" | custom-call | flops 2147483648 | bytes 4456448 | tf_op jit(solution)/shard_map/pallas_call | solution.py:131
  75.6 13.9 %shard_map.82 = f32[64,128]{1,0:T(8,128)} custom-call(f32[64,128]{1,0:T(8,128)} %bitcast.77), custom_call_target="tpu_custom_call" | custom-call | tf_op jit(solution)/shard_map/pallas_call | solution.py:60
  90.9 0.9 copy.56.b_ref
  91.8 10.4 %shard_map.83 = f32[512,1]{1,0:T(8,128)} custom-call(bf16[8192,256]{1,0:T(8,128)(2,1)} %bitcast.51, bf16[512,256]{1,0:T(8,128)(2,1)} %cap_ref.25, f32[1,8192]{1,0:T(1,128)} %get-tuple-element.19.a_ref, f32[512,1]{1,0:T(8,128)} %broadcast_6_b_ref_w_ref.2.b_ref.w_ref, f32[1,8192]{1,0:T(1,128)} %broadcast_7_a_ref_w_ref.2.a_ref.w_ref), custom_call_target="tpu_custom_call" | custom-call | flops 2147483648 | bytes 4456448 | tf_op jit(solution)/shard_map/pallas_call | solution.py:193
  102.1 1.7 reduce.1
  103.8 6.5 %shard_map.84 = f32[4,128]{1,0:T(4,128)} custom-call(f32[4,128]{1,0:T(4,128)} %bitcast.81), custom_call_target="tpu_custom_call" | custom-call | tf_op jit(solution)/shard_map/pallas_call | solution.py:60
  111.0 0.9 copy.48.b_ref
  111.9 9.9 %shard_map.85 = f32[1,8192]{1,0:T(1,128)} custom-call(bf16[8192,256]{1,0:T(8,128)(2,1)} %bitcast.52, bf16[512,256]{1,0:T(8,128)(2,1)} %cap_ref.25, f32[1,8192]{1,0:T(1,128)} %broadcast_7_a_ref_w_ref.2.a_ref.w_ref, f32[512,1]{1,0:T(8,128)} %copy.48.b_ref, f32[512,1]{1,0:T(8,128)} %broadcast_6_b_ref_w_ref.2.b_ref.w_ref), custom_call_target="tpu_custom_call" | custom-call | flops 2147483648 | bytes 4456448 | tf_op jit(solution)/shard_map/pallas_call | solution.py:131
  121.8 14.0 %shard_map.86 = f32[64,128]{1,0:T(8,128)} custom-call(f32[64,128]{1,0:T(8,128)} %bitcast.78), custom_call_target="tpu_custom_call" | custom-call | tf_op jit(solution)/shard_map/pallas_call | solution.py:60
  137.3 0.9 copy.53.b_ref
  138.1 10.4 %shard_map.87 = f32[512,1]{1,0:T(8,128)} custom-call(bf16[8192,256]{1,0:T(8,128)(2,1)} %bitcast.53, bf16[512,256]{1,0:T(8,128)(2,1)} %cap_ref.25, f32[1,8192]{1,0:T(1,128)} %get-tuple-element.17.a_ref, f32[512,1]{1,0:T(8,128)} %broadcast_6_b_ref_w_ref.2.b_ref.w_ref, f32[1,8192]{1,0:T(1,128)} %broadcast_7_a_ref_w_ref.2.a_ref.w_ref), custom_call_target="tpu_custom_call" | custom-call | flops 2147483648 | bytes 4456448 | tf_op jit(solution)/shard_map/pallas_call | solution.py:193
  148.5 1.7 reduce.2
  150.2 6.6 %shard_map.88 = f32[4,128]{1,0:T(4,128)} custom-call(f32[4,128]{1,0:T(4,128)} %bitcast.82), custom_call_target="tpu_custom_call" | custom-call | tf_op jit(solution)/shard_map/pallas_call | solution.py:60
  157.5 0.9 copy.50.b_ref
  158.3 9.0 %shard_map.89 = f32[1,8192]{1,0:T(1,128)} custom-call(bf16[8192,256]{1,0:T(8,128)(2,1)} %bitcast.54, bf16[512,256]{1,0:T(8,128)(2,1)} %cap_ref.25, f32[1,8192]{1,0:T(1,128)} %get-tuple-element.17.a_ref, f32[512,1]{1,0:T(8,128)} %copy.50.b_ref, f32[512,1]{1,0:T(8,128)} %copy.51.w_ref), custom_call_target="tpu_custom_call" | custom-call | flops 2147483648 | bytes 4456448 | tf_op jit(solution)/shard_map/pallas_call | solution.py:131
  167.4 13.9 %shard_map.90 = f32[64,128]{1,0:T(8,128)} custom-call(f32[64,128]{1,0:T(8,128)} %bitcast.73), custom_call_target="tpu_custom_call" | custom-call | tf_op jit(solution)/shard_map/pallas_call | solution.py:60
  182.7 9.4 %shard_map.91 = f32[512,1]{1,0:T(8,128)} custom-call(bf16[8192,256]{1,0:T(8,128)(2,1)} %bitcast.55, bf16[512,256]{1,0:T(8,128)(2,1)} %cap_ref.25, f32[1,8192]{1,0:T(1,128)} %get-tuple-element.16.a_ref, f32[512,1]{1,0:T(8,128)} %copy.48.b_ref, f32[1,8192]{1,0:T(1,128)} %add.19.w_ref), custom_call_target="tpu_custom_call" | custom-call | flops 2147483648 | bytes 4456448 | tf_op jit(solution)/shard_map/pallas_call | solution.py:193
  192.0 1.7 reduce.3
  193.7 6.5 %shard_map.92 = f32[4,128]{1,0:T(4,128)} custom-call(f32[4,128]{1,0:T(4,128)} %bitcast.83), custom_call_target="tpu_custom_call" | custom-call | tf_op jit(solution)/shard_map/pallas_call | solution.py:60
  200.9 0.9 copy.54.w_ref
  201.8 9.0 %shard_map.93 = f32[1,8192]{1,0:T(1,128)} custom-call(bf16[8192,256]{1,0:T(8,128)(2,1)} %bitcast.56, bf16[512,256]{1,0:T(8,128)(2,1)} %cap_ref.25, f32[1,8192]{1,0:T(1,128)} %get-tuple-element.19.a_ref, f32[512,1]{1,0:T(8,128)} %copy.53.b_ref, f32[512,1]{1,0:T(8,128)} %copy.54.w_ref), custom_call_target="tpu_custom_call" | custom-call | flops 2147483648 | bytes 4456448 | tf_op jit(solution)/shard_map/pallas_call | solution.py:131
  210.8 13.9 %shard_map.94 = f32[64,128]{1,0:T(8,128)} custom-call(f32[64,128]{1,0:T(8,128)} %bitcast.74), custom_call_target="tpu_custom_call" | custom-call | tf_op jit(solution)/shard_map/pallas_call | solution.py:60
  224.7 1.4 neg.69
  226.1 9.4 %shard_map.95 = f32[512,1]{1,0:T(8,128)} custom-call(bf16[8192,256]{1,0:T(8,128)(2,1)} %bitcast.57, bf16[512,256]{1,0:T(8,128)(2,1)} %cap_ref.25, f32[1,8192]{1,0:T(1,128)} %get-tuple-element.18.a_ref, f32[512,1]{1,0:T(8,128)} %copy.47.b_ref, f32[1,8192]{1,0:T(1,128)} %bitcast.63), custom_call_target="tpu_custom_call" | custom-call | flops 2147483648 | bytes 4456448 | tf_op jit(solution)/shard_map/pallas_call | solution.py:193
  235.4 1.7 reduce.4
  237.1 6.6 %shard_map.96 = f32[4,128]{1,0:T(4,128)} custom-call(f32[4,128]{1,0:T(4,128)} %bitcast.79), custom_call_target="tpu_custom_call" | custom-call | tf_op jit(solution)/shard_map/pallas_call | solution.py:60
  244.5 0.9 copy.57.w_ref
  245.3 9.0 %shard_map.97 = f32[1,8192]{1,0:T(1,128)} custom-call(bf16[8192,256]{1,0:T(8,128)(2,1)} %bitcast.58, bf16[512,256]{1,0:T(8,128)(2,1)} %cap_ref.25, f32[1,8192]{1,0:T(1,128)} %fusion.2.a_ref, f32[512,1]{1,0:T(8,128)} %copy.56.b_ref, f32[512,1]{1,0:T(8,128)} %copy.57.w_ref), custom_call_target="tpu_custom_call" | custom-call | flops 2147483648 | bytes 4456448 | tf_op jit(solution)/shard_map/pallas_call | solution.py:131
  254.4 13.9 %shard_map.98 = f32[64,128]{1,0:T(8,128)} custom-call(f32[64,128]{1,0:T(8,128)} %bitcast.75), custom_call_target="tpu_custom_call" | custom-call | tf_op jit(solution)/shard_map/pallas_call | solution.py:60
  270.4 4.8 fusion.3
  275.3 1.4 stack.11.cols_ref
  276.7 20.8 %shard_map.100 = (f32[4096,256]{1,0:T(8,128)}, f32[512,256]{1,0:T(8,128)}) custom-call(bf16[4096,256]{1,0:T(8,128)(2,1)} %bitcast.62, bf16[512,256]{1,0:T(8,128)(2,1)} %cap_ref.25, f32[8,4096]{1,0:T(8,128)} %get-tuple-element.15.rows_ref, f32[512,8]{1,0:T(8,128)} %stack.11.cols_ref), custom_call_target="tpu_custom_call" | custom-call | flops 3221225472 | bytes 7077888 | tf_op jit(solution)/shard_map/pallas_call | solution.py:241
  297.6 21.1 %shard_map.99 = (f32[4096,256]{1,0:T(8,128)}, f32[512,256]{1,0:T(8,128)}) custom-call(bf16[4096,256]{1,0:T(8,128)(2,1)} %bitcast.61, bf16[512,256]{1,0:T(8,128)(2,1)} %cap_ref.25, f32[8,4096]{1,0:T(8,128)} %get-tuple-element.14.rows_ref, f32[512,8]{1,0:T(8,128)} %stack.11.cols_ref), custom_call_target="tpu_custom_call" | custom-call | flops 3221225472 | bytes 7077888 | tf_op jit(solution)/shard_map/pallas_call | solution.py:241
  318.8 1.0 copy-done.6
  320.0 0.9 add.20
  320.9 54.4 %reduce-scatter.6.cloned.1.call-done = f32[256,256]{1,0:T(8,128)} async-done(((f32[4096,256]{1,0:T(8,128)}), f32[256,256]{1,0:T(8,128)}) %reduce-scatter.6.cloned.1.call-update) | async-done | bytes 262160 | tf_op jit(solution)/shard_map/reduce_scatter | solution.py:314
  375.3 80.9 %reduce-scatter.4.cloned.1.call-done = f32[256,256]{1,0:T(8,128)} async-done(((f32[4096,256]{1,0:T(8,128)}), f32[256,256]{1,0:T(8,128)}) %reduce-scatter.4.cloned.1.call-update) | async-done | bytes 262160 | tf_op jit(solution)/shard_map/reduce_scatter | solution.py:314
  456.3 1.9 pad_maximum_fusion
  458.1 31.8 %reduce-scatter.8.cloned.1.call-done = f32[64,256]{1,0:T(8,128)} async-done(((f32[512,256]{1,0:T(8,128)}), f32[64,256]{1,0:T(8,128)}) %reduce-scatter.8.cloned.1.call-update) | async-done | bytes 65552 | tf_op jit(solution)/shard_map/reduce_scatter | solution.py:317
  (60 shorter events, 14.5 us)
Async XLA Ops:
  7.2 368.1 %reduce-scatter.6.cloned.1.call-start = ((), (), s32[]{:S(2)}) async-start(), calls=%async_computation.4 | async-start | bytes 4456448 | tf_op jit(solution)/shard_map/reduce_scatter | solution.py:314
  42.1 22.0 %copy-start.14 = (f32[512]{0:T(512)S(1)}, f32[512]{0:T(512)}, u32[]{:S(2)}) copy-start(f32[512]{0:T(512)} %param.9) | copy-start | bytes 6148
  237.1 31.9 %copy-start.8 = (f32[1,8192]{1,0:T(1,128)S(1)}, f32[1,8192]{1,0:T(1,128)}, u32[]{:S(2)}) copy-start(f32[1,8192]{1,0:T(1,128)} %fusion.2.a_ref) | copy-start | bytes 98308
  237.1 31.9 %copy-start.9 = (f32[1,8192]{1,0:T(1,128)S(1)}, f32[1,8192]{1,0:T(1,128)}, u32[]{:S(2)}) copy-start(f32[1,8192]{1,0:T(1,128)} %add.19.w_ref) | copy-start | bytes 98308
  237.1 31.9 %copy-start.10 = (f32[1,8192]{1,0:T(1,128)S(1)}, f32[1,8192]{1,0:T(1,128)}, u32[]{:S(2)}) copy-start(f32[1,8192]{1,0:T(1,128)} %broadcast_7_a_ref_w_ref.2.a_ref.w_ref) | copy-start | bytes 98308
  237.1 31.9 %copy-start.11 = (f32[64,128]{1,0:T(8,128)S(1)}, f32[64,128]{1,0:T(8,128)}, u32[]{:S(2)}) copy-start(f32[64,128]{1,0:T(8,128)} %neg.69) | copy-start | bytes 98308
  237.1 31.9 %copy-start.12 = (f32[1,8192]{1,0:T(1,128)S(1)}, f32[1,8192]{1,0:T(1,128)}, u32[]{:S(2)}) copy-start(f32[1,8192]{1,0:T(1,128)} %get-tuple-element.19.a_ref) | copy-start | bytes 98308
  237.1 31.9 %copy-start.13 = (f32[1,8192]{1,0:T(1,128)S(1)}, f32[1,8192]{1,0:T(1,128)}, u32[]{:S(2)}) copy-start(f32[1,8192]{1,0:T(1,128)} %get-tuple-element.17.a_ref) | copy-start | bytes 98308
  270.3 4.9 copy-start
  270.3 4.9 copy-start.1
  270.4 4.9 copy-start.2
  270.4 4.9 copy-start.3
  270.4 4.9 copy-start.4
  270.4 4.9 copy-start.5
  297.5 158.7 %reduce-scatter.4.cloned.1.call-start = ((), (), s32[]{:S(2)}) async-start(), calls=%async_computation.3 | async-start | bytes 4456448 | tf_op jit(solution)/shard_map/reduce_scatter | solution.py:314
  318.7 1.1 copy-start.6
  318.7 1.3 copy-start.7
  318.7 171.2 %reduce-scatter.8.cloned.1.call-start = ((), (), s32[]{:S(2)}) async-start(), calls=%async_computation.5 | async-start | bytes 589824 | tf_op jit(solution)/shard_map/reduce_scatter | solution.py:317
Sparse Core Ops, SparseCore 0:
  297.7 77.5 reduce-scatter.5
  378.6 77.5 reduce-scatter.3
  459.2 30.6 reduce-scatter.7

commit v8 on v4

--- a/solution.py
+++ b/solution.py
@@ -77,6 +77,50 @@
 
 
 SMOOTHING = 0.25
+
+
+def _scatter_kernel(axis, n, x_ref, o_ref, buf, send_sem, recv_sem):
+    me = lax.axis_index(axis)
+    barrier = pltpu.get_barrier_semaphore()
+    for k in range(1, n):
+        pl.semaphore_signal(barrier, inc=1, device_id=_peer(axis, k, n), device_id_type=MESH)
+    pl.semaphore_wait(barrier, n - 1)
+    copies = []
+    for k in range(1, n):
+        copy = pltpu.make_async_remote_copy(
+            src_ref=x_ref.at[lax.rem(me + k, n)],
+            dst_ref=buf.at[k],
+            send_sem=send_sem.at[k],
+            recv_sem=recv_sem.at[k],
+            device_id=_peer(axis, k, n),
+            device_id_type=MESH,
+        )
+        copy.start()
+        copies.append(copy)
+    for copy in copies:
+        copy.wait()
+    acc = x_ref[me]
+    for k in range(1, n):
+        acc = acc + buf[k]
+    o_ref[...] = acc
+
+
+def scatter_sum(x, axis, cid):
+    n = lax.axis_size(axis)
+    rows = x.shape[0] // n
+    lanes = x.shape[1]
+    return pl.pallas_call(
+        functools.partial(_scatter_kernel, axis, n),
+        out_shape=jax.ShapeDtypeStruct((rows, lanes), jnp.float32),
+        in_specs=[pl.BlockSpec(memory_space=pltpu.VMEM)],
+        out_specs=pl.BlockSpec(memory_space=pltpu.VMEM),
+        scratch_shapes=[
+            pltpu.VMEM((n, rows, lanes), jnp.float32),
+            pltpu.SemaphoreType.DMA((n,)),
+            pltpu.SemaphoreType.DMA((n,)),
+        ],
+        compiler_params=pltpu.CompilerParams(collective_id=cid, has_side_effects=True),
+    )(x.reshape(n, rows, lanes))
 
 
 _IDS = {("cap", "lse"): 0, ("img", "lse"): 1, ("cap", "sum"): 2, ("img", "sum"): 3}
@@ -293,7 +337,7 @@
     cols = jnp.stack(col_hist + col_bars + [caption_logw], axis=1)
     ig_part, cg_part = final_pass(images, captions, rows, cols)
     image_grad = lax.psum_scatter(ig_part, "cap", scatter_dimension=0, tiled=True)
-    caption_grad = lax.psum_scatter(cg_part, "img", scatter_dimension=0, tiled=True)
+    caption_grad = scatter_sum(cg_part, "img", 4)
     return (image_grad, caption_grad)
 
 

time: 434 us -> 401 us (0.924)
  waiting for transfers between devices: 119 us -> 74 us
  Pallas kernels: 266 us -> 277 us
    reduce_scatter x1 -> x0, waiting for transfers between devices: 30.1 us -> none  [body(): lax.psum_scatter(cg_part, 'img', scatter_dimension=0, tiled=True)]
    reduce_scatter x1, waiting for transfers between devices: 88.2 us -> 74 us  [body(): lax.psum_scatter(ig_part, 'cap', scatter_dimension=0, tiled=True)]
    pallas_call x0 -> x1, Pallas kernels: none -> 11.2 us  [scatter_sum(): pl.pallas_call(functools.partial(_scatter_kernel, axis, n), out_shape=jax...]
  transfers between devices with their start and end apart: 2 -> 1, of which waited for: 2 -> 1; matrix products, arithmetic and copies ran while one was open for 0% -> 0% of each run, Pallas kernels for 0% -> 3%
where the time goes in v8:
time: 401 us; the launch traced here: 398 us
  Pallas kernels  277 us (69%)
  waiting for transfers between devices  74 us (18%)
  other arithmetic  19.5 us (5%)
  between operations  14.3 us (4%)
  local copies, waits for them, and re-layouts  13.3 us (3%)
    pallas_call x11, Pallas kernels, combine(): pl.pallas_call(functools.partial(_combine_kernel, axis, n, mode), out_sha...  119 us
    reduce_scatter x1, waiting for transfers between devices, body(): lax.psum_scatter(ig_part, 'cap', scatter_dimension=0, tiled=True)  74 us
    pallas_call x6, Pallas kernels, row_pass(): pl.pallas_call(functools.partial(_row_kernel, mode, inv_root), out_shape=...  57 us
    pallas_call x5, Pallas kernels, col_pass(): pl.pallas_call(functools.partial(_col_kernel, mode, inv_root), out_shape=...  49.9 us
    pallas_call x1, Pallas kernels, final_pass(): pl.pallas_call(functools.partial(_final_kernel, inv_root), out_shape=(jax...  39.7 us
    pallas_call x1, Pallas kernels, scatter_sum(): pl.pallas_call(functools.partial(_scatter_kernel, axis, n), out_shape=jax...  11.2 us
    pallas_call x5, other arithmetic, col_pass(): pl.pallas_call(functools.partial(_col_kernel, mode, inv_root), out_shape=...  8.38 us
  transfers between devices with their start and end apart: 1, of which 1 were waited for; matrix products, arithmetic and copies ran while one was open for 0% of the time, Pallas kernels for 3%

profile of v8, /device:TPU:0, one launch (start us, length us, event | category | flops | bytes accessed | tf_op | source)
XLA Modules:
  0.0 398.1 jit_solution(16205753145210813571)
XLA Ops:
  7.9 0.7 broadcast_7_b_ref_w_ref.2.b_ref.w_ref
  8.6 10.0 %shard_map.77 = f32[1,8192]{1,0:T(1,128)} custom-call(bf16[8192,256]{1,0:T(8,128)(2,1)} %img_ref.23, bf16[512,256]{1,0:T(8,128)(2,1)} %cap_ref.23, f32[1,8192]{1,0:T(1,128)} %broadcast_6_a_ref_w_ref.2.a_ref.w_ref, f32[512,1]{1,0:T(8,128)} %broadcast_7_b_ref_w_ref.2.b_ref.w_ref, f32[512,1]{1,0:T(8,128)} %broadcast_7_b_ref_w_ref.2.b_ref.w_ref), custom_call_target="tpu_custom_call" | custom-call | flops 2147483648 | bytes 4456448 | tf_op jit(solution)/shard_map/pallas_call | solution.py:175
  18.6 14.9 %shard_map.78 = f32[64,128]{1,0:T(8,128)} custom-call(f32[64,128]{1,0:T(8,128)} %bitcast.75), custom_call_target="tpu_custom_call" | custom-call | tf_op jit(solution)/shard_map/pallas_call | solution.py:60
  33.5 1.5 copy.40.w_ref
  35.0 1.4 bitcast_subtract_fusion.2
  36.4 10.3 %shard_map.79 = f32[512,1]{1,0:T(8,128)} custom-call(bf16[8192,256]{1,0:T(8,128)(2,1)} %img_ref.23, bf16[512,256]{1,0:T(8,128)(2,1)} %cap_ref.23, f32[1,8192]{1,0:T(1,128)} %bitcast.57, f32[512,1]{1,0:T(8,128)} %broadcast_7_b_ref_w_ref.2.b_ref.w_ref, f32[1,8192]{1,0:T(1,128)} %broadcast_6_a_ref_w_ref.2.a_ref.w_ref), custom_call_target="tpu_custom_call" | custom-call | flops 2147483648 | bytes 4456448 | tf_op jit(solution)/shard_map/pallas_call | solution.py:237
  46.7 1.7 reduce
  48.4 8.5 %shard_map.80 = f32[4,128]{1,0:T(4,128)} custom-call(f32[4,128]{1,0:T(4,128)} %bitcast.81), custom_call_target="tpu_custom_call" | custom-call | tf_op jit(solution)/shard_map/pallas_call | solution.py:60
  57.7 0.9 copy.37.b_ref
  58.5 9.9 %shard_map.81 = f32[1,8192]{1,0:T(1,128)} custom-call(bf16[8192,256]{1,0:T(8,128)(2,1)} %img_ref.23, bf16[512,256]{1,0:T(8,128)(2,1)} %cap_ref.23, f32[1,8192]{1,0:T(1,128)} %broadcast_6_a_ref_w_ref.2.a_ref.w_ref, f32[512,1]{1,0:T(8,128)} %copy.37.b_ref, f32[512,1]{1,0:T(8,128)} %broadcast_7_b_ref_w_ref.2.b_ref.w_ref), custom_call_target="tpu_custom_call" | custom-call | flops 2147483648 | bytes 4456448 | tf_op jit(solution)/shard_map/pallas_call | solution.py:175
  68.4 13.9 %shard_map.82 = f32[64,128]{1,0:T(8,128)} custom-call(f32[64,128]{1,0:T(8,128)} %bitcast.76), custom_call_target="tpu_custom_call" | custom-call | tf_op jit(solution)/shard_map/pallas_call | solution.py:60
  82.4 1.4 multiply_subtract_fusion.1
  83.8 0.9 copy.45.b_ref
  84.6 10.4 %shard_map.83 = f32[512,1]{1,0:T(8,128)} custom-call(bf16[8192,256]{1,0:T(8,128)(2,1)} %img_ref.23, bf16[512,256]{1,0:T(8,128)(2,1)} %cap_ref.23, f32[1,8192]{1,0:T(1,128)} %bitcast.65, f32[512,1]{1,0:T(8,128)} %broadcast_7_b_ref_w_ref.2.b_ref.w_ref, f32[1,8192]{1,0:T(1,128)} %broadcast_6_a_ref_w_ref.2.a_ref.w_ref), custom_call_target="tpu_custom_call" | custom-call | flops 2147483648 | bytes 4456448 | tf_op jit(solution)/shard_map/pallas_call | solution.py:237
  95.0 1.7 reduce.1
  96.7 6.6 %shard_map.84 = f32[4,128]{1,0:T(4,128)} custom-call(f32[4,128]{1,0:T(4,128)} %bitcast.82), custom_call_target="tpu_custom_call" | custom-call | tf_op jit(solution)/shard_map/pallas_call | solution.py:60
  103.9 0.9 copy.38.b_ref
  104.8 9.9 %shard_map.85 = f32[1,8192]{1,0:T(1,128)} custom-call(bf16[8192,256]{1,0:T(8,128)(2,1)} %img_ref.23, bf16[512,256]{1,0:T(8,128)(2,1)} %cap_ref.23, f32[1,8192]{1,0:T(1,128)} %broadcast_6_a_ref_w_ref.2.a_ref.w_ref, f32[512,1]{1,0:T(8,128)} %copy.38.b_ref, f32[512,1]{1,0:T(8,128)} %broadcast_7_b_ref_w_ref.2.b_ref.w_ref), custom_call_target="tpu_custom_call" | custom-call | flops 2147483648 | bytes 4456448 | tf_op jit(solution)/shard_map/pallas_call | solution.py:175
  114.7 14.0 %shard_map.86 = f32[64,128]{1,0:T(8,128)} custom-call(f32[64,128]{1,0:T(8,128)} %bitcast.77), custom_call_target="tpu_custom_call" | custom-call | tf_op jit(solution)/shard_map/pallas_call | solution.py:60
  128.7 1.4 multiply_subtract_fusion
  130.1 0.9 copy.42.b_ref
  130.9 10.4 %shard_map.87 = f32[512,1]{1,0:T(8,128)} custom-call(bf16[8192,256]{1,0:T(8,128)(2,1)} %img_ref.23, bf16[512,256]{1,0:T(8,128)(2,1)} %cap_ref.23, f32[1,8192]{1,0:T(1,128)} %bitcast.68, f32[512,1]{1,0:T(8,128)} %broadcast_7_b_ref_w_ref.2.b_ref.w_ref, f32[1,8192]{1,0:T(1,128)} %broadcast_6_a_ref_w_ref.2.a_ref.w_ref), custom_call_target="tpu_custom_call" | custom-call | flops 2147483648 | bytes 4456448 | tf_op jit(solution)/shard_map/pallas_call | solution.py:237
  141.3 1.7 reduce.2
  143.0 6.6 %shard_map.88 = f32[4,128]{1,0:T(4,128)} custom-call(f32[4,128]{1,0:T(4,128)} %bitcast.83), custom_call_target="tpu_custom_call" | custom-call | tf_op jit(solution)/shard_map/pallas_call | solution.py:60
  150.3 0.9 copy.39.b_ref
  151.1 9.0 %shard_map.89 = f32[1,8192]{1,0:T(1,128)} custom-call(bf16[8192,256]{1,0:T(8,128)(2,1)} %img_ref.23, bf16[512,256]{1,0:T(8,128)(2,1)} %cap_ref.23, f32[1,8192]{1,0:T(1,128)} %bitcast.69, f32[512,1]{1,0:T(8,128)} %copy.39.b_ref, f32[512,1]{1,0:T(8,128)} %copy.40.w_ref), custom_call_target="tpu_custom_call" | custom-call | flops 2147483648 | bytes 4456448 | tf_op jit(solution)/shard_map/pallas_call | solution.py:175
  160.2 13.9 %shard_map.90 = f32[64,128]{1,0:T(8,128)} custom-call(f32[64,128]{1,0:T(8,128)} %bitcast.72), custom_call_target="tpu_custom_call" | custom-call | tf_op jit(solution)/shard_map/pallas_call | solution.py:60
  174.1 1.4 bitcast_add_fusion
  175.5 9.4 %shard_map.91 = f32[512,1]{1,0:T(8,128)} custom-call(bf16[8192,256]{1,0:T(8,128)(2,1)} %img_ref.23, bf16[512,256]{1,0:T(8,128)(2,1)} %cap_ref.23, f32[1,8192]{1,0:T(1,128)} %bitcast.79, f32[512,1]{1,0:T(8,128)} %copy.38.b_ref, f32[1,8192]{1,0:T(1,128)} %bitcast.60), custom_call_target="tpu_custom_call" | custom-call | flops 2147483648 | bytes 4456448 | tf_op jit(solution)/shard_map/pallas_call | solution.py:237
  184.8 1.7 reduce.3
  186.5 6.5 %shard_map.92 = f32[4,128]{1,0:T(4,128)} custom-call(f32[4,128]{1,0:T(4,128)} %bitcast.84), custom_call_target="tpu_custom_call" | custom-call | tf_op jit(solution)/shard_map/pallas_call | solution.py:60
  193.7 0.9 copy.43.w_ref
  194.6 9.0 %shard_map.93 = f32[1,8192]{1,0:T(1,128)} custom-call(bf16[8192,256]{1,0:T(8,128)(2,1)} %img_ref.23, bf16[512,256]{1,0:T(8,128)(2,1)} %cap_ref.23, f32[1,8192]{1,0:T(1,128)} %bitcast.66, f32[512,1]{1,0:T(8,128)} %copy.42.b_ref, f32[512,1]{1,0:T(8,128)} %copy.43.w_ref), custom_call_target="tpu_custom_call" | custom-call | flops 2147483648 | bytes 4456448 | tf_op jit(solution)/shard_map/pallas_call | solution.py:175
  203.6 13.9 %shard_map.94 = f32[64,128]{1,0:T(8,128)} custom-call(f32[64,128]{1,0:T(8,128)} %bitcast.73), custom_call_target="tpu_custom_call" | custom-call | tf_op jit(solution)/shard_map/pallas_call | solution.py:60
  217.5 1.4 neg.62
  219.0 9.5 %shard_map.95 = f32[512,1]{1,0:T(8,128)} custom-call(bf16[8192,256]{1,0:T(8,128)(2,1)} %img_ref.23, bf16[512,256]{1,0:T(8,128)(2,1)} %cap_ref.23, f32[1,8192]{1,0:T(1,128)} %bitcast.78, f32[512,1]{1,0:T(8,128)} %copy.37.b_ref, f32[1,8192]{1,0:T(1,128)} %bitcast.62), custom_call_target="tpu_custom_call" | custom-call | flops 2147483648 | bytes 4456448 | tf_op jit(solution)/shard_map/pallas_call | solution.py:237
  228.4 1.6 reduce.4
  230.1 6.5 %shard_map.96 = f32[4,128]{1,0:T(4,128)} custom-call(f32[4,128]{1,0:T(4,128)} %bitcast.80), custom_call_target="tpu_custom_call" | custom-call | tf_op jit(solution)/shard_map/pallas_call | solution.py:60
  237.3 0.9 copy.46.w_ref
  238.2 9.1 %shard_map.97 = f32[1,8192]{1,0:T(1,128)} custom-call(bf16[8192,256]{1,0:T(8,128)(2,1)} %img_ref.23, bf16[512,256]{1,0:T(8,128)(2,1)} %cap_ref.23, f32[1,8192]{1,0:T(1,128)} %bitcast.58, f32[512,1]{1,0:T(8,128)} %copy.45.b_ref, f32[512,1]{1,0:T(8,128)} %copy.46.w_ref), custom_call_target="tpu_custom_call" | custom-call | flops 2147483648 | bytes 4456448 | tf_op jit(solution)/shard_map/pallas_call | solution.py:175
  247.2 13.9 %shard_map.98 = f32[64,128]{1,0:T(8,128)} custom-call(f32[64,128]{1,0:T(8,128)} %bitcast.74), custom_call_target="tpu_custom_call" | custom-call | tf_op jit(solution)/shard_map/pallas_call | solution.py:60
  261.1 0.8 neg.66
  262.3 1.1 stack.36.rows_ref
  263.4 1.4 stack.39.cols_ref
  264.8 39.7 %shard_map.99 = (f32[8192,256]{1,0:T(8,128)}, f32[512,256]{1,0:T(8,128)}) custom-call(bf16[8192,256]{1,0:T(8,128)(2,1)} %img_ref.23, bf16[512,256]{1,0:T(8,128)(2,1)} %cap_ref.23, f32[8,8192]{1,0:T(8,128)} %stack.36.rows_ref, f32[512,8]{1,0:T(8,128)} %stack.39.cols_ref), custom_call_target="tpu_custom_call" | custom-call | flops 6442450944 | bytes 13369344 | tf_op jit(solution)/shard_map/pallas_call | solution.py:285
  304.6 11.2 %shard_map.100 = f32[64,256]{1,0:T(8,128)} custom-call(f32[8,64,256]{2,1,0:T(8,128)} %bitcast.55), custom_call_target="tpu_custom_call" | custom-call | tf_op jit(solution)/shard_map/pallas_call | solution.py:112
  315.8 74.0 %reduce-scatter.2.cloned.1.call-done = f32[512,256]{1,0:T(8,128)} async-done(((f32[8192,256]{1,0:T(8,128)}), f32[512,256]{1,0:T(8,128)}) %reduce-scatter.2.cloned.1.call-update) | async-done | bytes 524304 | tf_op jit(solution)/shard_map/reduce_scatter | solution.py:339
  389.8 1.5 copy.55
  (40 shorter events, 4.4 us)
Async XLA Ops:
  7.2 27.8 %copy-start.6 = (f32[8192]{0:T(1024)S(1)}, f32[8192]{0:T(1024)}, u32[]{:S(2)}) copy-start(f32[8192]{0:T(1024)} %param.8) | copy-start | bytes 98308
  7.2 382.6 %reduce-scatter.2.cloned.1.call-start = ((), (), s32[]{:S(2)}) async-start(), calls=%async_computation.1 | async-start | bytes 8912896 | tf_op jit(solution)/shard_map/reduce_scatter | solution.py:339
  7.9 49.1 %copy-start.13 = (f32[512]{0:T(512)S(1)}, f32[512]{0:T(512)}, u32[]{:S(2)}) copy-start(f32[512]{0:T(512)} %param.9) | copy-start | bytes 6148
  130.1 44.0 %copy-start.14 = (f32[8192]{0:T(1024)S(1)}, f32[8192]{0:T(1024)}, u32[]{:S(2)}) copy-start(f32[8192]{0:T(1024)} %param.10) | copy-start | bytes 98308
  218.9 43.3 %copy-start.7 = (f32[8192]{0:T(1024)S(1)}, f32[8192]{0:T(1024)}, u32[]{:S(2)}) copy-start(f32[8192]{0:T(1024)} %bitcast_subtract_fusion.2) | copy-start | bytes 98308
  218.9 43.3 %copy-start.8 = (f32[8192]{0:T(1024)S(1)}, f32[8192]{0:T(1024)}, u32[]{:S(2)}) copy-start(f32[8192]{0:T(1024)} %bitcast_add_fusion) | copy-start | bytes 98308
  218.9 43.4 %copy-start.9 = (f32[1,8192]{1,0:T(1,128)S(1)}, f32[1,8192]{1,0:T(1,128)}, u32[]{:S(2)}) copy-start(f32[1,8192]{1,0:T(1,128)} %broadcast_6_a_ref_w_ref.2.a_ref.w_ref) | copy-start | bytes 98308
  218.9 43.4 %copy-start.10 = (f32[64,128]{1,0:T(8,128)S(1)}, f32[64,128]{1,0:T(8,128)}, u32[]{:S(2)}) copy-start(f32[64,128]{1,0:T(8,128)} %neg.62) | copy-start | bytes 98308
  218.9 43.4 %copy-start.11 = (f32[8192]{0:T(1024)S(1)}, f32[8192]{0:T(1024)}, u32[]{:S(2)}) copy-start(f32[8192]{0:T(1024)} %get-tuple-element.9) | copy-start | bytes 98308
  218.9 43.4 %copy-start.12 = (f32[8192]{0:T(1024)S(1)}, f32[8192]{0:T(1024)}, u32[]{:S(2)}) copy-start(f32[8192]{0:T(1024)} %get-tuple-element.7) | copy-start | bytes 98308
  218.9 44.5 %copy-start = (f32[512,1]{1,0:T(8,128)S(1)}, f32[512,1]{1,0:T(8,128)}, u32[]{:S(2)}) copy-start(f32[512,1]{1,0:T(8,128)} %broadcast_7_b_ref_w_ref.2.b_ref.w_ref) | copy-start | bytes 6148
  218.9 44.5 %copy-start.1 = (f32[512,1]{1,0:T(8,128)S(1)}, f32[512,1]{1,0:T(8,128)}, u32[]{:S(2)}) copy-start(f32[512,1]{1,0:T(8,128)} %copy.40.w_ref) | copy-start | bytes 6148
  218.9 44.4 %copy-start.2 = (f32[512,1]{1,0:T(8,128)S(1)}, f32[512,1]{1,0:T(8,128)}, u32[]{:S(2)}) copy-start(f32[512,1]{1,0:T(8,128)} %copy.37.b_ref) | copy-start | bytes 6148
  218.9 44.4 %copy-start.3 = (f32[512,1]{1,0:T(8,128)S(1)}, f32[512,1]{1,0:T(8,128)}, u32[]{:S(2)}) copy-start(f32[512,1]{1,0:T(8,128)} %copy.38.b_ref) | copy-start | bytes 6148
  219.0 44.4 %copy-start.4 = (f32[512,1]{1,0:T(8,128)S(1)}, f32[512,1]{1,0:T(8,128)}, u32[]{:S(2)}) copy-start(f32[512,1]{1,0:T(8,128)} %copy.43.w_ref) | copy-start | bytes 6148
  238.1 25.3 %copy-start.5 = (f32[512,1]{1,0:T(8,128)S(1)}, f32[512,1]{1,0:T(8,128)}, u32[]{:S(2)}) copy-start(f32[512,1]{1,0:T(8,128)} %copy.46.w_ref) | copy-start | bytes 6148
Sparse Core Ops, SparseCore 0:
  304.7 85.0 reduce-scatter.1

commit v9 on v8

--- a/solution.py
+++ b/solution.py
@@ -248,7 +248,7 @@
     return out.reshape(c)
 
 
-def _final_kernel(inv_root, img_ref, cap_ref, rows_ref, cols_ref, ig_ref, cg_ref):
+def _final_kernel(inv_root, img_ref, cap_ref, rows_ref, cols_ref, ia_ref, ib_ref, cg_ref):
     step = pl.program_id(0)
     s = _scores_t(img_ref, cap_ref, inv_root)
     rows = rows_ref[...]
@@ -267,9 +267,12 @@
         row_plan = jnp.exp((g_prev + s) * INV_EPS - (logw_r - f * INV_EPS))
         adjoint = adjoint - row_plan * fb
     rounded = adjoint.astype(jnp.bfloat16)
-    ig_ref[...] = lax.dot_general(
+    ig = lax.dot_general(
         rounded, cap_ref[...], (((0,), (0,)), ((), ())), preferred_element_type=jnp.float32
     ) * inv_root
+    ig = ig.reshape(ia_ref.shape[0], 2, ia_ref.shape[1], ia_ref.shape[2])
+    ia_ref[...] = ig[:, 0]
+    ib_ref[...] = ig[:, 1]
 
     @pl.when(step == 0)
     def _():
@@ -278,14 +281,17 @@
     cg_ref[...] += jnp.dot(rounded, img_ref[...], preferred_element_type=jnp.float32) * inv_root
 
 
-def final_pass(images, captions, rows, cols):
+def final_pass(images, captions, rows, cols, owners):
     n, e = images.shape
     c = captions.shape[0]
     inv_root = 1.0 / math.sqrt(e)
+    half = n // owners // 2
+    per_tile = TM // (2 * half)
     return pl.pallas_call(
         functools.partial(_final_kernel, inv_root),
         out_shape=(
-            jax.ShapeDtypeStruct((n, e), jnp.float32),
+            jax.ShapeDtypeStruct((owners, half, e), jnp.float32),
+            jax.ShapeDtypeStruct((owners, half, e), jnp.float32),
             jax.ShapeDtypeStruct((c, e), jnp.float32),
         ),
         grid=(n // TM,),
@@ -296,7 +302,8 @@
             pl.BlockSpec((c, 8), lambda i: (0, 0)),
         ],
         out_specs=(
-            pl.BlockSpec((TM, e), lambda i: (i, 0)),
+            pl.BlockSpec((per_tile, half, e), lambda i: (i, 0, 0)),
+            pl.BlockSpec((per_tile, half, e), lambda i: (i, 0, 0)),
             pl.BlockSpec((c, e), lambda i: (0, 0)),
         ),
         cost_estimate=pl.CostEstimate(
@@ -335,8 +342,11 @@
             col_bar = -gathered_sum(part, "img")
     rows = jnp.stack(row_hist + row_bars + [image_logw, zeros_r], axis=0)
     cols = jnp.stack(col_hist + col_bars + [caption_logw], axis=1)
-    ig_part, cg_part = final_pass(images, captions, rows, cols)
-    image_grad = lax.psum_scatter(ig_part, "cap", scatter_dimension=0, tiled=True)
+    owners = lax.axis_size("cap")
+    ig_a, ig_b, cg_part = final_pass(images, captions, rows, cols, owners)
+    got_a = lax.psum_scatter(ig_a.reshape(-1, ig_a.shape[2]), "cap", scatter_dimension=0, tiled=True)
+    got_b = scatter_sum(ig_b.reshape(-1, ig_b.shape[2]), "cap", 5)
+    image_grad = jnp.concatenate([got_a, got_b], axis=0)
     caption_grad = scatter_sum(cg_part, "img", 4)
     return (image_grad, caption_grad)
 

time: 401 us -> 451 us (1.12)
  Pallas kernels: 277 us -> 359 us
  waiting for transfers between devices: 74 us -> 42.1 us
    pallas_call x1 -> x2, Pallas kernels: 11.2 us -> 92.8 us  [scatter_sum(): pl.pallas_call(functools.partial(_scatter_kernel, axis, n), out_shape=jax...]
    reduce_scatter x1, waiting for transfers between devices: 74 us -> 42 us  [body(): lax.psum_scatter(ig_a.reshape(-1, ig_a.shape[2]), 'cap', scatter_dimensio...]
  transfers between devices with their start and end apart: 1 -> 1, of which waited for: 1 -> 1; matrix products, arithmetic and copies ran while one was open for 0% -> 0% of each run, Pallas kernels for 3% -> 21%
where the time goes in v9:
time: 451 us; the launch traced here: 448 us
  Pallas kernels  359 us (80%)
  waiting for transfers between devices  42.1 us (9%)
  other arithmetic  21.3 us (5%)
  between operations  14.3 us (3%)
  local copies, waits for them, and re-layouts  11.8 us (3%)
    pallas_call x11, Pallas kernels, combine(): pl.pallas_call(functools.partial(_combine_kernel, axis, n, mode), out_sha...  119 us
    pallas_call x2, Pallas kernels, scatter_sum(): pl.pallas_call(functools.partial(_scatter_kernel, axis, n), out_shape=jax...  92.8 us
    pallas_call x6, Pallas kernels, row_pass(): pl.pallas_call(functools.partial(_row_kernel, mode, inv_root), out_shape=...  57.1 us
    pallas_call x5, Pallas kernels, col_pass(): pl.pallas_call(functools.partial(_col_kernel, mode, inv_root), out_shape=...  49.8 us
    reduce_scatter x1, waiting for transfers between devices, body(): lax.psum_scatter(ig_a.reshape(-1, ig_a.shape[2]), 'cap', scatter_dimensio...  42 us
    pallas_call x1, Pallas kernels, final_pass(): pl.pallas_call(functools.partial(_final_kernel, inv_root), out_shape=(jax...  39.7 us
  transfers between devices with their start and end apart: 1, of which 1 were waited for; matrix products, arithmetic and copies ran while one was open for 0% of the time, Pallas kernels for 21%

profile of v9, /device:TPU:0, one launch (start us, length us, event | category | flops | bytes accessed | tf_op | source)
XLA Modules:
  0.0 448.2 jit_solution(15889720444271931774)
XLA Ops:
  8.6 10.0 %shard_map.77 = f32[1,8192]{1,0:T(1,128)} custom-call(bf16[8192,256]{1,0:T(8,128)(2,1)} %img_ref.23, bf16[512,256]{1,0:T(8,128)(2,1)} %cap_ref.23, f32[1,8192]{1,0:T(1,128)} %broadcast_6_a_ref_w_ref.2.a_ref.w_ref, f32[512,1]{1,0:T(8,128)} %broadcast_7_b_ref_w_ref.2.b_ref.w_ref, f32[512,1]{1,0:T(8,128)} %broadcast_7_b_ref_w_ref.2.b_ref.w_ref), custom_call_target="tpu_custom_call" | custom-call | flops 2147483648 | bytes 4456448 | tf_op jit(solution)/shard_map/pallas_call | solution.py:175
  18.6 14.9 %shard_map.78 = f32[64,128]{1,0:T(8,128)} custom-call(f32[64,128]{1,0:T(8,128)} %bitcast.77), custom_call_target="tpu_custom_call" | custom-call | tf_op jit(solution)/shard_map/pallas_call | solution.py:60
  33.5 0.9 copy.40.w_ref
  34.4 1.4 bitcast_subtract_fusion.2
  35.8 10.4 %shard_map.79 = f32[512,1]{1,0:T(8,128)} custom-call(bf16[8192,256]{1,0:T(8,128)(2,1)} %img_ref.23, bf16[512,256]{1,0:T(8,128)(2,1)} %cap_ref.23, f32[1,8192]{1,0:T(1,128)} %bitcast.59, f32[512,1]{1,0:T(8,128)} %broadcast_7_b_ref_w_ref.2.b_ref.w_ref, f32[1,8192]{1,0:T(1,128)} %broadcast_6_a_ref_w_ref.2.a_ref.w_ref), custom_call_target="tpu_custom_call" | custom-call | flops 2147483648 | bytes 4456448 | tf_op jit(solution)/shard_map/pallas_call | solution.py:237
  46.1 1.7 reduce
  47.8 8.5 %shard_map.80 = f32[4,128]{1,0:T(4,128)} custom-call(f32[4,128]{1,0:T(4,128)} %bitcast.83), custom_call_target="tpu_custom_call" | custom-call | tf_op jit(solution)/shard_map/pallas_call | solution.py:60
  57.0 0.9 copy.37.b_ref
  57.9 9.9 %shard_map.81 = f32[1,8192]{1,0:T(1,128)} custom-call(bf16[8192,256]{1,0:T(8,128)(2,1)} %img_ref.23, bf16[512,256]{1,0:T(8,128)(2,1)} %cap_ref.23, f32[1,8192]{1,0:T(1,128)} %broadcast_6_a_ref_w_ref.2.a_ref.w_ref, f32[512,1]{1,0:T(8,128)} %copy.37.b_ref, f32[512,1]{1,0:T(8,128)} %broadcast_7_b_ref_w_ref.2.b_ref.w_ref), custom_call_target="tpu_custom_call" | custom-call | flops 2147483648 | bytes 4456448 | tf_op jit(solution)/shard_map/pallas_call | solution.py:175
  67.8 13.9 %shard_map.82 = f32[64,128]{1,0:T(8,128)} custom-call(f32[64,128]{1,0:T(8,128)} %bitcast.78), custom_call_target="tpu_custom_call" | custom-call | tf_op jit(solution)/shard_map/pallas_call | solution.py:60
  81.7 1.4 multiply_subtract_fusion.1
  83.1 0.9 copy.45.b_ref
  84.0 10.4 %shard_map.83 = f32[512,1]{1,0:T(8,128)} custom-call(bf16[8192,256]{1,0:T(8,128)(2,1)} %img_ref.23, bf16[512,256]{1,0:T(8,128)(2,1)} %cap_ref.23, f32[1,8192]{1,0:T(1,128)} %bitcast.67, f32[512,1]{1,0:T(8,128)} %broadcast_7_b_ref_w_ref.2.b_ref.w_ref, f32[1,8192]{1,0:T(1,128)} %broadcast_6_a_ref_w_ref.2.a_ref.w_ref), custom_call_target="tpu_custom_call" | custom-call | flops 2147483648 | bytes 4456448 | tf_op jit(solution)/shard_map/pallas_call | solution.py:237
  94.3 1.6 reduce.1
  96.0 6.5 %shard_map.84 = f32[4,128]{1,0:T(4,128)} custom-call(f32[4,128]{1,0:T(4,128)} %bitcast.84), custom_call_target="tpu_custom_call" | custom-call | tf_op jit(solution)/shard_map/pallas_call | solution.py:60
  103.2 0.9 copy.38.b_ref
  104.1 9.9 %shard_map.85 = f32[1,8192]{1,0:T(1,128)} custom-call(bf16[8192,256]{1,0:T(8,128)(2,1)} %img_ref.23, bf16[512,256]{1,0:T(8,128)(2,1)} %cap_ref.23, f32[1,8192]{1,0:T(1,128)} %broadcast_6_a_ref_w_ref.2.a_ref.w_ref, f32[512,1]{1,0:T(8,128)} %copy.38.b_ref, f32[512,1]{1,0:T(8,128)} %broadcast_7_b_ref_w_ref.2.b_ref.w_ref), custom_call_target="tpu_custom_call" | custom-call | flops 2147483648 | bytes 4456448 | tf_op jit(solution)/shard_map/pallas_call | solution.py:175
  114.0 14.0 %shard_map.86 = f32[64,128]{1,0:T(8,128)} custom-call(f32[64,128]{1,0:T(8,128)} %bitcast.79), custom_call_target="tpu_custom_call" | custom-call | tf_op jit(solution)/shard_map/pallas_call | solution.py:60
  128.0 1.4 multiply_subtract_fusion
  129.4 0.9 copy.42.b_ref
  130.3 10.4 %shard_map.87 = f32[512,1]{1,0:T(8,128)} custom-call(bf16[8192,256]{1,0:T(8,128)(2,1)} %img_ref.23, bf16[512,256]{1,0:T(8,128)(2,1)} %cap_ref.23, f32[1,8192]{1,0:T(1,128)} %bitcast.70, f32[512,1]{1,0:T(8,128)} %broadcast_7_b_ref_w_ref.2.b_ref.w_ref, f32[1,8192]{1,0:T(1,128)} %broadcast_6_a_ref_w_ref.2.a_ref.w_ref), custom_call_target="tpu_custom_call" | custom-call | flops 2147483648 | bytes 4456448 | tf_op jit(solution)/shard_map/pallas_call | solution.py:237
  140.7 1.7 reduce.2
  142.3 6.6 %shard_map.88 = f32[4,128]{1,0:T(4,128)} custom-call(f32[4,128]{1,0:T(4,128)} %bitcast.85), custom_call_target="tpu_custom_call" | custom-call | tf_op jit(solution)/shard_map/pallas_call | solution.py:60
  149.6 0.9 copy.39.b_ref
  150.5 9.0 %shard_map.89 = f32[1,8192]{1,0:T(1,128)} custom-call(bf16[8192,256]{1,0:T(8,128)(2,1)} %img_ref.23, bf16[512,256]{1,0:T(8,128)(2,1)} %cap_ref.23, f32[1,8192]{1,0:T(1,128)} %bitcast.71, f32[512,1]{1,0:T(8,128)} %copy.39.b_ref, f32[512,1]{1,0:T(8,128)} %copy.40.w_ref), custom_call_target="tpu_custom_call" | custom-call | flops 2147483648 | bytes 4456448 | tf_op jit(solution)/shard_map/pallas_call | solution.py:175
  159.5 13.9 %shard_map.90 = f32[64,128]{1,0:T(8,128)} custom-call(f32[64,128]{1,0:T(8,128)} %bitcast.74), custom_call_target="tpu_custom_call" | custom-call | tf_op jit(solution)/shard_map/pallas_call | solution.py:60
  173.4 1.4 bitcast_add_fusion
  174.8 9.4 %shard_map.91 = f32[512,1]{1,0:T(8,128)} custom-call(bf16[8192,256]{1,0:T(8,128)(2,1)} %img_ref.23, bf16[512,256]{1,0:T(8,128)(2,1)} %cap_ref.23, f32[1,8192]{1,0:T(1,128)} %bitcast.81, f32[512,1]{1,0:T(8,128)} %copy.38.b_ref, f32[1,8192]{1,0:T(1,128)} %bitcast.62), custom_call_target="tpu_custom_call" | custom-call | flops 2147483648 | bytes 4456448 | tf_op jit(solution)/shard_map/pallas_call | solution.py:237
  184.2 1.7 reduce.3
  185.8 6.5 %shard_map.92 = f32[4,128]{1,0:T(4,128)} custom-call(f32[4,128]{1,0:T(4,128)} %bitcast.86), custom_call_target="tpu_custom_call" | custom-call | tf_op jit(solution)/shard_map/pallas_call | solution.py:60
  193.0 0.9 copy.43.w_ref
  193.9 9.0 %shard_map.93 = f32[1,8192]{1,0:T(1,128)} custom-call(bf16[8192,256]{1,0:T(8,128)(2,1)} %img_ref.23, bf16[512,256]{1,0:T(8,128)(2,1)} %cap_ref.23, f32[1,8192]{1,0:T(1,128)} %bitcast.68, f32[512,1]{1,0:T(8,128)} %copy.42.b_ref, f32[512,1]{1,0:T(8,128)} %copy.43.w_ref), custom_call_target="tpu_custom_call" | custom-call | flops 2147483648 | bytes 4456448 | tf_op jit(solution)/shard_map/pallas_call | solution.py:175
  202.9 13.9 %shard_map.94 = f32[64,128]{1,0:T(8,128)} custom-call(f32[64,128]{1,0:T(8,128)} %bitcast.75), custom_call_target="tpu_custom_call" | custom-call | tf_op jit(solution)/shard_map/pallas_call | solution.py:60
  216.8 1.4 neg.62
  218.2 9.3 %shard_map.95 = f32[512,1]{1,0:T(8,128)} custom-call(bf16[8192,256]{1,0:T(8,128)(2,1)} %img_ref.23, bf16[512,256]{1,0:T(8,128)(2,1)} %cap_ref.23, f32[1,8192]{1,0:T(1,128)} %bitcast.80, f32[512,1]{1,0:T(8,128)} %copy.37.b_ref, f32[1,8192]{1,0:T(1,128)} %bitcast.64), custom_call_target="tpu_custom_call" | custom-call | flops 2147483648 | bytes 4456448 | tf_op jit(solution)/shard_map/pallas_call | solution.py:237
  227.6 1.7 reduce.4
  229.3 6.6 %shard_map.96 = f32[4,128]{1,0:T(4,128)} custom-call(f32[4,128]{1,0:T(4,128)} %bitcast.82), custom_call_target="tpu_custom_call" | custom-call | tf_op jit(solution)/shard_map/pallas_call | solution.py:60
  236.5 0.9 copy.46.w_ref
  237.5 9.2 %shard_map.97 = f32[1,8192]{1,0:T(1,128)} custom-call(bf16[8192,256]{1,0:T(8,128)(2,1)} %img_ref.23, bf16[512,256]{1,0:T(8,128)(2,1)} %cap_ref.23, f32[1,8192]{1,0:T(1,128)} %bitcast.60, f32[512,1]{1,0:T(8,128)} %copy.45.b_ref, f32[512,1]{1,0:T(8,128)} %copy.46.w_ref), custom_call_target="tpu_custom_call" | custom-call | flops 2147483648 | bytes 4456448 | tf_op jit(solution)/shard_map/pallas_call | solution.py:175
  246.7 13.9 %shard_map.98 = f32[64,128]{1,0:T(8,128)} custom-call(f32[64,128]{1,0:T(8,128)} %bitcast.76), custom_call_target="tpu_custom_call" | custom-call | tf_op jit(solution)/shard_map/pallas_call | solution.py:60
  260.6 0.8 neg.66
  261.7 1.1 stack.36.rows_ref
  262.8 1.4 stack.39.cols_ref
  264.3 39.7 %shard_map.99 = (f32[16,256,256]{2,1,0:T(8,128)}, f32[16,256,256]{2,1,0:T(8,128)}, f32[512,256]{1,0:T(8,128)}) custom-call(bf16[8192,256]{1,0:T(8,128)(2,1)} %img_ref.23, bf16[512,256]{1,0:T(8,128)(2,1)} %cap_ref.23, f32[8,8192]{1,0:T(8,128)} %stack.36.rows_ref, f32[512,8]{1,0:T(8,128)} %stack.39.cols_ref), custom_call_target="tpu_custom_call" | custom-call | flops 6442450944 | bytes 13369344 | tf_op jit(solution)/shard_map/pallas_call | solution.py:290
  304.0 11.2 %shard_map.101 = f32[64,256]{1,0:T(8,128)} custom-call(f32[8,64,256]{2,1,0:T(8,128)} %bitcast.57), custom_call_target="tpu_custom_call" | custom-call | tf_op jit(solution)/shard_map/pallas_call | solution.py:112
  315.2 81.6 %shard_map.100 = f32[256,256]{1,0:T(8,128)} custom-call(f32[16,256,256]{2,1,0:T(8,128)} %get-tuple-element.6.x_ref), custom_call_target="tpu_custom_call" | custom-call | tf_op jit(solution)/shard_map/pallas_call | solution.py:112
  396.8 42.0 %reduce-scatter.2.cloned.1.call-done = f32[256,256]{1,0:T(8,128)} async-done(((f32[4096,256]{1,0:T(8,128)}), f32[256,256]{1,0:T(8,128)}) %reduce-scatter.2.cloned.1.call-update) | async-done | bytes 262160 | tf_op jit(solution)/shard_map/reduce_scatter | solution.py:347
  438.8 1.9 pad_maximum_fusion
  (46 shorter events, 5.8 us)
Async XLA Ops:
  7.2 26.3 %copy-start.16 = (f32[512]{0:T(512)S(1)}, f32[512]{0:T(512)}, u32[]{:S(2)}) copy-start(f32[512]{0:T(512)} %param.11) | copy-start | bytes 6148
  7.2 431.7 %reduce-scatter.2.cloned.1.call-start = ((), (), s32[]{:S(2)}) async-start(), calls=%async_computation.1 | async-start | bytes 4456448 | tf_op jit(solution)/shard_map/reduce_scatter | solution.py:347
  8.6 25.8 %copy-start.6 = (f32[8192]{0:T(1024)S(1)}, f32[8192]{0:T(1024)}, u32[]{:S(2)}) copy-start(f32[8192]{0:T(1024)} %param.8) | copy-start | bytes 98308
  34.4 22.0 %copy-start.14 = (f32[512]{0:T(512)S(1)}, f32[512]{0:T(512)}, u32[]{:S(2)}) copy-start(f32[512]{0:T(512)} %param.9) | copy-start | bytes 6148
  142.3 31.1 %copy-start.15 = (f32[8192]{0:T(1024)S(1)}, f32[8192]{0:T(1024)}, u32[]{:S(2)}) copy-start(f32[8192]{0:T(1024)} %param.10) | copy-start | bytes 98308
  237.4 24.3 %copy-start.8 = (f32[8192]{0:T(1024)S(1)}, f32[8192]{0:T(1024)}, u32[]{:S(2)}) copy-start(f32[8192]{0:T(1024)} %bitcast_subtract_fusion.2) | copy-start | bytes 98308
  237.4 24.3 %copy-start.9 = (f32[8192]{0:T(1024)S(1)}, f32[8192]{0:T(1024)}, u32[]{:S(2)}) copy-start(f32[8192]{0:T(1024)} %bitcast_add_fusion) | copy-start | bytes 98308
  237.4 24.3 %copy-start.10 = (f32[1,8192]{1,0:T(1,128)S(1)}, f32[1,8192]{1,0:T(1,128)}, u32[]{:S(2)}) copy-start(f32[1,8192]{1,0:T(1,128)} %broadcast_6_a_ref_w_ref.2.a_ref.w_ref) | copy-start | bytes 98308
  237.4 24.3 %copy-start.11 = (f32[64,128]{1,0:T(8,128)S(1)}, f32[64,128]{1,0:T(8,128)}, u32[]{:S(2)}) copy-start(f32[64,128]{1,0:T(8,128)} %neg.62) | copy-start | bytes 98308
  237.4 24.3 %copy-start.12 = (f32[8192]{0:T(1024)S(1)}, f32[8192]{0:T(1024)}, u32[]{:S(2)}) copy-start(f32[8192]{0:T(1024)} %get-tuple-element.11) | copy-start | bytes 98308
  237.4 24.3 %copy-start.13 = (f32[8192]{0:T(1024)S(1)}, f32[8192]{0:T(1024)}, u32[]{:S(2)}) copy-start(f32[8192]{0:T(1024)} %get-tuple-element.9) | copy-start | bytes 98308
  237.4 25.4 %copy-start = (f32[512,1]{1,0:T(8,128)S(1)}, f32[512,1]{1,0:T(8,128)}, u32[]{:S(2)}) copy-start(f32[512,1]{1,0:T(8,128)} %broadcast_7_b_ref_w_ref.2.b_ref.w_ref) | copy-start | bytes 6148
  237.4 25.4 %copy-start.1 = (f32[512,1]{1,0:T(8,128)S(1)}, f32[512,1]{1,0:T(8,128)}, u32[]{:S(2)}) copy-start(f32[512,1]{1,0:T(8,128)} %copy.40.w_ref) | copy-start | bytes 6148
  237.4 25.4 %copy-start.2 = (f32[512,1]{1,0:T(8,128)S(1)}, f32[512,1]{1,0:T(8,128)}, u32[]{:S(2)}) copy-start(f32[512,1]{1,0:T(8,128)} %copy.37.b_ref) | copy-start | bytes 6148
  237.5 25.4 %copy-start.3 = (f32[512,1]{1,0:T(8,128)S(1)}, f32[512,1]{1,0:T(8,128)}, u32[]{:S(2)}) copy-start(f32[512,1]{1,0:T(8,128)} %copy.38.b_ref) | copy-start | bytes 6148
  237.5 25.3 %copy-start.4 = (f32[512,1]{1,0:T(8,128)S(1)}, f32[512,1]{1,0:T(8,128)}, u32[]{:S(2)}) copy-start(f32[512,1]{1,0:T(8,128)} %copy.43.w_ref) | copy-start | bytes 6148
  237.5 25.3 %copy-start.5 = (f32[512,1]{1,0:T(8,128)S(1)}, f32[512,1]{1,0:T(8,128)}, u32[]{:S(2)}) copy-start(f32[512,1]{1,0:T(8,128)} %copy.46.w_ref) | copy-start | bytes 6148
  315.2 125.5 %copy-start.7 = (f32[64,256]{1,0:T(8,128)S(1)}, f32[64,256]{1,0:T(8,128)}, u32[]{:S(2)}) copy-start(f32[64,256]{1,0:T(8,128)} %shard_map.101) | copy-start | bytes 196612
Sparse Core Ops, SparseCore 0:
  304.1 134.6 reduce-scatter.1

commit v10 on v8

--- a/solution.py
+++ b/solution.py
@@ -135,6 +135,7 @@
 
 
 TM = 1024
+TM_PASS = 2048
 INV_EPS = 1.0 / SMOOTHING
 
 
@@ -161,9 +162,9 @@
 
 def _specs(n, c, e):
     return [
-        pl.BlockSpec((TM, e), lambda i: (i, 0)),
+        pl.BlockSpec((TM_PASS, e), lambda i: (i, 0)),
         pl.BlockSpec((c, e), lambda i: (0, 0)),
-        pl.BlockSpec((1, TM), lambda i: (0, i)),
+        pl.BlockSpec((1, TM_PASS), lambda i: (0, i)),
         pl.BlockSpec((c, 1), lambda i: (0, 0)),
     ]
 
@@ -175,9 +176,9 @@
     out = pl.pallas_call(
         functools.partial(_row_kernel, mode, inv_root),
         out_shape=jax.ShapeDtypeStruct((1, n), jnp.float32),
-        grid=(n // TM,),
+        grid=(n // TM_PASS,),
         in_specs=_specs(n, c, e) + [pl.BlockSpec((c, 1), lambda i: (0, 0))],
-        out_specs=pl.BlockSpec((1, TM), lambda i: (0, i)),
+        out_specs=pl.BlockSpec((1, TM_PASS), lambda i: (0, i)),
         cost_estimate=pl.CostEstimate(
             flops=2 * n * c * e, transcendentals=n * c, bytes_accessed=n * e * 2 + c * e * 2
         ),
@@ -237,8 +238,8 @@
     out = pl.pallas_call(
         functools.partial(_col_kernel, mode, inv_root),
         out_shape=jax.ShapeDtypeStruct((c, 1), jnp.float32),
-        grid=(n // TM,),
-        in_specs=_specs(n, c, e) + [pl.BlockSpec((1, TM), lambda i: (0, i))],
+        grid=(n // TM_PASS,),
+        in_specs=_specs(n, c, e) + [pl.BlockSpec((1, TM_PASS), lambda i: (0, i))],
         out_specs=pl.BlockSpec((c, 1), lambda i: (0, 0)),
         scratch_shapes=[pltpu.VMEM((c, 128), jnp.float32), pltpu.VMEM((c, 128), jnp.float32)],
         cost_estimate=pl.CostEstimate(

time: 401 us -> 387 us (0.965)
  Pallas kernels: 277 us -> 264 us
    pallas_call x6, Pallas kernels: 57 us -> 49.8 us  [row_pass(): pl.pallas_call(functools.partial(_row_kernel, mode, inv_root), out_shape=...]
    pallas_call x5, Pallas kernels: 49.9 us -> 44.5 us  [col_pass(): pl.pallas_call(functools.partial(_col_kernel, mode, inv_root), out_shape=...]
where the time goes in v10:
time: 387 us; the launch traced here: 385 us
  Pallas kernels  264 us (68%)
  waiting for transfers between devices  73.9 us (19%)
  other arithmetic  19.5 us (5%)
  between operations  14.3 us (4%)
  local copies, waits for them, and re-layouts  13.3 us (3%)
    pallas_call x11, Pallas kernels, combine(): pl.pallas_call(functools.partial(_combine_kernel, axis, n, mode), out_sha...  119 us
    reduce_scatter x1, waiting for transfers between devices, body(): lax.psum_scatter(ig_part, 'cap', scatter_dimension=0, tiled=True)  73.9 us
    pallas_call x6, Pallas kernels, row_pass(): pl.pallas_call(functools.partial(_row_kernel, mode, inv_root), out_shape=...  49.8 us
    pallas_call x5, Pallas kernels, col_pass(): pl.pallas_call(functools.partial(_col_kernel, mode, inv_root), out_shape=...  44.5 us
    pallas_call x1, Pallas kernels, final_pass(): pl.pallas_call(functools.partial(_final_kernel, inv_root), out_shape=(jax...  39.7 us
    pallas_call x1, Pallas kernels, scatter_sum(): pl.pallas_call(functools.partial(_scatter_kernel, axis, n), out_shape=jax...  11.2 us
    pallas_call x5, other arithmetic, col_pass(): pl.pallas_call(functools.partial(_col_kernel, mode, inv_root), out_shape=...  8.38 us
  transfers between devices with their start and end apart: 1, of which 1 were waited for; matrix products, arithmetic and copies ran while one was open for 0% of the time, Pallas kernels for 3%

profile of v10, /device:TPU:0, one launch (start us, length us, event | category | flops | bytes accessed | tf_op | source)
XLA Modules:
  0.0 385.4 jit_solution(3752336142481871729)
XLA Ops:
  7.9 0.7 broadcast_7_b_ref_w_ref.2.b_ref.w_ref
  8.6 9.0 %shard_map.77 = f32[1,8192]{1,0:T(1,128)} custom-call(bf16[8192,256]{1,0:T(8,128)(2,1)} %img_ref.23, bf16[512,256]{1,0:T(8,128)(2,1)} %cap_ref.23, f32[1,8192]{1,0:T(1,128)} %broadcast_6_a_ref_w_ref.2.a_ref.w_ref, f32[512,1]{1,0:T(8,128)} %broadcast_7_b_ref_w_ref.2.b_ref.w_ref, f32[512,1]{1,0:T(8,128)} %broadcast_7_b_ref_w_ref.2.b_ref.w_ref), custom_call_target="tpu_custom_call" | custom-call | flops 2147483648 | bytes 4456448 | tf_op jit(solution)/shard_map/pallas_call | solution.py:176
  17.6 14.9 %shard_map.78 = f32[64,128]{1,0:T(8,128)} custom-call(f32[64,128]{1,0:T(8,128)} %bitcast.75), custom_call_target="tpu_custom_call" | custom-call | tf_op jit(solution)/shard_map/pallas_call | solution.py:60
  32.5 1.5 copy.40.w_ref
  34.0 1.4 bitcast_subtract_fusion.2
  35.4 9.4 %shard_map.79 = f32[512,1]{1,0:T(8,128)} custom-call(bf16[8192,256]{1,0:T(8,128)(2,1)} %img_ref.23, bf16[512,256]{1,0:T(8,128)(2,1)} %cap_ref.23, f32[1,8192]{1,0:T(1,128)} %bitcast.57, f32[512,1]{1,0:T(8,128)} %broadcast_7_b_ref_w_ref.2.b_ref.w_ref, f32[1,8192]{1,0:T(1,128)} %broadcast_6_a_ref_w_ref.2.a_ref.w_ref), custom_call_target="tpu_custom_call" | custom-call | flops 2147483648 | bytes 4456448 | tf_op jit(solution)/shard_map/pallas_call | solution.py:238
  44.8 1.7 reduce
  46.5 8.6 %shard_map.80 = f32[4,128]{1,0:T(4,128)} custom-call(f32[4,128]{1,0:T(4,128)} %bitcast.81), custom_call_target="tpu_custom_call" | custom-call | tf_op jit(solution)/shard_map/pallas_call | solution.py:60
  55.7 0.9 copy.37.b_ref
  56.6 8.8 %shard_map.81 = f32[1,8192]{1,0:T(1,128)} custom-call(bf16[8192,256]{1,0:T(8,128)(2,1)} %img_ref.23, bf16[512,256]{1,0:T(8,128)(2,1)} %cap_ref.23, f32[1,8192]{1,0:T(1,128)} %broadcast_6_a_ref_w_ref.2.a_ref.w_ref, f32[512,1]{1,0:T(8,128)} %copy.37.b_ref, f32[512,1]{1,0:T(8,128)} %broadcast_7_b_ref_w_ref.2.b_ref.w_ref), custom_call_target="tpu_custom_call" | custom-call | flops 2147483648 | bytes 4456448 | tf_op jit(solution)/shard_map/pallas_call | solution.py:176
  65.4 13.9 %shard_map.82 = f32[64,128]{1,0:T(8,128)} custom-call(f32[64,128]{1,0:T(8,128)} %bitcast.76), custom_call_target="tpu_custom_call" | custom-call | tf_op jit(solution)/shard_map/pallas_call | solution.py:60
  79.3 1.4 multiply_subtract_fusion.1
  80.7 0.9 copy.45.b_ref
  81.6 9.4 %shard_map.83 = f32[512,1]{1,0:T(8,128)} custom-call(bf16[8192,256]{1,0:T(8,128)(2,1)} %img_ref.23, bf16[512,256]{1,0:T(8,128)(2,1)} %cap_ref.23, f32[1,8192]{1,0:T(1,128)} %bitcast.65, f32[512,1]{1,0:T(8,128)} %broadcast_7_b_ref_w_ref.2.b_ref.w_ref, f32[1,8192]{1,0:T(1,128)} %broadcast_6_a_ref_w_ref.2.a_ref.w_ref), custom_call_target="tpu_custom_call" | custom-call | flops 2147483648 | bytes 4456448 | tf_op jit(solution)/shard_map/pallas_call | solution.py:238
  91.0 1.7 reduce.1
  92.6 6.6 %shard_map.84 = f32[4,128]{1,0:T(4,128)} custom-call(f32[4,128]{1,0:T(4,128)} %bitcast.82), custom_call_target="tpu_custom_call" | custom-call | tf_op jit(solution)/shard_map/pallas_call | solution.py:60
  99.9 0.9 copy.38.b_ref
  100.7 8.8 %shard_map.85 = f32[1,8192]{1,0:T(1,128)} custom-call(bf16[8192,256]{1,0:T(8,128)(2,1)} %img_ref.23, bf16[512,256]{1,0:T(8,128)(2,1)} %cap_ref.23, f32[1,8192]{1,0:T(1,128)} %broadcast_6_a_ref_w_ref.2.a_ref.w_ref, f32[512,1]{1,0:T(8,128)} %copy.38.b_ref, f32[512,1]{1,0:T(8,128)} %broadcast_7_b_ref_w_ref.2.b_ref.w_ref), custom_call_target="tpu_custom_call" | custom-call | flops 2147483648 | bytes 4456448 | tf_op jit(solution)/shard_map/pallas_call | solution.py:176
  109.5 14.0 %shard_map.86 = f32[64,128]{1,0:T(8,128)} custom-call(f32[64,128]{1,0:T(8,128)} %bitcast.77), custom_call_target="tpu_custom_call" | custom-call | tf_op jit(solution)/shard_map/pallas_call | solution.py:60
  123.5 1.4 multiply_subtract_fusion
  124.9 0.9 copy.42.b_ref
  125.8 9.4 %shard_map.87 = f32[512,1]{1,0:T(8,128)} custom-call(bf16[8192,256]{1,0:T(8,128)(2,1)} %img_ref.23, bf16[512,256]{1,0:T(8,128)(2,1)} %cap_ref.23, f32[1,8192]{1,0:T(1,128)} %bitcast.68, f32[512,1]{1,0:T(8,128)} %broadcast_7_b_ref_w_ref.2.b_ref.w_ref, f32[1,8192]{1,0:T(1,128)} %broadcast_6_a_ref_w_ref.2.a_ref.w_ref), custom_call_target="tpu_custom_call" | custom-call | flops 2147483648 | bytes 4456448 | tf_op jit(solution)/shard_map/pallas_call | solution.py:238
  135.2 1.7 reduce.2
  136.9 6.6 %shard_map.88 = f32[4,128]{1,0:T(4,128)} custom-call(f32[4,128]{1,0:T(4,128)} %bitcast.83), custom_call_target="tpu_custom_call" | custom-call | tf_op jit(solution)/shard_map/pallas_call | solution.py:60
  144.2 0.9 copy.39.b_ref
  145.0 7.7 %shard_map.89 = f32[1,8192]{1,0:T(1,128)} custom-call(bf16[8192,256]{1,0:T(8,128)(2,1)} %img_ref.23, bf16[512,256]{1,0:T(8,128)(2,1)} %cap_ref.23, f32[1,8192]{1,0:T(1,128)} %bitcast.69, f32[512,1]{1,0:T(8,128)} %copy.39.b_ref, f32[512,1]{1,0:T(8,128)} %copy.40.w_ref), custom_call_target="tpu_custom_call" | custom-call | flops 2147483648 | bytes 4456448 | tf_op jit(solution)/shard_map/pallas_call | solution.py:176
  152.7 13.9 %shard_map.90 = f32[64,128]{1,0:T(8,128)} custom-call(f32[64,128]{1,0:T(8,128)} %bitcast.72), custom_call_target="tpu_custom_call" | custom-call | tf_op jit(solution)/shard_map/pallas_call | solution.py:60
  166.6 1.4 bitcast_add_fusion
  168.0 8.1 %shard_map.91 = f32[512,1]{1,0:T(8,128)} custom-call(bf16[8192,256]{1,0:T(8,128)(2,1)} %img_ref.23, bf16[512,256]{1,0:T(8,128)(2,1)} %cap_ref.23, f32[1,8192]{1,0:T(1,128)} %bitcast.79, f32[512,1]{1,0:T(8,128)} %copy.38.b_ref, f32[1,8192]{1,0:T(1,128)} %bitcast.60), custom_call_target="tpu_custom_call" | custom-call | flops 2147483648 | bytes 4456448 | tf_op jit(solution)/shard_map/pallas_call | solution.py:238
  176.1 1.7 reduce.3
  177.8 6.5 %shard_map.92 = f32[4,128]{1,0:T(4,128)} custom-call(f32[4,128]{1,0:T(4,128)} %bitcast.84), custom_call_target="tpu_custom_call" | custom-call | tf_op jit(solution)/shard_map/pallas_call | solution.py:60
  185.0 0.9 copy.43.w_ref
  185.9 7.7 %shard_map.93 = f32[1,8192]{1,0:T(1,128)} custom-call(bf16[8192,256]{1,0:T(8,128)(2,1)} %img_ref.23, bf16[512,256]{1,0:T(8,128)(2,1)} %cap_ref.23, f32[1,8192]{1,0:T(1,128)} %bitcast.66, f32[512,1]{1,0:T(8,128)} %copy.42.b_ref, f32[512,1]{1,0:T(8,128)} %copy.43.w_ref), custom_call_target="tpu_custom_call" | custom-call | flops 2147483648 | bytes 4456448 | tf_op jit(solution)/shard_map/pallas_call | solution.py:176
  193.6 13.9 %shard_map.94 = f32[64,128]{1,0:T(8,128)} custom-call(f32[64,128]{1,0:T(8,128)} %bitcast.73), custom_call_target="tpu_custom_call" | custom-call | tf_op jit(solution)/shard_map/pallas_call | solution.py:60
  207.5 1.4 neg.62
  208.9 8.2 %shard_map.95 = f32[512,1]{1,0:T(8,128)} custom-call(bf16[8192,256]{1,0:T(8,128)(2,1)} %img_ref.23, bf16[512,256]{1,0:T(8,128)(2,1)} %cap_ref.23, f32[1,8192]{1,0:T(1,128)} %bitcast.78, f32[512,1]{1,0:T(8,128)} %copy.37.b_ref, f32[1,8192]{1,0:T(1,128)} %bitcast.62), custom_call_target="tpu_custom_call" | custom-call | flops 2147483648 | bytes 4456448 | tf_op jit(solution)/shard_map/pallas_call | solution.py:238
  217.1 1.6 reduce.4
  218.8 6.5 %shard_map.96 = f32[4,128]{1,0:T(4,128)} custom-call(f32[4,128]{1,0:T(4,128)} %bitcast.80), custom_call_target="tpu_custom_call" | custom-call | tf_op jit(solution)/shard_map/pallas_call | solution.py:60
  226.0 0.9 copy.46.w_ref
  226.8 7.8 %shard_map.97 = f32[1,8192]{1,0:T(1,128)} custom-call(bf16[8192,256]{1,0:T(8,128)(2,1)} %img_ref.23, bf16[512,256]{1,0:T(8,128)(2,1)} %cap_ref.23, f32[1,8192]{1,0:T(1,128)} %bitcast.58, f32[512,1]{1,0:T(8,128)} %copy.45.b_ref, f32[512,1]{1,0:T(8,128)} %copy.46.w_ref), custom_call_target="tpu_custom_call" | custom-call | flops 2147483648 | bytes 4456448 | tf_op jit(solution)/shard_map/pallas_call | solution.py:176
  234.6 13.9 %shard_map.98 = f32[64,128]{1,0:T(8,128)} custom-call(f32[64,128]{1,0:T(8,128)} %bitcast.74), custom_call_target="tpu_custom_call" | custom-call | tf_op jit(solution)/shard_map/pallas_call | solution.py:60
  248.5 0.8 neg.66
  249.7 1.1 stack.36.rows_ref
  250.8 1.4 stack.39.cols_ref
  252.2 39.7 %shard_map.99 = (f32[8192,256]{1,0:T(8,128)}, f32[512,256]{1,0:T(8,128)}) custom-call(bf16[8192,256]{1,0:T(8,128)(2,1)} %img_ref.23, bf16[512,256]{1,0:T(8,128)(2,1)} %cap_ref.23, f32[8,8192]{1,0:T(8,128)} %stack.36.rows_ref, f32[512,8]{1,0:T(8,128)} %stack.39.cols_ref), custom_call_target="tpu_custom_call" | custom-call | flops 6442450944 | bytes 13369344 | tf_op jit(solution)/shard_map/pallas_call | solution.py:286
  292.0 11.2 %shard_map.100 = f32[64,256]{1,0:T(8,128)} custom-call(f32[8,64,256]{2,1,0:T(8,128)} %bitcast.55), custom_call_target="tpu_custom_call" | custom-call | tf_op jit(solution)/shard_map/pallas_call | solution.py:112
  303.2 73.9 %reduce-scatter.2.cloned.1.call-done = f32[512,256]{1,0:T(8,128)} async-done(((f32[8192,256]{1,0:T(8,128)}), f32[512,256]{1,0:T(8,128)}) %reduce-scatter.2.cloned.1.call-update) | async-done | bytes 524304 | tf_op jit(solution)/shard_map/reduce_scatter | solution.py:340
  377.0 1.5 copy.55
  (40 shorter events, 4.4 us)
Async XLA Ops:
  7.2 26.8 %copy-start.6 = (f32[8192]{0:T(1024)S(1)}, f32[8192]{0:T(1024)}, u32[]{:S(2)}) copy-start(f32[8192]{0:T(1024)} %param.8) | copy-start | bytes 98308
  7.2 369.9 %reduce-scatter.2.cloned.1.call-start = ((), (), s32[]{:S(2)}) async-start(), calls=%async_computation.1 | async-start | bytes 8912896 | tf_op jit(solution)/shard_map/reduce_scatter | solution.py:340
  7.9 47.2 %copy-start.13 = (f32[512]{0:T(512)S(1)}, f32[512]{0:T(512)}, u32[]{:S(2)}) copy-start(f32[512]{0:T(512)} %param.9) | copy-start | bytes 6148
  124.9 41.7 %copy-start.14 = (f32[8192]{0:T(1024)S(1)}, f32[8192]{0:T(1024)}, u32[]{:S(2)}) copy-start(f32[8192]{0:T(1024)} %param.10) | copy-start | bytes 98308
  208.9 40.7 %copy-start.7 = (f32[8192]{0:T(1024)S(1)}, f32[8192]{0:T(1024)}, u32[]{:S(2)}) copy-start(f32[8192]{0:T(1024)} %bitcast_subtract_fusion.2) | copy-start | bytes 98308
  208.9 40.7 %copy-start.8 = (f32[8192]{0:T(1024)S(1)}, f32[8192]{0:T(1024)}, u32[]{:S(2)}) copy-start(f32[8192]{0:T(1024)} %bitcast_add_fusion) | copy-start | bytes 98308
  208.9 40.8 %copy-start.9 = (f32[1,8192]{1,0:T(1,128)S(1)}, f32[1,8192]{1,0:T(1,128)}, u32[]{:S(2)}) copy-start(f32[1,8192]{1,0:T(1,128)} %broadcast_6_a_ref_w_ref.2.a_ref.w_ref) | copy-start | bytes 98308
  208.9 40.8 %copy-start.10 = (f32[64,128]{1,0:T(8,128)S(1)}, f32[64,128]{1,0:T(8,128)}, u32[]{:S(2)}) copy-start(f32[64,128]{1,0:T(8,128)} %neg.62) | copy-start | bytes 98308
  208.9 40.8 %copy-start.11 = (f32[8192]{0:T(1024)S(1)}, f32[8192]{0:T(1024)}, u32[]{:S(2)}) copy-start(f32[8192]{0:T(1024)} %get-tuple-element.9) | copy-start | bytes 98308
  208.9 40.8 %copy-start.12 = (f32[8192]{0:T(1024)S(1)}, f32[8192]{0:T(1024)}, u32[]{:S(2)}) copy-start(f32[8192]{0:T(1024)} %get-tuple-element.7) | copy-start | bytes 98308
  208.9 41.9 %copy-start = (f32[512,1]{1,0:T(8,128)S(1)}, f32[512,1]{1,0:T(8,128)}, u32[]{:S(2)}) copy-start(f32[512,1]{1,0:T(8,128)} %broadcast_7_b_ref_w_ref.2.b_ref.w_ref) | copy-start | bytes 6148
  208.9 41.9 %copy-start.1 = (f32[512,1]{1,0:T(8,128)S(1)}, f32[512,1]{1,0:T(8,128)}, u32[]{:S(2)}) copy-start(f32[512,1]{1,0:T(8,128)} %copy.40.w_ref) | copy-start | bytes 6148
  208.9 41.9 %copy-start.2 = (f32[512,1]{1,0:T(8,128)S(1)}, f32[512,1]{1,0:T(8,128)}, u32[]{:S(2)}) copy-start(f32[512,1]{1,0:T(8,128)} %copy.37.b_ref) | copy-start | bytes 6148
  208.9 41.8 %copy-start.3 = (f32[512,1]{1,0:T(8,128)S(1)}, f32[512,1]{1,0:T(8,128)}, u32[]{:S(2)}) copy-start(f32[512,1]{1,0:T(8,128)} %copy.38.b_ref) | copy-start | bytes 6148
  208.9 41.8 %copy-start.4 = (f32[512,1]{1,0:T(8,128)S(1)}, f32[512,1]{1,0:T(8,128)}, u32[]{:S(2)}) copy-start(f32[512,1]{1,0:T(8,128)} %copy.43.w_ref) | copy-start | bytes 6148
  226.8 23.9 %copy-start.5 = (f32[512,1]{1,0:T(8,128)S(1)}, f32[512,1]{1,0:T(8,128)}, u32[]{:S(2)}) copy-start(f32[512,1]{1,0:T(8,128)} %copy.46.w_ref) | copy-start | bytes 6148
Sparse Core Ops, SparseCore 0:
  292.1 84.9 reduce-scatter.1

commit v11 on v10

--- a/solution.py
+++ b/solution.py
@@ -18,7 +18,7 @@
     return (lax.rem(me_img + k, n), me_cap)
 
 
-def _combine_kernel(axis, n, mode, x_ref, o_ref, buf, send_sem, recv_sem):
+def _combine_kernel(axis, n, mode, x_ref, add_ref, o_ref, buf, send_sem, recv_sem):
     barrier = pltpu.get_barrier_semaphore()
     for k in range(1, n):
         pl.semaphore_signal(barrier, inc=1, device_id=_peer(axis, k, n), device_id_type=MESH)
@@ -38,7 +38,7 @@
     for copy in copies:
         copy.wait()
     x = x_ref[...]
-    if mode == "sum":
+    if mode != "lse":
         acc = x
         for k in range(1, n):
             acc = acc + buf[k]
@@ -50,17 +50,22 @@
         for k in range(1, n):
             tot = tot + jnp.exp(buf[k] - top)
         acc = top + jnp.log(tot)
-    o_ref[...] = acc
-
-
-def combine(x, axis, n, mode, cid):
+    if mode == "lse":
+        o_ref[...] = SMOOTHING * add_ref[...] - SMOOTHING * acc
+    elif mode == "sum+":
+        o_ref[...] = add_ref[...] + (-acc)
+    else:
+        o_ref[...] = -acc
+
+
+def combine(x, axis, n, mode, cid, addend):
     size = x.shape[0]
     rows = size // 128
     x2 = x.reshape(rows, 128)
     out = pl.pallas_call(
         functools.partial(_combine_kernel, axis, n, mode),
         out_shape=jax.ShapeDtypeStruct((rows, 128), jnp.float32),
-        in_specs=[pl.BlockSpec(memory_space=pltpu.VMEM)],
+        in_specs=[pl.BlockSpec(memory_space=pltpu.VMEM)] * 2,
         out_specs=pl.BlockSpec(memory_space=pltpu.VMEM),
         scratch_shapes=[
             pltpu.VMEM((n, rows, 128), jnp.float32),
@@ -68,7 +73,7 @@
             pltpu.SemaphoreType.DMA((n,)),
         ],
         compiler_params=pltpu.CompilerParams(collective_id=cid, has_side_effects=True),
-    )(x2)
+    )(x2, addend.reshape(rows, 128))
     return out.reshape(size)
 
 from jax.sharding import PartitionSpec as P
@@ -123,15 +128,17 @@
     )(x.reshape(n, rows, lanes))
 
 
-_IDS = {("cap", "lse"): 0, ("img", "lse"): 1, ("cap", "sum"): 2, ("img", "sum"): 3}
-
-
-def gathered_lse(part, axis):
-    return combine(part, axis, lax.axis_size(axis), "lse", _IDS[(axis, "lse")])
-
-
-def gathered_sum(part, axis):
-    return combine(part, axis, lax.axis_size(axis), "sum", _IDS[(axis, "sum")])
+_IDS = {("cap", "lse"): 0, ("img", "lse"): 1, ("cap", "sum"): 2, ("img", "sum"): 3, ("cap", "sum+"): 5}
+
+
+def potential(part, axis, logw):
+    return combine(part, axis, lax.axis_size(axis), "lse", _IDS[(axis, "lse")], logw)
+
+
+def neg_sum(part, axis, addend=None):
+    if addend is None:
+        return combine(part, axis, lax.axis_size(axis), "sum", _IDS[(axis, "sum")], part)
+    return combine(part, axis, lax.axis_size(axis), "sum+", _IDS[(axis, "sum+")], addend)
 
 
 TM = 1024
@@ -315,10 +322,10 @@
     row_hist = []
     for level in range(ITERS):
         part = row_pass("lse", images, captions, zeros_r, col_hist[-1], zeros_c)
-        row_pot = SMOOTHING * image_logw - SMOOTHING * gathered_lse(part, "cap")
+        row_pot = potential(part, "cap", image_logw)
         row_hist.append(row_pot)
         part = col_pass("lse", images, captions, row_pot, zeros_r, zeros_c)
-        col_hist.append(SMOOTHING * caption_logw - SMOOTHING * gathered_lse(part, "img"))
+        col_hist.append(potential(part, "img", caption_logw))
     col_bar = caption_cot
     row_bars = [None] * ITERS
     col_bars = [None] * ITERS
@@ -326,14 +333,12 @@
         col_bars[level] = col_bar
         shift_col = caption_logw - col_hist[level + 1] / SMOOTHING
         part = row_pass("wsum", images, captions, row_hist[level], shift_col, col_bar)
-        row_bar = -gathered_sum(part, "cap")
-        if level == ITERS - 1:
-            row_bar = image_cot + row_bar
+        row_bar = neg_sum(part, "cap", image_cot if level == ITERS - 1 else None)
         row_bars[level] = row_bar
         if level > 0:
             shift_row = image_logw - row_hist[level] / SMOOTHING
             part = col_pass("wsum", images, captions, shift_row, row_bar, col_hist[level])
-            col_bar = -gathered_sum(part, "img")
+            col_bar = neg_sum(part, "img")
     rows = jnp.stack(row_hist + row_bars + [image_logw, zeros_r], axis=0)
     cols = jnp.stack(col_hist + col_bars + [caption_logw], axis=1)
     ig_part, cg_part = final_pass(images, captions, rows, cols)

time: 387 us -> 382 us (0.987)
  other arithmetic: 19.5 us -> 10.5 us
    another operation x2 -> x6, local copies, waits for them, and re-layouts: 1.35 us -> 7.5 us  [the longest x2 3.09 us: row_pass(): b.reshape(c, 1)]
where the time goes in v11:
time: 382 us; the launch traced here: 381 us
  Pallas kernels  265 us (69%)
  waiting for transfers between devices  74.1 us (19%)
  local copies, waits for them, and re-layouts  16.7 us (4%)
  between operations  14.4 us (4%)
  other arithmetic  10.5 us (3%)
    pallas_call x11, Pallas kernels, combine(): pl.pallas_call(functools.partial(_combine_kernel, axis, n, mode), out_sha...  120 us
    reduce_scatter x1, waiting for transfers between devices, body(): lax.psum_scatter(ig_part, 'cap', scatter_dimension=0, tiled=True)  74.1 us
    pallas_call x6, Pallas kernels, row_pass(): pl.pallas_call(functools.partial(_row_kernel, mode, inv_root), out_shape=...  49.7 us
    pallas_call x5, Pallas kernels, col_pass(): pl.pallas_call(functools.partial(_col_kernel, mode, inv_root), out_shape=...  44.5 us
    pallas_call x1, Pallas kernels, final_pass(): pl.pallas_call(functools.partial(_final_kernel, inv_root), out_shape=(jax...  39.7 us
    pallas_call x1, Pallas kernels, scatter_sum(): pl.pallas_call(functools.partial(_scatter_kernel, axis, n), out_shape=jax...  11.2 us
    pallas_call x5, other arithmetic, col_pass(): pl.pallas_call(functools.partial(_col_kernel, mode, inv_root), out_shape=...  8.41 us
  transfers between devices with their start and end apart: 1, of which 1 were waited for; matrix products, arithmetic and copies ran while one was open for 0% of the time, Pallas kernels for 3%

profile of v11, /device:TPU:0, one launch (start us, length us, event | category | flops | bytes accessed | tf_op | source)
XLA Modules:
  0.0 380.7 jit_solution(4094537433971252918)
XLA Ops:
  7.2 0.0 reduce-scatter.2.cloned.1.call-start
  7.2 1.5 copy.40.w_ref
  8.7 0.6 broadcast_6_a_ref_w_ref.2.a_ref.w_ref
  9.4 0.7 broadcast_7_b_ref_w_ref.2.b_ref.w_ref
  10.1 9.0 %shard_map.77 = f32[1,8192]{1,0:T(1,128)} custom-call(bf16[8192,256]{1,0:T(8,128)(2,1)} %img_ref.23, bf16[512,256]{1,0:T(8,128)(2,1)} %cap_ref.23, f32[1,8192]{1,0:T(1,128)} %broadcast_6_a_ref_w_ref.2.a_ref.w_ref, f32[512,1]{1,0:T(8,128)} %broadcast_7_b_ref_w_ref.2.b_ref.w_ref, f32[512,1]{1,0:T(8,128)} %broadcast_7_b_ref_w_ref.2.b_ref.w_ref), custom_call_target="tpu_custom_call" | custom-call | flops 2147483648 | bytes 4456448 | tf_op jit(solution)/shard_map/pallas_call | solution.py:183
  19.1 14.9 %shard_map.78 = f32[64,128]{1,0:T(8,128)} custom-call(f32[64,128]{1,0:T(8,128)} %bitcast.75, f32[64,128]{1,0:T(8,128)} %bitcast.44), custom_call_target="tpu_custom_call" | custom-call | tf_op jit(solution)/shard_map/pallas_call | solution.py:65
  34.0 9.4 %shard_map.79 = f32[512,1]{1,0:T(8,128)} custom-call(bf16[8192,256]{1,0:T(8,128)(2,1)} %img_ref.23, bf16[512,256]{1,0:T(8,128)(2,1)} %cap_ref.23, f32[1,8192]{1,0:T(1,128)} %bitcast.55, f32[512,1]{1,0:T(8,128)} %broadcast_7_b_ref_w_ref.2.b_ref.w_ref, f32[1,8192]{1,0:T(1,128)} %broadcast_6_a_ref_w_ref.2.a_ref.w_ref), custom_call_target="tpu_custom_call" | custom-call | flops 2147483648 | bytes 4456448 | tf_op jit(solution)/shard_map/pallas_call | solution.py:245
  43.5 1.7 reduce
  45.1 8.5 %shard_map.80 = f32[4,128]{1,0:T(4,128)} custom-call(f32[4,128]{1,0:T(4,128)} %bitcast.88, f32[4,128]{1,0:T(4,128)} %bitcast.67), custom_call_target="tpu_custom_call" | custom-call | tf_op jit(solution)/shard_map/pallas_call | solution.py:65
  53.7 1.5 copy.37.b_ref
  55.1 8.8 %shard_map.81 = f32[1,8192]{1,0:T(1,128)} custom-call(bf16[8192,256]{1,0:T(8,128)(2,1)} %img_ref.23, bf16[512,256]{1,0:T(8,128)(2,1)} %cap_ref.23, f32[1,8192]{1,0:T(1,128)} %broadcast_6_a_ref_w_ref.2.a_ref.w_ref, f32[512,1]{1,0:T(8,128)} %copy.37.b_ref, f32[512,1]{1,0:T(8,128)} %broadcast_7_b_ref_w_ref.2.b_ref.w_ref), custom_call_target="tpu_custom_call" | custom-call | flops 2147483648 | bytes 4456448 | tf_op jit(solution)/shard_map/pallas_call | solution.py:183
  64.0 14.0 %shard_map.82 = f32[64,128]{1,0:T(8,128)} custom-call(f32[64,128]{1,0:T(8,128)} %bitcast.76, f32[64,128]{1,0:T(8,128)} %bitcast.45), custom_call_target="tpu_custom_call" | custom-call | tf_op jit(solution)/shard_map/pallas_call | solution.py:65
  78.0 9.4 %shard_map.83 = f32[512,1]{1,0:T(8,128)} custom-call(bf16[8192,256]{1,0:T(8,128)(2,1)} %img_ref.23, bf16[512,256]{1,0:T(8,128)(2,1)} %cap_ref.23, f32[1,8192]{1,0:T(1,128)} %bitcast.49, f32[512,1]{1,0:T(8,128)} %broadcast_7_b_ref_w_ref.2.b_ref.w_ref, f32[1,8192]{1,0:T(1,128)} %broadcast_6_a_ref_w_ref.2.a_ref.w_ref), custom_call_target="tpu_custom_call" | custom-call | flops 2147483648 | bytes 4456448 | tf_op jit(solution)/shard_map/pallas_call | solution.py:245
  87.4 1.7 reduce.1
  89.1 6.7 %shard_map.84 = f32[4,128]{1,0:T(4,128)} custom-call(f32[4,128]{1,0:T(4,128)} %bitcast.89, f32[4,128]{1,0:T(4,128)} %bitcast.68), custom_call_target="tpu_custom_call" | custom-call | tf_op jit(solution)/shard_map/pallas_call | solution.py:65
  95.8 1.6 copy.38.b_ref
  97.4 8.8 %shard_map.85 = f32[1,8192]{1,0:T(1,128)} custom-call(bf16[8192,256]{1,0:T(8,128)(2,1)} %img_ref.23, bf16[512,256]{1,0:T(8,128)(2,1)} %cap_ref.23, f32[1,8192]{1,0:T(1,128)} %broadcast_6_a_ref_w_ref.2.a_ref.w_ref, f32[512,1]{1,0:T(8,128)} %copy.38.b_ref, f32[512,1]{1,0:T(8,128)} %broadcast_7_b_ref_w_ref.2.b_ref.w_ref), custom_call_target="tpu_custom_call" | custom-call | flops 2147483648 | bytes 4456448 | tf_op jit(solution)/shard_map/pallas_call | solution.py:183
  106.2 14.0 %shard_map.86 = f32[64,128]{1,0:T(8,128)} custom-call(f32[64,128]{1,0:T(8,128)} %bitcast.77, f32[64,128]{1,0:T(8,128)} %bitcast.46), custom_call_target="tpu_custom_call" | custom-call | tf_op jit(solution)/shard_map/pallas_call | solution.py:65
  120.2 1.4 bitcast_subtract_fusion
  121.6 9.4 %shard_map.87 = f32[512,1]{1,0:T(8,128)} custom-call(bf16[8192,256]{1,0:T(8,128)(2,1)} %img_ref.23, bf16[512,256]{1,0:T(8,128)(2,1)} %cap_ref.23, f32[1,8192]{1,0:T(1,128)} %bitcast.52, f32[512,1]{1,0:T(8,128)} %broadcast_7_b_ref_w_ref.2.b_ref.w_ref, f32[1,8192]{1,0:T(1,128)} %broadcast_6_a_ref_w_ref.2.a_ref.w_ref), custom_call_target="tpu_custom_call" | custom-call | flops 2147483648 | bytes 4456448 | tf_op jit(solution)/shard_map/pallas_call | solution.py:245
  131.0 1.7 reduce.2
  132.7 6.6 %shard_map.88 = f32[4,128]{1,0:T(4,128)} custom-call(f32[4,128]{1,0:T(4,128)} %bitcast.90, f32[4,128]{1,0:T(4,128)} %bitcast.69), custom_call_target="tpu_custom_call" | custom-call | tf_op jit(solution)/shard_map/pallas_call | solution.py:65
  139.3 0.7 bitcast_subtract_fusion.2
  140.0 0.9 copy.42.b_ref
  140.9 0.9 copy.39.b_ref
  141.7 7.7 %shard_map.89 = f32[1,8192]{1,0:T(1,128)} custom-call(bf16[8192,256]{1,0:T(8,128)(2,1)} %img_ref.23, bf16[512,256]{1,0:T(8,128)(2,1)} %cap_ref.23, f32[1,8192]{1,0:T(1,128)} %bitcast.53, f32[512,1]{1,0:T(8,128)} %copy.39.b_ref, f32[512,1]{1,0:T(8,128)} %copy.40.w_ref), custom_call_target="tpu_custom_call" | custom-call | flops 2147483648 | bytes 4456448 | tf_op jit(solution)/shard_map/pallas_call | solution.py:183
  149.4 13.9 %shard_map.90 = f32[64,128]{1,0:T(8,128)} custom-call(f32[64,128]{1,0:T(8,128)} %bitcast.74, f32[64,128]{1,0:T(8,128)} %bitcast.71), custom_call_target="tpu_custom_call" | custom-call | tf_op jit(solution)/shard_map/pallas_call | solution.py:65
  163.3 8.1 %shard_map.91 = f32[512,1]{1,0:T(8,128)} custom-call(bf16[8192,256]{1,0:T(8,128)(2,1)} %img_ref.23, bf16[512,256]{1,0:T(8,128)(2,1)} %cap_ref.23, f32[1,8192]{1,0:T(1,128)} %bitcast.73, f32[512,1]{1,0:T(8,128)} %copy.38.b_ref, f32[1,8192]{1,0:T(1,128)} %bitcast.58), custom_call_target="tpu_custom_call" | custom-call | flops 2147483648 | bytes 4456448 | tf_op jit(solution)/shard_map/pallas_call | solution.py:245
  171.4 1.7 reduce.3
  173.1 6.6 %shard_map.92 = f32[4,128]{1,0:T(4,128)} custom-call(f32[4,128]{1,0:T(4,128)} %bitcast.83, f32[4,128]{1,0:T(4,128)} %bitcast.84), custom_call_target="tpu_custom_call" | custom-call | tf_op jit(solution)/shard_map/pallas_call | solution.py:65
  179.8 1.5 copy.43.w_ref
  181.3 7.7 %shard_map.93 = f32[1,8192]{1,0:T(1,128)} custom-call(bf16[8192,256]{1,0:T(8,128)(2,1)} %img_ref.23, bf16[512,256]{1,0:T(8,128)(2,1)} %cap_ref.23, f32[1,8192]{1,0:T(1,128)} %bitcast.50, f32[512,1]{1,0:T(8,128)} %copy.42.b_ref, f32[512,1]{1,0:T(8,128)} %copy.43.w_ref), custom_call_target="tpu_custom_call" | custom-call | flops 2147483648 | bytes 4456448 | tf_op jit(solution)/shard_map/pallas_call | solution.py:183
  189.0 14.0 %shard_map.94 = f32[64,128]{1,0:T(8,128)} custom-call(f32[64,128]{1,0:T(8,128)} %bitcast.63, f32[64,128]{1,0:T(8,128)} %bitcast.64), custom_call_target="tpu_custom_call" | custom-call | tf_op jit(solution)/shard_map/pallas_call | solution.py:65
  203.1 8.2 %shard_map.95 = f32[512,1]{1,0:T(8,128)} custom-call(bf16[8192,256]{1,0:T(8,128)(2,1)} %img_ref.23, bf16[512,256]{1,0:T(8,128)(2,1)} %cap_ref.23, f32[1,8192]{1,0:T(1,128)} %bitcast.72, f32[512,1]{1,0:T(8,128)} %copy.37.b_ref, f32[1,8192]{1,0:T(1,128)} %bitcast.60), custom_call_target="tpu_custom_call" | custom-call | flops 2147483648 | bytes 4456448 | tf_op jit(solution)/shard_map/pallas_call | solution.py:245
  211.3 1.7 reduce.4
  213.0 6.6 %shard_map.96 = f32[4,128]{1,0:T(4,128)} custom-call(f32[4,128]{1,0:T(4,128)} %bitcast.81, f32[4,128]{1,0:T(4,128)} %bitcast.82), custom_call_target="tpu_custom_call" | custom-call | tf_op jit(solution)/shard_map/pallas_call | solution.py:65
  219.6 1.5 copy.46.w_ref
  221.1 0.9 copy.45.b_ref
  222.0 7.7 %shard_map.97 = f32[1,8192]{1,0:T(1,128)} custom-call(bf16[8192,256]{1,0:T(8,128)(2,1)} %img_ref.23, bf16[512,256]{1,0:T(8,128)(2,1)} %cap_ref.23, f32[1,8192]{1,0:T(1,128)} %bitcast.56, f32[512,1]{1,0:T(8,128)} %copy.45.b_ref, f32[512,1]{1,0:T(8,128)} %copy.46.w_ref), custom_call_target="tpu_custom_call" | custom-call | flops 2147483648 | bytes 4456448 | tf_op jit(solution)/shard_map/pallas_call | solution.py:183
  229.7 14.0 %shard_map.98 = f32[64,128]{1,0:T(8,128)} custom-call(f32[64,128]{1,0:T(8,128)} %bitcast.65, f32[64,128]{1,0:T(8,128)} %bitcast.66), custom_call_target="tpu_custom_call" | custom-call | tf_op jit(solution)/shard_map/pallas_call | solution.py:65
  243.7 0.1 copy.49
  243.8 0.1 copy.53
  244.0 1.8 stack.14.rows_ref
  245.9 1.4 stack.16.cols_ref
  247.3 39.7 %shard_map.99 = (f32[8192,256]{1,0:T(8,128)}, f32[512,256]{1,0:T(8,128)}) custom-call(bf16[8192,256]{1,0:T(8,128)(2,1)} %img_ref.23, bf16[512,256]{1,0:T(8,128)(2,1)} %cap_ref.23, f32[8,8192]{1,0:T(8,128)} %stack.14.rows_ref, f32[512,8]{1,0:T(8,128)} %stack.16.cols_ref), custom_call_target="tpu_custom_call" | custom-call | flops 6442450944 | bytes 13369344 | tf_op jit(solution)/shard_map/pallas_call | solution.py:293
  287.1 11.2 %shard_map.100 = f32[64,256]{1,0:T(8,128)} custom-call(f32[8,64,256]{2,1,0:T(8,128)} %bitcast.48), custom_call_target="tpu_custom_call" | custom-call | tf_op jit(solution)/shard_map/pallas_call | solution.py:117
  298.3 74.1 %reduce-scatter.2.cloned.1.call-done = f32[512,256]{1,0:T(8,128)} async-done(((f32[8192,256]{1,0:T(8,128)}), f32[512,256]{1,0:T(8,128)}) %reduce-scatter.2.cloned.1.call-update) | async-done | bytes 524304 | tf_op jit(solution)/shard_map/reduce_scatter | solution.py:345
  372.4 1.5 copy.55
  (37 shorter events, 0.1 us)
Async XLA Ops:
  7.2 365.2 %reduce-scatter.2.cloned.1.call-start = ((), (), s32[]{:S(2)}) async-start(), calls=%async_computation.1 | async-start | bytes 8912896 | tf_op jit(solution)/shard_map/reduce_scatter | solution.py:345
  64.0 56.3 %copy-start.6 = (f32[8192]{0:T(1024)S(1)}, f32[8192]{0:T(1024)}, u32[]{:S(2)}) copy-start(f32[8192]{0:T(1024)} %param.8) | copy-start | bytes 98308
  78.0 42.3 %copy-start.7 = (f32[64,128]{1,0:T(8,128)S(1)}, f32[64,128]{1,0:T(8,128)}, u32[]{:S(2)}) copy-start(f32[64,128]{1,0:T(8,128)} %shard_map.82) | copy-start | bytes 98308
  89.1 50.2 %copy-start.14 = (f32[512]{0:T(512)S(1)}, f32[512]{0:T(512)}, u32[]{:S(2)}) copy-start(f32[512]{0:T(512)} %param.9) | copy-start | bytes 6148
  89.1 50.2 %copy-start.16 = (f32[4,128]{1,0:T(4,128)S(1)}, f32[4,128]{1,0:T(4,128)}, u32[]{:S(2)}) copy-start(f32[4,128]{1,0:T(4,128)} %shard_map.80) | copy-start | bytes 6148
  95.7 43.6 %copy-start.17 = (f32[4,128]{1,0:T(4,128)S(1)}, f32[4,128]{1,0:T(4,128)}, u32[]{:S(2)}) copy-start(f32[4,128]{1,0:T(4,128)} %shard_map.84) | copy-start | bytes 6148
  202.9 40.7 %copy-start.15 = (f32[4,128]{1,0:T(4,128)S(1)}, f32[4,128]{1,0:T(4,128)}, u32[]{:S(2)}) copy-start(f32[4,128]{1,0:T(4,128)} %shard_map.88) | copy-start | bytes 6148
  203.0 41.0 %copy-start.8 = (f32[64,128]{1,0:T(8,128)S(1)}, f32[64,128]{1,0:T(8,128)}, u32[]{:S(2)}) copy-start(f32[64,128]{1,0:T(8,128)} %shard_map.82) | copy-start | bytes 98308
  203.0 41.0 %copy-start.9 = (f32[64,128]{1,0:T(8,128)S(1)}, f32[64,128]{1,0:T(8,128)}, u32[]{:S(2)}) copy-start(f32[64,128]{1,0:T(8,128)} %shard_map.86) | copy-start | bytes 98308
  203.0 41.0 %copy-start.10 = (f32[64,128]{1,0:T(8,128)S(1)}, f32[64,128]{1,0:T(8,128)}, u32[]{:S(2)}) copy-start(f32[64,128]{1,0:T(8,128)} %shard_map.78) | copy-start | bytes 98308
  203.0 41.0 %copy-start.11 = (f32[64,128]{1,0:T(8,128)S(1)}, f32[64,128]{1,0:T(8,128)}, u32[]{:S(2)}) copy-start(f32[64,128]{1,0:T(8,128)} %shard_map.90) | copy-start | bytes 98308
  203.0 41.0 %copy-start.12 = (f32[64,128]{1,0:T(8,128)S(1)}, f32[64,128]{1,0:T(8,128)}, u32[]{:S(2)}) copy-start(f32[64,128]{1,0:T(8,128)} %shard_map.94) | copy-start | bytes 98308
  203.0 41.0 %copy-start.13 = (f32[1,8192]{1,0:T(1,128)S(1)}, f32[1,8192]{1,0:T(1,128)}, u32[]{:S(2)}) copy-start(f32[1,8192]{1,0:T(1,128)} %broadcast_6_a_ref_w_ref.2.a_ref.w_ref) | copy-start | bytes 98308
  203.0 42.8 %copy-start = (f32[512,1]{1,0:T(8,128)S(1)}, f32[512,1]{1,0:T(8,128)}, u32[]{:S(2)}) copy-start(f32[512,1]{1,0:T(8,128)} %copy.40.w_ref) | copy-start | bytes 6148
  203.0 42.8 %copy-start.1 = (f32[512,1]{1,0:T(8,128)S(1)}, f32[512,1]{1,0:T(8,128)}, u32[]{:S(2)}) copy-start(f32[512,1]{1,0:T(8,128)} %broadcast_7_b_ref_w_ref.2.b_ref.w_ref) | copy-start | bytes 6148
  203.0 42.8 %copy-start.2 = (f32[512,1]{1,0:T(8,128)S(1)}, f32[512,1]{1,0:T(8,128)}, u32[]{:S(2)}) copy-start(f32[512,1]{1,0:T(8,128)} %copy.37.b_ref) | copy-start | bytes 6148
  203.1 42.8 %copy-start.3 = (f32[512,1]{1,0:T(8,128)S(1)}, f32[512,1]{1,0:T(8,128)}, u32[]{:S(2)}) copy-start(f32[512,1]{1,0:T(8,128)} %copy.38.b_ref) | copy-start | bytes 6148
  203.1 42.8 %copy-start.4 = (f32[512,1]{1,0:T(8,128)S(1)}, f32[512,1]{1,0:T(8,128)}, u32[]{:S(2)}) copy-start(f32[512,1]{1,0:T(8,128)} %copy.43.w_ref) | copy-start | bytes 6148
  221.1 24.8 %copy-start.5 = (f32[512,1]{1,0:T(8,128)S(1)}, f32[512,1]{1,0:T(8,128)}, u32[]{:S(2)}) copy-start(f32[512,1]{1,0:T(8,128)} %copy.46.w_ref) | copy-start | bytes 6148
Sparse Core Ops, SparseCore 0:
  287.2 85.1 reduce-scatter.1
